TPU v7x, 32 devices: a whole 2x2x4 slice. The times are simulated.
32 devices in a mesh: task: 4 (over y, x), batch: 8 (over z, core).
Axes of the slice: x: 2, y: 2, z: 4, core: 2. Of those that a mesh axis runs over, the one named last changes fastest.
Arguments:
- hidden_in: bfloat16 [128, 512, 768], P(('task', 'batch')), may hold values from -6 to 6
- out_grad: bfloat16 [128, 512, 768], P(('task', 'batch')), may hold values from -6 to 6
- segment_ids: int32 [128, 512], P(('task', 'batch')), may hold values from 0 to 3, never falling along the last dimension, each value on 1 to 256 neighbouring positions
- pad_mask: int32 [128, 512], P(('task', 'batch')), may hold values 0 or 1
- task_weight: float32 [4], P('task'), may hold values from 0.002 to 0.008
- w_qkv: bfloat16 [768, 2304], P(('task', 'batch')), may hold values from -0.3125 to 0.3125
- b_query: bfloat16 [768], P(('task', 'batch')), may hold values from -3 to 3
- b_value: bfloat16 [768], P(('task', 'batch')), may hold values from -3 to 3
- w_out: bfloat16 [768, 768], P(('task', 'batch')), may hold values from -0.625 to 0.625
- b_out: bfloat16 [768], P(('task', 'batch')), may hold values from -3 to 3
- gain_one: bfloat16 [768], P(('task', 'batch')), may hold values from 0.5 to 1.5
- shift_one: bfloat16 [768], P(('task', 'batch')), may hold values from -2 to 2
- w_in: bfloat16 [768, 3072], P(('task', 'batch')), may hold values from -0.21875 to 0.21875
- b_in: bfloat16 [3072], P(('task', 'batch')), may hold values from -3 to 3
- w_down: bfloat16 [3072, 768], P(('task', 'batch')), may hold values from -0.15625 to 0.15625
- b_down: bfloat16 [768], P(('task', 'batch')), may hold values from -3 to 3
- gain_two: bfloat16 [768], P(('task', 'batch')), may hold values from 0.5 to 1.5
- shift_two: bfloat16 [768], P(('task', 'batch')), may hold values from -2 to 2
Outputs:
- hidden_out: bfloat16 [128, 512, 768], P(('task', 'batch'))
- input_grad: float32 [128, 512, 768], P(('task', 'batch'))
- grad_w_qkv: float32 [768, 2304], P(('task', 'batch'))
- grad_b_query: float32 [768], P(('task', 'batch'))
- grad_b_value: float32 [768], P(('task', 'batch'))
- grad_w_out: float32 [768, 768], P(('task', 'batch'))
- grad_b_out: float32 [768], P(('task', 'batch'))
- grad_gain_one: float32 [768], P(('task', 'batch'))
- grad_shift_one: float32 [768], P(('task', 'batch'))
- grad_w_in: float32 [768, 3072], P(('task', 'batch'))
- grad_b_in: float32 [3072], P(('task', 'batch'))
- grad_w_down: float32 [3072, 768], P(('task', 'batch'))
- grad_b_down: float32 [768], P(('task', 'batch'))
- grad_gain_two: float32 [768], P(('task', 'batch'))
- grad_shift_two: float32 [768], P(('task', 'batch'))
All inputs are finite; a program needn't handle non-finite values. No bound on the sum of `pad_mask` on one device may be relied on, other than what follows from the above.
Results may differ from a plain program's by a relative error of at most 0.014.
The roundings to bfloat16 on the way count: a program that leaves them out, or rounds other values in their place, can miss the bound.
Values may be sent and summed in bfloat16 or wider, within the bound.
A program may use at most 256 MiB of HBM per device.

v0:
```python
from functools import partial

import jax
import jax.numpy as jnp
from jax import lax
from jax.sharding import PartitionSpec as P

HEADS = 12


def normalize(arr_in, gain_in, shift_in):
    centre = arr_in - jnp.mean(arr_in, -1, keepdims=True)
    spread = jnp.mean(centre * centre, -1, keepdims=True)
    return centre * lax.rsqrt(spread + 1e-12) * gain_in + shift_in


def allowed_mask(segment_row, pad_row):
    places = lax.iota(jnp.int32, segment_row.shape[0])
    same = segment_row[:, None] == segment_row[None, :]
    return same & ((pad_row[None, :] == 1) | (places[:, None] == places[None, :]))


def masked_scores(queries, keys_in, segment_row, pad_row):
    scores = (
        jnp.einsum("qhd,khd->hqk", queries, keys_in, preferred_element_type=jnp.float32) * 0.125
    )
    return jnp.where(allowed_mask(segment_row, pad_row)[None], scores, -1e30)


def attend_forward(inputs):
    queries, keys_in, values_in, segment_row, pad_row = inputs
    scores = masked_scores(queries, keys_in, segment_row, pad_row)
    top_row = jnp.max(scores, -1, keepdims=True)
    expo = jnp.exp(scores - top_row)
    row_sum = jnp.sum(expo, -1, keepdims=True)
    probs_row = (expo / row_sum).astype(jnp.bfloat16)
    attended = jnp.einsum("hqk,khd->qhd", probs_row, values_in, preferred_element_type=jnp.float32)
    return (attended.astype(jnp.bfloat16), top_row + jnp.log(row_sum))


def attend_backward(inputs):
    queries, keys_in, values_in, segment_row, pad_row, log_total, grad_att = inputs
    scores = masked_scores(queries, keys_in, segment_row, pad_row)
    probs_row = jnp.exp(scores - log_total)
    probs_low = probs_row.astype(jnp.bfloat16)
    grad_values = jnp.einsum(
        "hqk,qhd->khd", probs_low, grad_att, preferred_element_type=jnp.float32
    )
    grad_probs = jnp.einsum("qhd,khd->hqk", grad_att, values_in, preferred_element_type=jnp.float32)
    inner = jnp.sum(probs_row * grad_probs, -1, keepdims=True)
    grad_scores = (probs_row * (grad_probs - inner)).astype(jnp.bfloat16)
    grad_queries = (
        jnp.einsum("hqk,khd->qhd", grad_scores, keys_in, preferred_element_type=jnp.float32) * 0.125
    )
    grad_keys = (
        jnp.einsum("hqk,qhd->khd", grad_scores, queries, preferred_element_type=jnp.float32) * 0.125
    )
    return (
        grad_queries.astype(jnp.bfloat16),
        grad_keys.astype(jnp.bfloat16),
        grad_values.astype(jnp.bfloat16),
    )


def fetch_forward(params):
    return (
        lax.all_gather(params[0], ("task", "batch"), axis=0, tiled=True),
        lax.all_gather(params[1], ("task", "batch"), axis=0, tiled=True),
        lax.all_gather(params[2], ("task", "batch"), axis=0, tiled=True),
        lax.all_gather(params[3], ("task", "batch"), axis=0, tiled=True),
        lax.all_gather(params[4], ("task", "batch"), axis=0, tiled=True),
        lax.all_gather(params[5], ("task", "batch"), axis=0, tiled=True),
        lax.all_gather(params[6], ("task", "batch"), axis=0, tiled=True),
        lax.all_gather(params[7], ("task", "batch"), axis=0, tiled=True),
        lax.all_gather(params[8], ("task", "batch"), axis=0, tiled=True),
        lax.all_gather(params[9], ("task", "batch"), axis=0, tiled=True),
        lax.all_gather(params[10], ("task", "batch"), axis=0, tiled=True),
        lax.all_gather(params[11], ("task", "batch"), axis=0, tiled=True),
        lax.all_gather(params[12], ("task", "batch"), axis=0, tiled=True),
    )


def fetch_backward(params):
    return (
        lax.all_gather(params[0], ("task", "batch"), axis=0, tiled=True),
        lax.all_gather(params[1], ("task", "batch"), axis=0, tiled=True),
        lax.all_gather(params[2], ("task", "batch"), axis=0, tiled=True),
        lax.all_gather(params[3], ("task", "batch"), axis=0, tiled=True),
        lax.all_gather(params[4], ("task", "batch"), axis=0, tiled=True),
        lax.all_gather(params[5], ("task", "batch"), axis=0, tiled=True),
        lax.all_gather(params[6], ("task", "batch"), axis=0, tiled=True),
        lax.all_gather(params[7], ("task", "batch"), axis=0, tiled=True),
        lax.all_gather(params[8], ("task", "batch"), axis=0, tiled=True),
        lax.all_gather(params[9], ("task", "batch"), axis=0, tiled=True),
        lax.all_gather(params[10], ("task", "batch"), axis=0, tiled=True),
        lax.all_gather(params[11], ("task", "batch"), axis=0, tiled=True),
        lax.all_gather(params[12], ("task", "batch"), axis=0, tiled=True),
    )


def left_product(left, right):
    return lax.dot_general(
        left, right, (((0,), (0,)), ((), ())), preferred_element_type=jnp.float32
    )


def right_product(left, right):
    return lax.dot_general(
        left, right, (((1,), (1,)), ((), ())), preferred_element_type=jnp.float32
    )


def column_sum(grad_low):
    return jnp.sum(grad_low.astype(jnp.float32), 0)


def body(
    hidden_in,
    out_grad,
    segment_ids,
    pad_mask,
    task_weight,
    w_qkv,
    b_query,
    b_value,
    w_out,
    b_out,
    gain_one,
    shift_one,
    w_in,
    b_in,
    w_down,
    b_down,
    gain_two,
    shift_two,
):
    params = (
        w_qkv,
        b_query,
        b_value,
        w_out,
        b_out,
        gain_one,
        shift_one,
        w_in,
        b_in,
        w_down,
        b_down,
        gain_two,
        shift_two,
    )
    full = fetch_forward(params)
    (
        qkv_full,
        bq_full,
        bv_full,
        wo_full,
        bo_full,
        g1_full,
        s1_full,
        win_full,
        bin_full,
        wd_full,
        bd_full,
        g2_full,
        s2_full,
    ) = full
    seqs_here = hidden_in.shape[0]
    length = hidden_in.shape[1]
    width = hidden_in.shape[2]
    head_size = width // HEADS
    rows = hidden_in.reshape(-1, width)
    qkv = jnp.dot(rows, qkv_full, preferred_element_type=jnp.float32)
    queries = (qkv[:, :width] + bq_full.astype(jnp.float32)).astype(jnp.bfloat16)
    keys_all = qkv[:, width : 2 * width].astype(jnp.bfloat16)
    values_all = (qkv[:, 2 * width :] + bv_full.astype(jnp.float32)).astype(jnp.bfloat16)
    query_heads = queries.reshape(seqs_here, length, HEADS, head_size)
    key_heads = keys_all.reshape(seqs_here, length, HEADS, head_size)
    value_heads = values_all.reshape(seqs_here, length, HEADS, head_size)
    attended, log_total = lax.map(
        attend_forward, (query_heads, key_heads, value_heads, segment_ids, pad_mask)
    )
    att_rows = attended.reshape(-1, width)
    branch_one = jnp.dot(att_rows, wo_full, preferred_element_type=jnp.float32) + bo_full.astype(
        jnp.float32
    )
    first_in = rows.astype(jnp.float32) + branch_one
    first = normalize(first_in, g1_full.astype(jnp.float32), s1_full.astype(jnp.float32))
    first_low = first.astype(jnp.bfloat16)
    pre_act = jnp.dot(first_low, win_full, preferred_element_type=jnp.float32) + bin_full.astype(
        jnp.float32
    )
    act_low = jax.nn.gelu(pre_act, approximate=False).astype(jnp.bfloat16)
    branch_two = jnp.dot(act_low, wd_full, preferred_element_type=jnp.float32) + bd_full.astype(
        jnp.float32
    )
    second = first + branch_two
    hidden_out = (
        normalize(second, g2_full.astype(jnp.float32), s2_full.astype(jnp.float32))
        .astype(jnp.bfloat16)
        .reshape(hidden_in.shape)
    )
    back_full = fetch_backward(params)
    (
        qkv_back,
        bq_back,
        bv_back,
        wo_back,
        bo_back,
        g1_back,
        s1_back,
        win_back,
        bin_back,
        wd_back,
        bd_back,
        g2_back,
        s2_back,
    ) = back_full
    grad_rows = out_grad.reshape(-1, width).astype(jnp.float32)
    unused_two, norm_two_back = jax.vjp(
        normalize, second, g2_back.astype(jnp.float32), s2_back.astype(jnp.float32)
    )
    grad_second, grad_gain_two, grad_shift_two = norm_two_back(grad_rows)
    grad_branch_two = grad_second.astype(jnp.bfloat16)
    grad_b_down = column_sum(grad_branch_two)
    grad_w_down = left_product(act_low, grad_branch_two)
    grad_act = right_product(grad_branch_two, wd_back)
    unused_act, gelu_back = jax.vjp(partial(jax.nn.gelu, approximate=False), pre_act)
    grad_pre = gelu_back(grad_act)[0].astype(jnp.bfloat16)
    grad_b_in = column_sum(grad_pre)
    grad_w_in = left_product(first_low, grad_pre)
    grad_first = right_product(grad_pre, win_back) + grad_second
    unused_one, norm_one_back = jax.vjp(
        normalize, first_in, g1_back.astype(jnp.float32), s1_back.astype(jnp.float32)
    )
    grad_sum_one, grad_gain_one, grad_shift_one = norm_one_back(grad_first)
    grad_branch_one = grad_sum_one.astype(jnp.bfloat16)
    grad_b_out = column_sum(grad_branch_one)
    grad_w_out = left_product(att_rows, grad_branch_one)
    grad_att = (
        right_product(grad_branch_one, wo_back)
        .astype(jnp.bfloat16)
        .reshape(seqs_here, length, HEADS, head_size)
    )
    grad_q, grad_k, grad_v = lax.map(
        attend_backward,
        (query_heads, key_heads, value_heads, segment_ids, pad_mask, log_total, grad_att),
    )
    grad_q = grad_q.reshape(-1, width)
    grad_v = grad_v.reshape(-1, width)
    grad_qkv = jnp.concatenate([grad_q, grad_k.reshape(-1, width), grad_v], 1)
    grad_b_query = column_sum(grad_q)
    grad_b_value = column_sum(grad_v)
    grad_w_qkv = left_product(rows, grad_qkv)
    input_grad = (right_product(grad_qkv, qkv_back) + grad_sum_one).reshape(hidden_in.shape)
    scale_task = task_weight[0]
    terms = tuple(
        (
            scale_task * term
            for term in (
                grad_w_qkv,
                grad_b_query,
                grad_b_value,
                grad_w_out,
                grad_b_out,
                grad_gain_one,
                grad_shift_one,
                grad_w_in,
                grad_b_in,
                grad_w_down,
                grad_b_down,
                grad_gain_two,
                grad_shift_two,
            )
        )
    )
    summed = (
        lax.psum_scatter(terms[0], ("task", "batch"), scatter_dimension=0, tiled=True),
        lax.psum_scatter(terms[1], ("task", "batch"), scatter_dimension=0, tiled=True),
        lax.psum_scatter(terms[2], ("task", "batch"), scatter_dimension=0, tiled=True),
        lax.psum_scatter(terms[3], ("task", "batch"), scatter_dimension=0, tiled=True),
        lax.psum_scatter(terms[4], ("task", "batch"), scatter_dimension=0, tiled=True),
        lax.psum_scatter(terms[5], ("task", "batch"), scatter_dimension=0, tiled=True),
        lax.psum_scatter(terms[6], ("task", "batch"), scatter_dimension=0, tiled=True),
        lax.psum_scatter(terms[7], ("task", "batch"), scatter_dimension=0, tiled=True),
        lax.psum_scatter(terms[8], ("task", "batch"), scatter_dimension=0, tiled=True),
        lax.psum_scatter(terms[9], ("task", "batch"), scatter_dimension=0, tiled=True),
        lax.psum_scatter(terms[10], ("task", "batch"), scatter_dimension=0, tiled=True),
        lax.psum_scatter(terms[11], ("task", "batch"), scatter_dimension=0, tiled=True),
        lax.psum_scatter(terms[12], ("task", "batch"), scatter_dimension=0, tiled=True),
    )
    return (
        hidden_out,
        input_grad,
        summed[0],
        summed[1],
        summed[2],
        summed[3],
        summed[4],
        summed[5],
        summed[6],
        summed[7],
        summed[8],
        summed[9],
        summed[10],
        summed[11],
        summed[12],
    )


def solution(mesh):
    in_specs = (
        P(("task", "batch"), None, None),
        P(("task", "batch"), None, None),
        P(("task", "batch"), None),
        P(("task", "batch"), None),
        P("task"),
        P(("task", "batch"), None),
        P(("task", "batch")),
        P(("task", "batch")),
        P(("task", "batch"), None),
        P(("task", "batch")),
        P(("task", "batch")),
        P(("task", "batch")),
        P(("task", "batch"), None),
        P(("task", "batch")),
        P(("task", "batch"), None),
        P(("task", "batch")),
        P(("task", "batch")),
        P(("task", "batch")),
    )
    out_specs = (
        P(("task", "batch"), None, None),
        P(("task", "batch"), None, None),
        P(("task", "batch"), None),
        P(("task", "batch")),
        P(("task", "batch")),
        P(("task", "batch"), None),
        P(("task", "batch")),
        P(("task", "batch")),
        P(("task", "batch")),
        P(("task", "batch"), None),
        P(("task", "batch")),
        P(("task", "batch"), None),
        P(("task", "batch")),
        P(("task", "batch")),
        P(("task", "batch")),
    )
    return jax.shard_map(body, mesh=mesh, in_specs=in_specs, out_specs=out_specs, check_vma=False)
```

profile of v0, /device:TPU:0, one launch (start us, length us, event | category | flops | bytes accessed | tf_op | source)
XLA Modules:
  0.0 967.2 jit_solution(12853065611931419830)
XLA Ops:
  17.6 42.5 %all-reduce.19 = (bf16[768]{0:T(1024)(128)(2,1)S(1)}, bf16[768]{0:T(1024)(128)(2,1)S(1)}, bf16[768]{0:T(1024)(128)(2,1)S(1)}, bf16[768]{0:T(1024)(128)(2,1)S(1)}...) all-reduce(bf16[768]{0:T(1024)(128)(2,1)S(1)} %dynamic-update-slice, ...), channel_id=1, replica_groups=mesh['task'=4,'batch'=8] {'task','batch'}, use_global_device_ids=true, to_apply=%add | all-reduce | flops 9216 | bytes 36864
  64.9 9.2 all-gather.5.cloned.1.call-done
  74.1 10.7 %fusion.84 = f32[2048,2304]{1,0:T(8,128)S(1)} fusion(bf16[2048,768]{1,0:T(8,128)(2,1)} %bitcast.202, bf16[768,2304]{1,0:T(8,128)(2,1)} %all-gather.5.cloned.1.call-done), kind=kOutput, calls=%fused_computation.152 | convolution fusion | flops 7247757312 | bytes 25559040 | tf_op jit(solution)/shard_map/dot_general | solution.py:173
  128.9 54.3 %while.26 = (s32[]{:T(128)}, bf16[4,512,12,64]{1,3,2,0:T(8,128)(2,1)}, f32[4,12,512,1]{2,1,3,0:T(8,128)}, bf16[4,512,12,64]{1,3,2,0:T(8,128)(2,1)}, s32[4,512]{1...) while((s32[]{:T(128)}, ...), condition=%wide.region_3.4_spmd, body=%wide.region_0.3_spmd.sunk | while | flops 844491264 | bytes 42159716 | solution.py:180
  202.2 70.4 %multiply_convert_fusion.3 = (bf16[2048,3072]{1,0:T(8,128)(2,1)}, f32[2048,3072]{1,0:T(8,128)}, f32[2048,3072]{1,0:T(8,128)}) fusion(f32[3072]{0:T(1024)S(1)} %copy-done.29, bf16[768,3072]{1,0:T(8,128)(2,1)} %all-gather.9.cloned.1.call-done, f32[2048,768]{1,0:T(8,128)} %copy-done.5, f32[768]{0:T(1024)S(1)} %copy-done.30, f32[768]{0:T(1024)S(1)} %copy-done.26, ...), kind=kOutput, calls=%fused_computation.75 | convolution fusion | flops 10086776832 | bytes 73959424 | tf_op jit(solution)/shard_map/dot_general | solution.py:190
  272.6 16.0 %fusion.83 = (f32[2048]{0:T(1024)S(1)}, f32[2048,768]{1,0:T(8,128)S(1)}) fusion(f32[768]{0:T(1024)S(1)} %copy-done.32, bf16[2048,3072]{1,0:T(8,128)(2,1)} %get-tuple-element.293, bf16[3072,768]{1,0:T(8,128)(2,1)} %all-gather.11.cloned.1.call-done, f32[768]{0:T(1024)S(1)} %copy-done.30, f32[768]{0:T(1024)S(1)} %copy-done.26, f32[2048]{0:T(1024)S(1)} %fusion.74, ...), kind=kOutput, calls=%fused_computation.151 | convolution fusion | flops 9674684416 | bytes 29918208 | tf_op jit(solution)/shard_map/dot_general | solution.py:194
  301.9 29.0 %convert_reduce_fusion = (f32[3072]{0:T(1024)}, bf16[2048,3072]{1,0:T(8,128)(2,1)}) fusion(f32[2048,3072]{1,0:T(8,128)} %get-tuple-element.294, bf16[2048,768]{1,0:T(8,128)(2,1)S(1)} %get-tuple-element.286, bf16[3072,768]{1,0:T(8,128)(2,1)} %all-gather.11.cloned.1.call-done, f32[2048,3072]{1,0:T(8,128)} %get-tuple-element.304, f32[3072]{0:T(1024)S(1)} %copy-done.29), kind=kOutput, calls=%fused_computation.73 | convolution fusion | flops 9770628096 | bytes 70803456 | tf_op jit(solution)/shard_map/dot_general | solution.py:108
  330.9 19.3 %multiply_reduce_fusion.1 = (f32[768]{0:T(1024)}, f32[2048]{0:T(1024)S(1)}, f32[768]{0:T(1024)}, f32[2048,768]{1,0:T(8,128)S(1)}) fusion(f32[2048,768]{1,0:T(8,128)} %copy-done.5, f32[2048]{0:T(1024)S(1)} %fusion.74, f32[2048]{0:T(1024)S(1)} %broadcast_multiply_fusion.4, f32[768]{0:T(1024)S(1)} %copy-done.26, f32[2048,768]{1,0:T(8,128)} %copy-done.6, ...), kind=kOutput, calls=%fused_computation.105 | convolution fusion | flops 9679400960 | bytes 36217856 | tf_op jit(solution)/shard_map/dot_general | solution.py:108
  386.5 135.6 %while.27 = (s32[]{:T(128)}, bf16[4,512,12,64]{1,3,2,0:T(8,128)(2,1)}, bf16[4,512,12,64]{1,3,2,0:T(8,128)(2,1)}, bf16[4,512,12,64]{1,3,2,0:T(8,128)(2,1)}, bf16[...) while((s32[]{:T(128)}, ...), condition=%wide.region_14.15_spmd, body=%wide.region_12.14_spmd.sunk | while | flops 2063460864 | bytes 103471232 | solution.py:245
  392.1 10.1 %multiply_reduce_fusion.6 = (f32[12,512]{1,0:T(8,128)S(1)}, f32[12,512,512]{1,2,0:T(8,128)}) fusion(f32[12,512,512]{1,2,0:T(8,128)S(1)} %fusion.141, f32[12,512]{1,0:T(8,128)S(1)} %dynamic-slice_bitcast_fusion.2, pred[512,512]{0,1:T(8,128)(4,1)S(1)} %fusion.142, bf16[4,512,12,64]{1,3,2,0:T(8,128)(2,1)} %get-tuple-element.501, ...), kind=kOutput, calls=%fused_computation.27.clone.1 | convolution fusion | flops 418375680 | bytes 27051008 | tf_op jit(solution)/shard_map/while/body/eval_jaxpr/qhd,khd->hqk/dot_general | solution.py:49
  402.3 7.1 multiply_convert_fusion.5
  426.0 10.1 %multiply_reduce_fusion.6 = (f32[12,512]{1,0:T(8,128)S(1)}, f32[12,512,512]{1,2,0:T(8,128)}) fusion(f32[12,512,512]{1,2,0:T(8,128)S(1)} %fusion.141, f32[12,512]{1,0:T(8,128)S(1)} %dynamic-slice_bitcast_fusion.2, pred[512,512]{0,1:T(8,128)(4,1)S(1)} %fusion.142, bf16[4,512,12,64]{1,3,2,0:T(8,128)(2,1)} %get-tuple-element.501, ...), kind=kOutput, calls=%fused_computation.27.clone.1 | convolution fusion | flops 418375680 | bytes 27051008 | tf_op jit(solution)/shard_map/while/body/eval_jaxpr/qhd,khd->hqk/dot_general | solution.py:49
  436.1 7.1 multiply_convert_fusion.5
  459.8 10.1 %multiply_reduce_fusion.6 = (f32[12,512]{1,0:T(8,128)S(1)}, f32[12,512,512]{1,2,0:T(8,128)}) fusion(f32[12,512,512]{1,2,0:T(8,128)S(1)} %fusion.141, f32[12,512]{1,0:T(8,128)S(1)} %dynamic-slice_bitcast_fusion.2, pred[512,512]{0,1:T(8,128)(4,1)S(1)} %fusion.142, bf16[4,512,12,64]{1,3,2,0:T(8,128)(2,1)} %get-tuple-element.501, ...), kind=kOutput, calls=%fused_computation.27.clone.1 | convolution fusion | flops 418375680 | bytes 27051008 | tf_op jit(solution)/shard_map/while/body/eval_jaxpr/qhd,khd->hqk/dot_general | solution.py:49
  493.7 10.1 %multiply_reduce_fusion.6 = (f32[12,512]{1,0:T(8,128)S(1)}, f32[12,512,512]{1,2,0:T(8,128)}) fusion(f32[12,512,512]{1,2,0:T(8,128)S(1)} %fusion.141, f32[12,512]{1,0:T(8,128)S(1)} %dynamic-slice_bitcast_fusion.2, pred[512,512]{0,1:T(8,128)(4,1)S(1)} %fusion.142, bf16[4,512,12,64]{1,3,2,0:T(8,128)(2,1)} %get-tuple-element.501, ...), kind=kOutput, calls=%fused_computation.27.clone.1 | convolution fusion | flops 418375680 | bytes 27051008 | tf_op jit(solution)/shard_map/while/body/eval_jaxpr/qhd,khd->hqk/dot_general | solution.py:49
  539.3 10.0 %multiply_bitcast_fusion = f32[768,2304]{0,1:T(8,128)} fusion(bf16[2048,2304]{0,1:T(8,128)(2,1)S(1)} %constant_dynamic-update-slice_fusion, bf16[2048,768]{1,0:T(8,128)(2,1)S(1)} %bitcast.204, f32[]{:T(128)} %bitcast.179), kind=kOutput, calls=%fused_computation.91 | convolution fusion | flops 7249526784 | bytes 19660804 | tf_op jit(solution)/shard_map/dot_general | solution.py:102
  549.3 8.0 copy.89
  557.4 16.1 %convolution_multiply_fusion = f32[3072,768]{1,0:T(8,128)} fusion(bf16[2048,3072]{1,0:T(8,128)(2,1)} %get-tuple-element.293, bf16[2048,768]{1,0:T(8,128)(2,1)} %copy-done.8, f32[]{:T(128)} %bitcast.185), kind=kOutput, calls=%fused_computation.116 | convolution fusion | flops 9666035712 | bytes 25165828 | tf_op jit(solution)/shard_map/dot_general | solution.py:102
  574.2 18.7 %convolution_multiply_fusion.1 = f32[768,3072]{1,0:T(8,128)} fusion(bf16[2048,3072]{1,0:T(8,128)(2,1)} %get-tuple-element.309, f32[]{:T(128)} %bitcast.183, f32[2048,768]{1,0:T(8,128)} %copy-done.5, f32[768]{0:T(1024)S(1)} %copy-done.31, f32[768]{0:T(1024)S(1)} %copy-done.27, f32[2048]{0:T(1024)S(1)} %copy-done.21, f32[2048]{0:T(1024)S(1)} %copy-done.14), kind=kOutput, calls=%fused_computation.117 | convolution fusion | flops 9673900032 | bytes 28334084 | tf_op jit(solution)/shard_map/dot_general | solution.py:102
  598.8 41.5 %all-reduce.18 = (f32[768]{0:T(1024)S(1)}, f32[768]{0:T(1024)S(1)}, f32[768]{0:T(1024)S(1)}, f32[768]{0:T(1024)S(1)}, f32[768]{0:T(1024)S(1)}, /*index=5*/f32[30...) all-reduce(f32[768]{0:T(1024)S(1)} %mul.280, ...), channel_id=3, replica_groups=mesh['task'=4,'batch'=8] {'task','batch'}, use_global_device_ids=true, to_apply=%region_17.18.clone | all-reduce | flops 9216 | bytes 73728
  645.5 14.3 %add_add_fusion.4 = f32[2048,768]{1,0:T(8,128)} fusion(f32[2048,768]{1,0:T(8,128)} %copy-done.4, bf16[2048,2304]{0,1:T(8,128)(2,1)} %copy-done.12, bf16[768,2304]{1,0:T(8,128)(2,1)} %all-gather.5.cloned.1.call-done, f32[2048]{0:T(1024)S(1)} %copy-done.19), kind=kOutput, calls=%fused_computation.118 | convolution fusion | flops 7250903040 | bytes 25567232 | tf_op jit(solution)/shard_map/dot_general | solution.py:108
  659.8 16.7 %reduce-scatter.13.cloned.1.call-done = f32[24,2304]{1,0:T(8,128)} async-done(((f32[768,2304]{1,0:T(8,128)}), f32[24,2304]{1,0:T(8,128)}) %reduce-scatter.13.cloned.1.call-update) | async-done | bytes 221200
  676.5 141.3 %reduce-scatter.11.cloned.1.call-done = f32[96,768]{1,0:T(8,128)} async-done(((f32[3072,768]{1,0:T(8,128)}), f32[96,768]{1,0:T(8,128)}) %reduce-scatter.11.cloned.1.call-update) | async-done | bytes 294928 | tf_op jit(solution)/shard_map/reduce_scatter | solution.py:287
  817.8 142.3 %reduce-scatter.9.cloned.1.call-done = f32[24,3072]{1,0:T(8,128)} async-done(((f32[768,3072]{1,0:T(8,128)}), f32[24,3072]{1,0:T(8,128)}) %reduce-scatter.9.cloned.1.call-update) | async-done | bytes 294928 | tf_op jit(solution)/shard_map/reduce_scatter | solution.py:285
  (253 shorter events, 290.3 us)
Async XLA Ops:
  7.2 66.9 %all-gather.5.cloned.1.call-start = ((), (), s32[]{:S(2)}) async-start(), calls=%async_computation.4 | async-start | bytes 3649536 | tf_op jit(solution)/shard_map/all_gather | solution.py:67
  7.9 183.4 %all-gather.7.cloned.1.call-start = ((), (), s32[]{:S(2)}) async-start(), calls=%async_computation.5 | async-start | bytes 1216512 | tf_op jit(solution)/shard_map/all_gather | solution.py:70
  8.7 193.5 %all-gather.9.cloned.1.call-start = ((), (), s32[]{:S(2)}) async-start(), calls=%async_computation.6 | async-start | bytes 4866048 | tf_op jit(solution)/shard_map/all_gather | solution.py:74
  9.4 263.2 %all-gather.11.cloned.1.call-start = ((), (), s32[]{:S(2)}) async-start(), calls=%async_computation.7 | async-start | bytes 4866048 | tf_op jit(solution)/shard_map/all_gather | solution.py:76
  10.0 649.8 %reduce-scatter.7.cloned.1.call-start = ((), (), s32[]{:S(2)}) async-start(), calls=%async_computation.8 | async-start | bytes 2433024 | tf_op jit(solution)/shard_map/reduce_scatter | solution.py:281
  183.2 8.2 copy-start
  183.2 8.2 copy-start.33
  198.0 152.2 %copy-start.13 = (f32[2048]{0:T(1024)}, f32[2048]{0:T(1024)S(1)}, u32[]{:S(2)}) copy-start(f32[2048]{0:T(1024)S(1)} %broadcast_multiply_fusion.4) | copy-start | bytes 24580
  202.1 148.1 %copy-start.20 = (f32[2048]{0:T(1024)}, f32[2048]{0:T(1024)S(1)}, u32[]{:S(2)}) copy-start(f32[2048]{0:T(1024)S(1)} %fusion.74) | copy-start | bytes 24580
  202.2 70.4 %copy-start.32 = (f32[768]{0:T(1024)S(1)}, f32[768]{0:T(1024)}, u32[]{:S(2)}) copy-start(f32[768]{0:T(1024)} %convert_element_type.130) | copy-start | bytes 9220
  301.9 29.1 %copy-start.8 = (bf16[2048,768]{1,0:T(8,128)(2,1)}, bf16[2048,768]{1,0:T(8,128)(2,1)S(1)}, u32[]{:S(2)}) copy-start(bf16[2048,768]{1,0:T(8,128)(2,1)S(1)} %get-tuple-element.286) | copy-start | bytes 9437188
  330.9 19.3 %copy-start.16 = (f32[2048]{0:T(1024)S(1)}, f32[2048]{0:T(1024)}, u32[]{:S(2)}) copy-start(f32[2048]{0:T(1024)} %copy-done.15) | copy-start | bytes 24580
  354.9 5.7 copy-start.37
  380.2 6.3 copy-start.1
  380.3 296.2 %reduce-scatter.13.cloned.1.call-start = ((), (), s32[]{:S(2)}) async-start(), calls=%async_computation.11 | async-start | bytes 7299072
  557.3 260.5 %reduce-scatter.11.cloned.1.call-start = ((), (), s32[]{:S(2)}) async-start(), calls=%async_computation.10 | async-start | bytes 9732096 | tf_op jit(solution)/shard_map/reduce_scatter | solution.py:287
  573.6 386.5 %reduce-scatter.9.cloned.1.call-start = ((), (), s32[]{:S(2)}) async-start(), calls=%async_computation.9 | async-start | bytes 9732096 | tf_op jit(solution)/shard_map/reduce_scatter | solution.py:285
  593.0 5.7 copy-start.23
  593.0 5.7 copy-start.22
  593.0 5.7 copy-start.34
  593.0 5.7 copy-start.35
  593.0 5.7 copy-start.25
  593.1 5.7 copy-start.28
  593.1 52.4 %copy-start.19 = (f32[2048]{0:T(1024)S(1)}, f32[2048]{0:T(1024)}, u32[]{:S(2)}) copy-start(f32[2048]{0:T(1024)} %copy-done.18) | copy-start | bytes 24580
  (22 other events, 63.5 us)
Sparse Core Ops, SparseCore 0:
  11.0 63.0 all-gather.4
  77.1 53.1 all-gather.6
  133.3 62.5 all-gather.8
  198.8 62.4 all-gather.10
  380.4 98.2 reduce-scatter.6
  557.5 118.9 reduce-scatter.12
  683.0 134.8 reduce-scatter.10
  825.3 134.7 reduce-scatter.8
where the time goes:
time: 985 us; the launch traced here: 967 us
  matrix products  351 us (36%)
  waiting for transfers between devices  312 us (32%)
  local copies, waits for them, and re-layouts  126 us (13%)
  blocking collectives  83.9 us (9%)
  other arithmetic  77.9 us (8%)
  between operations  15.6 us (2%)
    reduce_scatter x1, waiting for transfers between devices, body(): lax.psum_scatter(terms[7], ('task', 'batch'), scatter_dimension=0, tiled=...  142 us
    reduce_scatter x1, waiting for transfers between devices, body(): lax.psum_scatter(terms[9], ('task', 'batch'), scatter_dimension=0, tiled=...  141 us
    unnamed x2, blocking collectives  83.9 us
    dot_general x1, matrix products, body(): jnp.dot(first_low, win_full, preferred_element_type=jnp.float32)  70.4 us
    dot_general x4, matrix products, right_product(): lax.dot_general(left, right, (((1,), (1,)), ((), ())), preferred_element_...  66.6 us
    dot_general x4, matrix products, left_product(): lax.dot_general(left, right, (((0,), (0,)), ((), ())), preferred_element_...  48.9 us
    unnamed x110, local copies, waits for them, and re-layouts  43.1 us
    dot_general x4, matrix products, attend_backward(): jnp.einsum('qhd,khd->hqk', grad_att, values_in, preferred_element_type=jn...  40.5 us
  transfers between devices with their start and end apart: 8, of which 4 were waited for; matrix products, arithmetic and copies ran while one was open for 45% of the time, Pallas kernels for 0%

commit v1 on v0

v1 whole, which is shorter than its diff:
```python
from functools import partial

import jax
import jax.numpy as jnp
from jax import lax
from jax.experimental import pallas as pl
from jax.experimental.pallas import tpu as pltpu
from jax.sharding import PartitionSpec as P

HEADS = 12
AXES = ("task", "batch")
F32 = jnp.float32
BF16 = jnp.bfloat16
VMEM_BYTES = 66_000_000
BQ, BV, BO, G1, S1, BD, G2, S2, BIN = range(9)
VECTORS = 12


def dot(left, right):
    return lax.dot_general(left, right, (((1,), (0,)), ((), ())), preferred_element_type=F32)


def dot_right(left, right):
    return lax.dot_general(left, right, (((1,), (1,)), ((), ())), preferred_element_type=F32)


def fill_mask(seg_ref, pad_ref, mask_ref):
    length = mask_ref.shape[0]
    seg_row = seg_ref[0].astype(F32)
    pad_row = pad_ref[0].astype(F32)
    seg_col = jnp.transpose(jnp.broadcast_to(seg_row, (128, length)))
    pad_col = jnp.transpose(jnp.broadcast_to(pad_row, (128, length)))
    key_at = lax.broadcasted_iota(jnp.int32, (length, 128), 0)
    lane = lax.broadcasted_iota(jnp.int32, (length, 128), 1)
    for block in range(length // 128):
        same = seg_col == seg_row[:, 128 * block : 128 * block + 128]
        seen = (pad_col == 1.0) | (key_at == lane + 128 * block)
        mask_ref[:, 128 * block : 128 * block + 128] = jnp.where(same & seen, 0.0, -1e30)


def forward_kernel(x_ref, w_ref, vec_ref, seg_ref, pad_ref, qkv_ref, att_ref, lse_ref, mask_ref):
    width = x_ref.shape[1]
    fill_mask(seg_ref, pad_ref, mask_ref)
    for part, row in enumerate((BQ, None, BV)):
        cols = slice(part * width, (part + 1) * width)
        product = dot(x_ref[...], w_ref[:, cols])
        if row is not None:
            product = product + vec_ref[row : row + 1, :]
        qkv_ref[:, cols] = product.astype(BF16)
    half = width // HEADS
    first_half = lax.broadcasted_iota(jnp.int32, (1, 2 * half), 1) < half

    def pair(index, carry):
        base = pl.multiple_of(index * 2 * half, 2 * half)
        queries = qkv_ref[:, pl.ds(base, 2 * half)]
        keys = qkv_ref[:, pl.ds(width + base, 2 * half)]
        values_t = jnp.transpose(qkv_ref[:, pl.ds(2 * width + base, 2 * half)])
        keys = keys * jnp.asarray(0.125, BF16)
        outs = []
        for head in range(2):
            mine = first_half if head == 0 else ~first_half
            scores = dot_right(jnp.where(mine, keys, jnp.zeros_like(keys)), queries)
            scores = scores + mask_ref[...]
            top = jnp.max(scores, 0, keepdims=True)
            expo = jnp.exp(scores - top)
            total = jnp.sum(expo, 0, keepdims=True)
            probs = (expo * (1.0 / total)).astype(BF16)
            outs.append(dot(values_t[head * half : (head + 1) * half], probs))
            lse_ref[0, pl.ds(2 * index + head, 1), :] = top + jnp.log(total)
        att_ref[:, pl.ds(base, 2 * half)] = jnp.transpose(jnp.concatenate(outs, 0)).astype(BF16)
        return carry

    lax.fori_loop(0, HEADS // 2, pair, 0)


def attention_forward(rows, w_qkv, vectors, segments, pads):
    seqs, _, length = segments.shape
    width = rows.shape[1]
    whole = lambda shape: pl.BlockSpec(shape, lambda i: (0,) * len(shape), pipeline_mode=pl.Buffered(1))
    row = lambda cols: pl.BlockSpec((length, cols), lambda i: (i, 0))
    tokens = pl.BlockSpec((1, 1, length), lambda i: (i, 0, 0))
    return pl.pallas_call(
        forward_kernel,
        name="attention_forward",
        grid=(seqs,),
        in_specs=[row(width), whole(w_qkv.shape), whole(vectors.shape), tokens, tokens],
        out_specs=[row(3 * width), row(width), pl.BlockSpec((1, 16, length), lambda i: (i, 0, 0))],
        out_shape=[
            jax.ShapeDtypeStruct((rows.shape[0], 3 * width), BF16),
            jax.ShapeDtypeStruct((rows.shape[0], width), BF16),
            jax.ShapeDtypeStruct((seqs, 16, length), F32),
        ],
        scratch_shapes=[pltpu.VMEM((length, length), F32)],
        compiler_params=pltpu.CompilerParams(vmem_limit_bytes=VMEM_BYTES),
        cost_estimate=pl.CostEstimate(flops=12_000_000_000, bytes_accessed=20_000_000, transcendentals=12_000_000),
    )(rows, w_qkv, vectors, segments, pads)


def norm_parts(arr):
    centre = arr - jnp.mean(arr, -1, keepdims=True)
    scale = lax.rsqrt(jnp.mean(centre * centre, -1, keepdims=True) + 1e-12)
    return centre * scale, scale


def norm_back(grad_normal, normal, scale):
    return scale * (
        grad_normal
        - jnp.mean(grad_normal, -1, keepdims=True)
        - normal * jnp.mean(grad_normal * normal, -1, keepdims=True)
    )


def column_sum(arr):
    return jnp.sum(arr.astype(F32), 0, keepdims=True)


def middle_kernel(
    scale_ref, x_ref, att_ref, cot_ref, wo_ref, win_ref, wd_ref, vec_ref, bin_ref,
    out_ref, sum_ref, datt_ref, gwo_ref, gwin_ref, gwd_ref, gvec_ref, gbin_ref,
    acc_wo, acc_win, acc_wd, act_ref, slope_ref,
):
    step = pl.program_id(0)
    width = x_ref.shape[1]
    hidden = win_ref.shape[1]
    chunks = hidden // width

    @pl.when(step == 0)
    def _():
        acc_wo[...] = jnp.zeros_like(acc_wo)
        acc_win[...] = jnp.zeros_like(acc_win)
        acc_wd[...] = jnp.zeros_like(acc_wd)
        gvec_ref[...] = jnp.zeros_like(gvec_ref)
        gbin_ref[...] = jnp.zeros_like(gbin_ref)

    vec = lambda row: vec_ref[row : row + 1, :]
    branch = dot(att_ref[...], wo_ref[...]) + vec(BO)
    normal_one, scale_one = norm_parts(x_ref[...].astype(F32) + branch)
    first = normal_one * vec(G1) + vec(S1)
    first_low = first.astype(BF16)
    second = first + vec(BD)
    for chunk in range(chunks):
        cols = slice(chunk * width, (chunk + 1) * width)
        pre = dot(first_low, win_ref[:, cols]) + bin_ref[:, cols]
        below = 0.5 + 0.5 * lax.erf(pre * 0.7071067811865476)
        act = (pre * below).astype(BF16)
        act_ref[:, cols] = act
        slope_ref[:, cols] = below + pre * (jnp.exp(pre * pre * -0.5) * 0.3989422804014327)
        second = second + dot(act, wd_ref[cols, :])
    normal_two, scale_two = norm_parts(second)
    out_ref[...] = (normal_two * vec(G2) + vec(S2)).astype(BF16)
    cot = cot_ref[...].astype(F32)
    gvec_ref[G2 : G2 + 1, :] += column_sum(cot * normal_two)
    gvec_ref[S2 : S2 + 1, :] += column_sum(cot)
    grad_second = norm_back(cot * vec(G2), normal_two, scale_two)
    grad_low = grad_second.astype(BF16)
    gvec_ref[BD : BD + 1, :] += column_sum(grad_low)
    first_t = jnp.transpose(first_low)
    grad_first = grad_second
    for chunk in range(chunks):
        cols = slice(chunk * width, (chunk + 1) * width)
        grad_pre = (slope_ref[:, cols] * dot_right(grad_low, wd_ref[cols, :])).astype(BF16)
        gbin_ref[:, cols] += column_sum(grad_pre)
        acc_wd[cols, :] += dot(jnp.transpose(act_ref[:, cols]), grad_low)
        acc_win[:, cols] += dot(first_t, grad_pre)
        grad_first = grad_first + dot_right(grad_pre, win_ref[:, cols])
    gvec_ref[G1 : G1 + 1, :] += column_sum(grad_first * normal_one)
    gvec_ref[S1 : S1 + 1, :] += column_sum(grad_first)
    grad_sum = norm_back(grad_first * vec(G1), normal_one, scale_one)
    sum_ref[...] = grad_sum
    grad_one = grad_sum.astype(BF16)
    gvec_ref[BO : BO + 1, :] += column_sum(grad_one)
    acc_wo[...] += dot(jnp.transpose(att_ref[...]), grad_one)
    datt_ref[...] = dot_right(grad_one, wo_ref[...]).astype(BF16)

    @pl.when(step == pl.num_programs(0) - 1)
    def _():
        weight = scale_ref[0]
        gwo_ref[...] = (acc_wo[...] * weight).astype(BF16)
        gwin_ref[...] = (acc_win[...] * weight).astype(BF16)
        gwd_ref[...] = (acc_wd[...] * weight).astype(BF16)
        gvec_ref[...] = gvec_ref[...] * weight
        gbin_ref[...] = gbin_ref[...] * weight


def middle(scale, rows, att, cot, w_out, w_in, w_down, vectors, b_in):
    count, width = rows.shape
    hidden = w_in.shape[1]
    tile = 256
    whole = lambda shape: pl.BlockSpec(shape, lambda i: (0,) * len(shape), pipeline_mode=pl.Buffered(1))
    row = pl.BlockSpec((tile, width), lambda i: (i, 0))
    shape = jax.ShapeDtypeStruct
    return pl.pallas_call(
        middle_kernel,
        name="middle",
        grid=(count // tile,),
        in_specs=[pl.BlockSpec(memory_space=pltpu.SMEM), row, row, row]
        + [whole(a.shape) for a in (w_out, w_in, w_down, vectors, b_in)],
        out_specs=[row, row, row]
        + [whole(s) for s in (w_out.shape, w_in.shape, w_down.shape, (16, width), (1, hidden))],
        out_shape=[
            shape((count, width), BF16),
            shape((count, width), F32),
            shape((count, width), BF16),
            shape(w_out.shape, BF16),
            shape(w_in.shape, BF16),
            shape(w_down.shape, BF16),
            shape((16, width), F32),
            shape((1, hidden), F32),
        ],
        scratch_shapes=[
            pltpu.VMEM(w_out.shape, F32),
            pltpu.VMEM(w_in.shape, F32),
            pltpu.VMEM(w_down.shape, F32),
            pltpu.VMEM((tile, hidden), BF16),
            pltpu.VMEM((tile, hidden), F32),
        ],
        compiler_params=pltpu.CompilerParams(vmem_limit_bytes=VMEM_BYTES),
        cost_estimate=pl.CostEstimate(flops=65_000_000_000, bytes_accessed=60_000_000, transcendentals=12_000_000),
    )(scale, rows, att, cot, w_out, w_in, w_down, vectors, b_in)


def backward_kernel(
    scale_ref, x_ref, qkv_ref, datt_ref, lse_ref, seg_ref, pad_ref, sum_ref, w_ref,
    gx_ref, gw_ref, gvec_ref, acc_ref, dqkv_ref, mask_ref,
):
    step = pl.program_id(0)
    width = x_ref.shape[1]
    half = width // HEADS
    fill_mask(seg_ref, pad_ref, mask_ref)
    first_half = lax.broadcasted_iota(jnp.int32, (1, 2 * half), 1) < half

    @pl.when(step == 0)
    def _():
        acc_ref[...] = jnp.zeros_like(acc_ref)
        gvec_ref[...] = jnp.zeros_like(gvec_ref)

    def pair(index, carry):
        base = pl.multiple_of(index * 2 * half, 2 * half)
        queries = qkv_ref[:, pl.ds(base, 2 * half)]
        keys = qkv_ref[:, pl.ds(width + base, 2 * half)]
        values = qkv_ref[:, pl.ds(2 * width + base, 2 * half)]
        grads = datt_ref[:, pl.ds(base, 2 * half)]
        keys_t = jnp.transpose(keys)
        keys = keys * jnp.asarray(0.125, BF16)
        grad_k = jnp.zeros(keys.shape, F32)
        grad_v = jnp.zeros(keys.shape, F32)
        grad_q = []
        for head in range(2):
            mine = first_half if head == 0 else ~first_half
            only = lambda arr: jnp.where(mine, arr, jnp.zeros_like(arr))
            scores = dot_right(only(keys), queries) + mask_ref[...]
            probs = jnp.exp(scores - lse_ref[0, pl.ds(2 * index + head, 1), :])
            grad_probs = dot_right(only(values), grads)
            inner = jnp.sum(probs * grad_probs, 0, keepdims=True)
            grad_scores = (probs * (grad_probs - inner)).astype(BF16)
            grad_v = grad_v + dot(probs.astype(BF16), only(grads))
            grad_k = grad_k + dot(grad_scores, only(queries))
            grad_q.append(dot(keys_t[head * half : (head + 1) * half], grad_scores))
        grad_q = jnp.transpose(jnp.concatenate(grad_q, 0))
        dqkv_ref[:, pl.ds(base, 2 * half)] = (grad_q * 0.125).astype(BF16)
        dqkv_ref[:, pl.ds(width + base, 2 * half)] = (grad_k * 0.125).astype(BF16)
        dqkv_ref[:, pl.ds(2 * width + base, 2 * half)] = grad_v.astype(BF16)
        return carry

    lax.fori_loop(0, HEADS // 2, pair, 0)
    x_t = jnp.transpose(x_ref[...])
    grad_x = sum_ref[...]
    for part in range(3):
        cols = slice(part * width, (part + 1) * width)
        grad = dqkv_ref[:, cols]
        acc_ref[:, cols] += dot(x_t, grad)
        grad_x = grad_x + dot_right(grad, w_ref[:, cols])
        if part != 1:
            row = BQ if part == 0 else BV
            gvec_ref[row : row + 1, :] += column_sum(grad)
    gx_ref[...] = grad_x

    @pl.when(step == pl.num_programs(0) - 1)
    def _():
        gw_ref[...] = (acc_ref[...] * scale_ref[0]).astype(BF16)
        gvec_ref[...] = gvec_ref[...] * scale_ref[0]


def attention_backward(scale, rows, qkv, datt, lse, segments, pads, grad_sum, w_qkv):
    seqs, _, length = segments.shape
    count, width = rows.shape
    whole = lambda shape: pl.BlockSpec(shape, lambda i: (0,) * len(shape), pipeline_mode=pl.Buffered(1))
    row = lambda cols: pl.BlockSpec((length, cols), lambda i: (i, 0))
    tokens = pl.BlockSpec((1, 1, length), lambda i: (i, 0, 0))
    shape = jax.ShapeDtypeStruct
    return pl.pallas_call(
        backward_kernel,
        name="attention_backward",
        grid=(seqs,),
        in_specs=[
            pl.BlockSpec(memory_space=pltpu.SMEM),
            row(width),
            row(3 * width),
            row(width),
            pl.BlockSpec((1, 16, length), lambda i: (i, 0, 0)),
            tokens,
            tokens,
            row(width),
            whole(w_qkv.shape),
        ],
        out_specs=[row(width), whole(w_qkv.shape), whole((8, width))],
        out_shape=[shape((count, width), F32), shape(w_qkv.shape, BF16), shape((8, width), F32)],
        scratch_shapes=[
            pltpu.VMEM(w_qkv.shape, F32),
            pltpu.VMEM((length, 3 * width), BF16),
            pltpu.VMEM((length, length), F32),
        ],
        compiler_params=pltpu.CompilerParams(vmem_limit_bytes=VMEM_BYTES),
        cost_estimate=pl.CostEstimate(flops=31_000_000_000, bytes_accessed=35_000_000, transcendentals=12_000_000),
    )(scale, rows, qkv, datt, lse, segments, pads, grad_sum, w_qkv)


def body(
    hidden_in, out_grad, segment_ids, pad_mask, task_weight, w_qkv, b_query, b_value, w_out, b_out,
    gain_one, shift_one, w_in, b_in, w_down, b_down, gain_two, shift_two,
):
    seqs, length, width = hidden_in.shape
    mine = w_qkv.shape[0]
    gather = partial(lax.all_gather, axis_name=AXES, axis=0, tiled=True)
    scatter = partial(lax.psum_scatter, axis_name=AXES, scatter_dimension=0, tiled=True)
    packed = jnp.stack([b_query, b_value, b_out, gain_one, shift_one, b_down, gain_two, shift_two], 1)
    packed = jnp.concatenate([packed, b_in.reshape(mine, -1)], 1)
    packed = jnp.pad(packed, ((0, 0), (0, 128 - packed.shape[1])))
    early = gather(jnp.concatenate([w_qkv, packed], 1))
    qkv_full = early[:, : 3 * width]
    vectors = jnp.transpose(early[:, 3 * width : 3 * width + 8].astype(F32))
    bin_full = early[:, 3 * width + BIN : 3 * width + VECTORS].astype(F32).reshape(1, -1)
    wo_full, win_full, wd_full = gather(w_out), gather(w_in), gather(w_down)
    rows = hidden_in.reshape(-1, width)
    segments = segment_ids.reshape(seqs, 1, length)
    pads = pad_mask.reshape(seqs, 1, length)
    qkv, att, lse = attention_forward(rows, qkv_full, vectors, segments, pads)
    hidden_out, grad_sum, datt, g_wo, g_win, g_wd, g_vec, g_bin = middle(
        task_weight, rows, att, out_grad.reshape(-1, width), wo_full, win_full, wd_full, vectors, bin_full
    )
    grad_x, g_qkv, g_vec_b = attention_backward(
        task_weight, rows, qkv, datt, lse, segments, pads, grad_sum, qkv_full
    )
    g_packed = jnp.concatenate([jnp.transpose(g_vec_b[:2]), jnp.transpose(g_vec[2:8]), g_bin.reshape(width, -1)], 1)
    g_packed = jnp.pad(g_packed, ((0, 0), (0, 128 - g_packed.shape[1]))).astype(BF16)
    late = scatter(jnp.concatenate([g_qkv, g_packed], 1)).astype(F32)
    vector = lambda row: late[:, 3 * width + row]
    return (
        hidden_out.reshape(hidden_in.shape),
        grad_x.reshape(hidden_in.shape),
        late[:, : 3 * width],
        vector(BQ),
        vector(BV),
        scatter(g_wo).astype(F32),
        vector(BO),
        vector(G1),
        vector(S1),
        scatter(g_win).astype(F32),
        late[:, 3 * width + BIN : 3 * width + VECTORS].reshape(-1),
        scatter(g_wd).astype(F32),
        vector(BD),
        vector(G2),
        vector(S2),
    )


def solution(mesh):
    seq, mat, vec = P(AXES, None, None), P(AXES, None), P(AXES)
    weights = (mat, vec, vec, mat, vec, vec, vec, mat, vec, mat, vec, vec, vec)
    return jax.shard_map(
        body,
        mesh=mesh,
        in_specs=(seq, seq, mat, mat, P("task")) + weights,
        out_specs=(seq, seq) + weights,
        check_vma=False,
    )
```

time: 985 us -> 791 us (0.80); the launches traced: 967 us -> 790 us
  matrix products: 351 us -> 0 us
  waiting for transfers between devices: 312 us -> 528 us
  Pallas kernels: 0 us -> 213 us
  local copies, waits for them, and re-layouts: 126 us -> 21.2 us
  blocking collectives: 83.9 us -> 0 us
  other arithmetic: 77.9 us -> 13.5 us
    dot_general x40 -> x0, matrix products: 351 us -> none  [the longest x1 70.4 us: body(): jnp.dot(first_low, win_full, preferred_element_type=jnp.float32)]
    pallas_call x0 -> x3, Pallas kernels: none -> 213 us  [the longest x1 93.6 us: middle(): pl.pallas_call(middle_kernel, name='middle', grid=(count // tile,), in_sp...]
    all_gather x4, waiting for transfers between devices: 9.21 us -> 193 us  [the longest x3 135 us: body(): wo_full, win_full, wd_full = (gather(w_out), gather(w_in), gather(w_down))]
    unnamed x9, waiting for transfers between devices: 19.3 us -> 105 us
    unnamed x2 -> x0, blocking collectives: 83.9 us -> none
    reduce_scatter x3, waiting for transfers between devices: 284 us -> 230 us  [the longest x1 111 us: body(): scatter(g_win).astype(F32)]
    unnamed x110 -> x2, local copies, waits for them, and re-layouts: 43.1 us -> 0.01 us
    reduce_sum x13 -> x0, other arithmetic: 31.8 us -> none  [the longest x4 10.3 us: attend_forward(): row_sum = jnp.sum(expo, -1, keepdims=True)]
  transfers between devices with their start and end apart: 8 -> 8, of which waited for: 4 -> 8; matrix products, arithmetic and copies ran while one was open for 45% -> 3% of each run, Pallas kernels for 0% -> 15%
where the time goes in v1:
time: 791 us; the launch traced here: 790 us
  waiting for transfers between devices  528 us (67%)
  Pallas kernels  213 us (27%)
  local copies, waits for them, and re-layouts  21.2 us (3%)
  between operations  14.9 us (2%)
  other arithmetic  13.5 us (2%)
    all_gather x3, waiting for transfers between devices, body(): wo_full, win_full, wd_full = (gather(w_out), gather(w_in), gather(w_down))  135 us
    reduce_scatter x1, waiting for transfers between devices, body(): scatter(g_win).astype(F32)  111 us
    reduce_scatter x1, waiting for transfers between devices, body(): scatter(g_wd).astype(F32)  107 us
    unnamed x9, waiting for transfers between devices  105 us
    pallas_call x1, Pallas kernels, middle(): pl.pallas_call(middle_kernel, name='middle', grid=(count // tile,), in_sp...  93.6 us
    pallas_call x1, Pallas kernels, attention_backward(): pl.pallas_call(backward_kernel, name='attention_backward', grid=(seqs,),...  74.7 us
    all_gather x1, waiting for transfers between devices, body(): early = gather(jnp.concatenate([w_qkv, packed], 1))  58.2 us
    pallas_call x1, Pallas kernels, attention_forward(): pl.pallas_call(forward_kernel, name='attention_forward', grid=(seqs,), in...  44.6 us
  transfers between devices with their start and end apart: 8, of which 8 were waited for; matrix products, arithmetic and copies ran while one was open for 3% of the time, Pallas kernels for 15%

profile of v1, /device:TPU:0, one launch (start us, length us, event | category | flops | bytes accessed | tf_op | source)
XLA Modules:
  0.0 790.4 jit_solution(7140078263203623319)
XLA Ops:
  14.1 1.6 fusion.6
  18.4 1.3 reshape.65.seg_ref
  19.7 1.3 reshape.66.pad_ref
  21.0 58.2 %all-gather.5.cloned.1.call-done = bf16[768,2432]{1,0:T(8,128)(2,1)} async-done(((bf16[24,2432]{1,0:T(8,128)(2,1)}), bf16[768,2432]{1,0:T(8,128)(2,1)}) %all-gather.5.cloned.1.call-update) | async-done | bytes 3735568 | tf_op jit(solution)/shard_map/all_gather | solution.py:329
  79.2 1.0 slice_convert_fusion
  80.3 0.9 reshape.75.bin_ref
  81.2 1.0 convert_bitcast_fusion
  82.9 4.1 slice.62.w_ref
  87.0 44.6 %attention_forward.1 = (bf16[2048,2304]{1,0:T(8,128)(2,1)}, bf16[2048,768]{1,0:T(8,128)(2,1)}, f32[4,16,512]{2,1,0:T(8,128)}) custom-call(bf16[2048,768]{1,0:T(8,128)(2,1)} %bitcast.27, bf16[768,2304]{1,0:T(8,128)(2,1)} %slice.62.w_ref, f32[8,768]{1,0:T(8,128)} %copy.77.vec_ref, s32[4,1,512]{2,1,0:T(1,128)} %reshape.65.seg_ref, s32[4,1,512]{2,1,0:T(1,128)} %reshape.66.pad_ref), custom_call_target="tpu_custom_call" | custom-call | flops 12000000000 | bytes 20000000 | tf_op jit(solution)/shard_map/attention_forward/pallas_call | solution.py:82
  131.6 3.8 all-gather.7.cloned.1.call-done.wo_ref
  135.3 65.7 %all-gather.9.cloned.1.call-done.win_ref = bf16[768,3072]{1,0:T(8,128)(2,1)} async-done(((bf16[24,3072]{1,0:T(8,128)(2,1)}), bf16[768,3072]{1,0:T(8,128)(2,1)}) %all-gather.9.cloned.1.call-update) | async-done | bytes 4718608 | tf_op jit(solution)/shard_map/all_gather | solution.py:333
  201.0 65.4 %all-gather.11.cloned.1.call-done.wd_ref = bf16[3072,768]{1,0:T(8,128)(2,1)} async-done(((bf16[96,768]{1,0:T(8,128)(2,1)}), bf16[3072,768]{1,0:T(8,128)(2,1)}) %all-gather.11.cloned.1.call-update) | async-done | bytes 4718608 | tf_op jit(solution)/shard_map/all_gather | solution.py:333
  266.4 93.6 %middle.1 = (bf16[2048,768]{1,0:T(8,128)(2,1)}, f32[2048,768]{1,0:T(8,128)}, bf16[2048,768]{1,0:T(8,128)(2,1)}, bf16[768,768]{1,0:T(8,128)(2,1)}, bf16[768,3072]...) custom-call(f32[1]{0:T(128)S(6)} %copy.81.scale_ref, ...), custom_call_target="tpu_custom_call" | custom-call | flops 65000001536 | bytes 60000000 | tf_op jit(solution)/shard_map/middle/pallas_call | solution.py:192
  360.0 74.7 %attention_backward.1 = (f32[2048,768]{1,0:T(8,128)}, bf16[768,2304]{1,0:T(8,128)(2,1)}, f32[8,768]{1,0:T(8,128)}) custom-call(f32[1]{0:T(128)S(6)} %copy.81.scale_ref, bf16[2048,768]{1,0:T(8,128)(2,1)} %bitcast.29, bf16[2048,2304]{1,0:T(8,128)(2,1)} %get-tuple-element.31.qkv_ref, bf16[2048,768]{1,0:T(8,128)(2,1)} %get-tuple-element.32.datt_ref, ...), custom_call_target="tpu_custom_call" | custom-call | flops 31000000512 | bytes 35000000 | tf_op jit(solution)/shard_map/attention_backward/pallas_call | solution.py:291
  437.3 4.1 pad_maximum_fusion
  442.9 12.3 %reduce-scatter.7.cloned.1.call-done = bf16[24,768]{1,0:T(8,128)(2,1)} async-done(((bf16[768,768]{1,0:T(8,128)(2,1)}), bf16[24,768]{1,0:T(8,128)(2,1)}) %reduce-scatter.7.cloned.1.call-update) | async-done | bytes 36880 | tf_op jit(solution)/shard_map/reduce_scatter | solution.py:354
  455.2 1.4 convert_element_type.20
  456.6 101.4 %reduce-scatter.13.cloned.1.call-done = bf16[24,2432]{1,0:T(8,128)(2,1)} async-done(((bf16[768,2432]{1,0:T(8,128)(2,1)}), bf16[24,2432]{1,0:T(8,128)(2,1)}) %reduce-scatter.13.cloned.1.call-update) | async-done | bytes 116752
  559.4 1.6 slice.67
  561.0 0.9 convert_element_type.19
  562.8 106.7 %reduce-scatter.11.cloned.1.call-done = bf16[96,768]{1,0:T(8,128)(2,1)} async-done(((bf16[3072,768]{1,0:T(8,128)(2,1)}), bf16[96,768]{1,0:T(8,128)(2,1)}) %reduce-scatter.11.cloned.1.call-update) | async-done | bytes 147472 | tf_op jit(solution)/shard_map/reduce_scatter | solution.py:360
  669.5 1.6 convert_element_type.22
  671.1 110.8 %reduce-scatter.9.cloned.1.call-done = bf16[24,3072]{1,0:T(8,128)(2,1)} async-done(((bf16[768,3072]{1,0:T(8,128)(2,1)}), bf16[24,3072]{1,0:T(8,128)(2,1)}) %reduce-scatter.9.cloned.1.call-update) | async-done | bytes 147472 | tf_op jit(solution)/shard_map/reduce_scatter | solution.py:358
  781.9 1.6 convert_element_type.21
  (39 shorter events, 16.0 us)
Async XLA Ops:
  7.2 72.1 %all-gather.5.cloned.1.call-start = ((), (), s32[]{:S(2)}) async-start(), calls=%async_computation.4 | async-start | bytes 3852288 | tf_op jit(solution)/shard_map/all_gather | solution.py:329
  15.7 119.7 %all-gather.7.cloned.1.call-start = ((), (), s32[]{:S(2)}) async-start(), calls=%async_computation.5 | async-start | bytes 1216512 | tf_op jit(solution)/shard_map/all_gather | solution.py:333
  16.4 184.6 %all-gather.9.cloned.1.call-start = ((), (), s32[]{:S(2)}) async-start(), calls=%async_computation.6 | async-start | bytes 4866048 | tf_op jit(solution)/shard_map/all_gather | solution.py:333
  17.1 249.2 %all-gather.11.cloned.1.call-start = ((), (), s32[]{:S(2)}) async-start(), calls=%async_computation.7 | async-start | bytes 4866048 | tf_op jit(solution)/shard_map/all_gather | solution.py:333
  17.7 437.5 %reduce-scatter.7.cloned.1.call-start = ((), (), s32[]{:S(2)}) async-start(), calls=%async_computation.8 | async-start | bytes 1216512 | tf_op jit(solution)/shard_map/reduce_scatter | solution.py:354
  360.0 198.1 %reduce-scatter.13.cloned.1.call-start = ((), (), s32[]{:S(2)}) async-start(), calls=%async_computation.11 | async-start | bytes 3852288
  360.0 75.7 %copy-start = (f32[1,3072]{1,0:T(1,128)S(1)}, f32[1,3072]{1,0:T(1,128)}, u32[]{:S(2)}) copy-start(f32[1,3072]{1,0:T(1,128)} %get-tuple-element.39) | copy-start | bytes 36868
  441.4 228.0 %reduce-scatter.11.cloned.1.call-start = ((), (), s32[]{:S(2)}) async-start(), calls=%async_computation.10 | async-start | bytes 4866048 | tf_op jit(solution)/shard_map/reduce_scatter | solution.py:360
  442.2 339.7 %reduce-scatter.9.cloned.1.call-start = ((), (), s32[]{:S(2)}) async-start(), calls=%async_computation.9 | async-start | bytes 4866048 | tf_op jit(solution)/shard_map/reduce_scatter | solution.py:358
Sparse Core Ops, SparseCore 0:
  15.8 63.4 all-gather.4
  82.3 53.0 all-gather.6
  138.4 62.5 all-gather.8
  203.9 62.4 all-gather.10
  360.1 95.0 reduce-scatter.6
  460.7 97.2 reduce-scatter.12
  563.5 105.9 reduce-scatter.10
  675.8 106.0 reduce-scatter.8

commit v2 on v1

--- a/solution.py
+++ b/solution.py
@@ -14,6 +14,434 @@
 VMEM_BYTES = 66_000_000
 BQ, BV, BO, G1, S1, BD, G2, S2, BIN = range(9)
 VECTORS = 12
+
+
+MESH = pl.DeviceIdType.MESH
+
+
+class Place:
+    def __init__(self):
+        self.task = lax.axis_index("task")
+        self.batch = lax.axis_index("batch")
+        self.core = self.batch % 2
+        self.z = self.batch // 2
+        x, y = self.task % 2, self.task // 2
+        flip_x, flip_y = self.task + 1 - 2 * x, self.task + 2 - 4 * y
+        self.task_a = (1 - self.core) * flip_x + self.core * flip_y
+        self.task_b = (1 - self.core) * flip_y + self.core * flip_x
+        self.task_ab = 3 - self.task
+        self.partner = (self.task, self.batch + 1 - 2 * self.core)
+        self.peer_a = (self.task_a, self.batch)
+        self.peer_b = (self.task_b, self.batch)
+        self.above = (self.task, self.batch + 2)
+        self.below = (self.task, self.batch - 2)
+
+    def device(self, task, z):
+        return task * 8 + z * 2
+
+    def meet(self):
+        barrier = pltpu.get_barrier_semaphore()
+        for peer in (self.partner, self.peer_a, self.peer_b):
+            pl.semaphore_signal(barrier, inc=1, device_id=peer, device_id_type=MESH)
+
+        @pl.when(self.z < 3)
+        def _():
+            pl.semaphore_signal(barrier, inc=1, device_id=self.above, device_id_type=MESH)
+
+        @pl.when(self.z > 0)
+        def _():
+            pl.semaphore_signal(barrier, inc=1, device_id=self.below, device_id_type=MESH)
+
+        pl.semaphore_wait(barrier, 4 + self.z * (3 - self.z) // 2)
+
+
+GATHER_SEMS = [
+    pltpu.SemaphoreType.DMA((16,)),
+    pltpu.SemaphoreType.DMA((16,)),
+    pltpu.SemaphoreType.DMA((14,)),
+    pltpu.SemaphoreType.DMA((4,)),
+]
+
+
+class Gather:
+    def __init__(self, place, shard, full, sems):
+        self.place, self.shard, self.full = place, shard, full
+        self.send, self.recv, self.recv_b, self.misc = sems
+        self.half = shard.shape[1] // 2
+
+    def chunk(self, task, z):
+        start = pl.multiple_of(self.place.core * self.half, 128)
+        first = self.place.device(task, z)
+        return self.full.at[pl.ds(first, 2), :, pl.ds(start, self.half)]
+
+    def copy(self, ref, send, recv, peer):
+        return pltpu.make_async_remote_copy(ref, ref, send, recv, device_id=peer, device_id_type=MESH)
+
+    def own(self):
+        place = self.place
+        return self.full.at[place.task * 8 + place.batch]
+
+    def begin(self):
+        place = self.place
+        pltpu.make_async_copy(self.shard, self.own(), self.misc.at[0]).start()
+        pltpu.make_async_remote_copy(
+            self.shard, self.own(), self.send.at[0], self.recv.at[0], device_id=place.partner, device_id_type=MESH
+        ).start()
+
+    def to_z(self, task, z, index, up, start):
+        slot = 2 + index + (0 if up else 6)
+        peer = self.place.above if up else self.place.below
+        copy = self.copy(self.chunk(task, z), self.send.at[slot], self.recv.at[slot], peer)
+        copy.start() if start else copy.wait_send()
+
+    def to_b(self, task, z, index):
+        self.copy(self.chunk(task, z), self.misc.at[1], self.recv_b.at[index], self.place.peer_b).start()
+
+    def hand_over(self, task, z):
+        self.copy(self.chunk(task, z), self.misc.at[2], self.misc.at[3], self.place.partner).start()
+
+    def spread(self):
+        place = self.place
+        pltpu.make_async_copy(self.shard, self.own(), self.misc.at[0]).wait()
+        other = self.full.at[place.task * 8 + place.partner[1]]
+        self.copy(other, self.send.at[0], self.recv.at[0], place.partner).wait_recv()
+        self.copy(self.chunk(place.task, place.z), self.send.at[1], self.recv.at[1], place.peer_a).start()
+        self.both_ways(place.task, place.z, 0)
+        self.to_b(place.task, place.z, 0)
+
+    def both_ways(self, task, z, index, start=True):
+        @pl.when(self.place.z < 3)
+        def _():
+            self.to_z(task, z, index, True, start)
+
+        @pl.when(self.place.z > 0)
+        def _():
+            self.to_z(task, z, index, False, start)
+
+    def from_a(self):
+        place = self.place
+        self.copy(self.chunk(place.task_a, place.z), self.send.at[1], self.recv.at[1], place.peer_a).wait_recv()
+        self.both_ways(place.task_a, place.z, 1)
+        self.to_b(place.task_a, place.z, 1)
+        self.hand_over(place.task_a, place.z)
+
+    def along_z(self, far, which):
+        place = self.place
+        task = place.task if which == 0 else place.task_a
+        index = 2 * (far - 1) + which
+        for up in (True, False):
+            z = place.z - far if up else place.z + far
+            here = (place.z >= far) if up else (place.z + far <= 3)
+            more = (place.z < 3) if up else (place.z > 0)
+            slot = 2 + index + (0 if up else 6)
+
+            @pl.when(here)
+            def _():
+                self.copy(self.chunk(task, z), self.send.at[slot], self.recv.at[slot], place.partner).wait_recv()
+                if far < 3:
+
+                    @pl.when(more)
+                    def _():
+                        self.to_z(task, z, index + 2, up, True)
+
+                self.to_b(task, z, 2 + index + (0 if up else 6))
+                self.hand_over(task, z)
+
+    def from_b(self, index):
+        place = self.place
+        if index < 2:
+            task = place.task_b if index == 0 else place.task_ab
+            self.arrived_b(task, place.z, index)
+            return
+        up, far, which = index < 8, (index - 2) % 6 // 2 + 1, index % 2
+        task = place.task_b if which == 0 else place.task_ab
+        z = place.z - far if up else place.z + far
+
+        @pl.when((place.z >= far) if up else (place.z + far <= 3))
+        def _():
+            self.arrived_b(task, z, index)
+
+    def arrived_b(self, task, z, index):
+        self.copy(self.chunk(task, z), self.misc.at[1], self.recv_b.at[index], self.place.peer_b).wait_recv()
+        self.hand_over(task, z)
+
+    def finish(self):
+        place = self.place
+        start = pl.multiple_of(place.core * self.half, 128)
+        other = pl.multiple_of((1 - place.core) * self.half, 128)
+        rest = self.full.at[pl.ds(0, 30), :, pl.ds(other, self.half)]
+        self.copy(rest, self.misc.at[2], self.misc.at[3], place.partner).wait_recv()
+        mine = self.full.at[pl.ds(0, 30), :, pl.ds(start, self.half)]
+        self.copy(mine, self.misc.at[2], self.misc.at[3], place.partner).wait_send()
+        eight = self.full.at[pl.ds(0, 16), :, pl.ds(start, self.half)]
+        self.copy(eight, self.misc.at[1], self.recv_b.at[0], place.peer_b).wait_send()
+        self.copy(self.shard, self.send.at[0], self.recv.at[0], place.partner).wait_send()
+        self.copy(self.chunk(place.task, place.z), self.send.at[1], self.recv.at[1], place.peer_a).wait_send()
+        self.both_ways(place.task, place.z, 0, False)
+        self.both_ways(place.task_a, place.z, 1, False)
+        for far in (1, 2):
+            for which in (0, 1):
+                task = place.task if which == 0 else place.task_a
+                index = 2 * (far - 1) + which
+
+                @pl.when((place.z >= far) & (place.z < 3))
+                def _():
+                    self.to_z(task, place.z - far, index + 2, True, False)
+
+                @pl.when((place.z + far <= 3) & (place.z > 0))
+                def _():
+                    self.to_z(task, place.z + far, index + 2, False, False)
+
+    def events(self):
+        out = [self.begin, self.spread, self.from_a]
+        out += [partial(self.along_z, 1, 0), partial(self.along_z, 1, 1), partial(self.from_b, 0), partial(self.from_b, 1)]
+        out += [partial(self.along_z, 2, 0), partial(self.along_z, 2, 1)]
+        out += [partial(self.from_b, i) for i in (2, 8, 3, 9)]
+        out += [partial(self.along_z, 3, 0), partial(self.along_z, 3, 1)]
+        out += [partial(self.from_b, i) for i in (4, 10, 5, 11, 6, 12, 7, 13)]
+        return out + [self.finish]
+
+
+def gather_kernel(count, *refs):
+    shards, fulls, sems = refs[:count], refs[count : 2 * count], refs[2 * count :]
+    place = Place()
+    place.meet()
+    jobs = [Gather(place, shards[i], fulls[i], sems[4 * i : 4 * i + 4]).events() for i in range(count)]
+    for step in range(len(jobs[0]) + count - 1):
+        for i in range(count):
+            if 0 <= step - i < len(jobs[i]):
+                jobs[i][step - i]()
+
+
+def gather_all(shards, identity):
+    count = len(shards)
+    place = pl.BlockSpec(memory_space=pl.ANY)
+    return pl.pallas_call(
+        partial(gather_kernel, count),
+        name="gather",
+        in_specs=[place] * count,
+        out_specs=[place] * count,
+        out_shape=[jax.ShapeDtypeStruct((32, *s.shape), s.dtype) for s in shards],
+        scratch_shapes=GATHER_SEMS * count,
+        compiler_params=pltpu.CompilerParams(collective_id=identity, has_side_effects=True),
+    )(*shards)
+
+
+SCATTER_SEMS = [
+    pltpu.SemaphoreType.DMA((4,)),
+    pltpu.SemaphoreType.DMA((4,)),
+    pltpu.SemaphoreType.DMA((4,)),
+    pltpu.SemaphoreType.DMA((8,)),
+    pltpu.SemaphoreType.DMA((8,)),
+    pltpu.SemaphoreType.DMA((8,)),
+    pltpu.SemaphoreType.DMA((10,)),
+    pltpu.SemaphoreType.DMA((4,)),
+]
+
+
+def scatter_buffers(rows, cols):
+    half = cols // 2
+    return [
+        pltpu.VMEM((16, rows, half), BF16),
+        pltpu.VMEM((16, rows, half), BF16),
+        pltpu.VMEM((8, rows, half), BF16),
+        pltpu.VMEM((10, rows, half), BF16),
+        pltpu.VMEM((rows, half), BF16),
+        pltpu.VMEM((rows, half), F32),
+        pltpu.VMEM((rows // 2, half), F32),
+    ] + SCATTER_SEMS
+
+
+class Scatter:
+    def __init__(self, place, terms, out, buffers):
+        self.place, self.terms, self.out = place, terms, out
+        (self.own, self.other, self.got_b, self.got_z, self.got_a, self.total, self.got_f) = buffers[:7]
+        (self.s_load, self.s_pair, self.r_pair, self.s_b, self.r_b, self.s_z, self.r_z, self.misc) = buffers[7:]
+        self.half = self.own.shape[2]
+        place_ = place
+        self.tasks = (place_.task_ab, place_.task_b, place_.task_a, place_.task)
+        self.tasks_partner = (place_.task_ab, place_.task_a, place_.task_b, place_.task)
+        self.low = 1 - place_.z // 2
+        self.inner = self.low * place_.z + (1 - self.low) * (3 - place_.z)
+        self.far = (place_.task, place_.batch + 4 * self.low - 2)
+        self.near = (place_.task, place_.batch + 2 - 4 * self.low)
+
+    def cols(self, core):
+        return pl.ds(pl.multiple_of(core * self.half, 128), self.half)
+
+    def remote(self, src, dst, send, recv, peer):
+        return pltpu.make_async_remote_copy(src, dst, send, recv, device_id=peer, device_id_type=MESH)
+
+    def load(self, index):
+        first = self.tasks[index] * 4
+        return pltpu.make_async_copy(
+            self.terms.at[pl.ds(first, 4), :, self.cols(self.place.core)],
+            self.own.at[pl.ds(first, 4)],
+            self.s_load.at[index],
+        )
+
+    def pair(self, index, sent=True):
+        first = (self.tasks_partner if sent else self.tasks)[index] * 4
+        return self.remote(
+            self.terms.at[pl.ds(first, 4), :, self.cols(1 - self.place.core)],
+            self.other.at[pl.ds(first, 4)],
+            self.s_pair.at[index],
+            self.r_pair.at[index],
+            self.place.partner,
+        )
+
+    def begin(self):
+        for index in range(4):
+            self.load(index).start()
+            self.pair(index).start()
+
+    def add(self, at, ref, where):
+        self.own[at] = (self.own[at].astype(F32) + ref[where].astype(F32)).astype(BF16)
+
+    def along_b(self, which, z):
+        at = self.tasks[which] * 4 + z
+        slot = which * 4 + z
+        return self.remote(
+            self.own.at[at], self.got_b.at[slot], self.s_b.at[slot], self.r_b.at[slot], self.place.peer_b
+        )
+
+    def add_pair(self, index):
+        self.load(index).wait()
+        self.pair(index, False).wait_recv()
+        first = self.tasks[index] * 4
+        for m in (3, 2, 1, 0):
+            z = self.level(m)
+            self.add(first + z, self.other, first + z)
+            if index < 2:
+                self.along_b(index, z).start()
+
+    def add_b(self, which, z):
+        self.along_b(which, z).wait_recv()
+        self.add(self.tasks[2 + which] * 4 + z, self.got_b, which * 4 + z)
+
+    def level(self, m):
+        return self.low * m + (1 - self.low) * (3 - m)
+
+    def along_z(self, which, m, far):
+        at = self.tasks[2 + which] * 4 + self.level(m)
+        into = 5 * which + ((1 - self.inner) * (m - 1) + self.inner * (6 - m) if far else 3 + m)
+        peer = self.far if far else self.near
+        return self.remote(
+            self.own.at[at], self.got_z.at[into], self.s_z.at[which * 4 + m], self.r_z.at[into], peer
+        )
+
+    def add_z(self, which, m, slot):
+        into = 5 * which + slot
+        self.remote(
+            self.got_z.at[into], self.got_z.at[into], self.s_z.at[0], self.r_z.at[into], self.place.partner
+        ).wait_recv()
+        self.add(self.tasks[2 + which] * 4 + self.level(m), self.got_z, into)
+
+    def step_far(self, which, m):
+        @pl.when(self.inner == 1)
+        def _():
+            self.add_z(which, m, m - 1)
+
+        @pl.when(self.inner < m)
+        def _():
+            self.along_z(which, m, True).start()
+
+    def step_near(self, which, m):
+        @pl.when(self.inner >= m)
+        def _():
+            self.add_z(which, m, 3 + m)
+
+        @pl.when(self.inner > m)
+        def _():
+            self.along_z(which, m, False).start()
+
+    def along_a(self):
+        at = self.tasks[2] * 4 + self.place.z
+        return self.remote(self.own.at[at], self.got_a, self.misc.at[0], self.misc.at[1], self.place.peer_a)
+
+    def to_a(self):
+        self.along_a().start()
+
+    def last(self):
+        rows = self.got_f.shape[0]
+        away = pl.multiple_of((1 - self.place.core) * rows, rows)
+        return self.remote(
+            self.total.at[pl.ds(away, rows)], self.got_f, self.misc.at[2], self.misc.at[3], self.place.partner
+        )
+
+    def add_a(self):
+        self.along_a().wait_recv()
+        self.total[...] = self.own[self.tasks[3] * 4 + self.place.z].astype(F32) + self.got_a[...].astype(F32)
+        self.last().start()
+
+    def finish(self):
+        rows = self.got_f.shape[0]
+        core = self.place.core
+        self.last().wait_recv()
+        self.out[:, self.cols(core)] = self.total[pl.ds(pl.multiple_of(core * rows, rows), rows), :]
+        self.out[:, self.cols(1 - core)] = self.got_f[...]
+        for index in range(4):
+            self.pair(index).wait_send()
+        for which in range(2):
+            for z in range(4):
+                self.along_b(which, z).wait_send()
+
+                @pl.when(self.inner < z)
+                def _():
+                    self.along_z(which, z, True).wait_send()
+
+                @pl.when(self.inner > z)
+                def _():
+                    self.along_z(which, z, False).wait_send()
+
+        self.along_a().wait_send()
+        self.last().wait_send()
+
+    def add_b_far(self, which, m):
+        self.add_b(which, self.level(m))
+
+    def events(self):
+        out = [self.begin] + [partial(self.add_pair, i) for i in range(4)]
+        for which in range(2):
+            for m in (3, 2, 1):
+                out += [partial(self.add_b_far, which, m), partial(self.step_far, which, m)]
+            out.append(partial(self.add_b_far, which, 0))
+        for which in range(2):
+            out += [partial(self.step_near, which, m) for m in range(2)]
+            if which == 0:
+                out.append(self.to_a)
+        return out + [self.add_a, self.finish]
+
+
+def scatter_kernel(count, *refs):
+    terms, outs, scratch = refs[:count], refs[count : 2 * count], refs[2 * count :]
+    place = Place()
+    place.meet()
+    size = len(scratch) // count
+    jobs = [Scatter(place, terms[i], outs[i], scratch[size * i : size * i + size]).events() for i in range(count)]
+    lag = 6
+    for step in range(len(jobs[0]) + lag * (count - 1)):
+        for i in range(count):
+            if 0 <= step - lag * i < len(jobs[i]):
+                jobs[i][step - lag * i]()
+
+
+def scatter_all(terms, identity):
+    count = len(terms)
+    scratch = []
+    for t in terms:
+        scratch += scatter_buffers(*t.shape[1:])
+    return pl.pallas_call(
+        partial(scatter_kernel, count),
+        name="scatter",
+        in_specs=[pl.BlockSpec(memory_space=pl.ANY)] * count,
+        out_specs=[pl.BlockSpec(memory_space=pltpu.VMEM)] * count,
+        out_shape=[jax.ShapeDtypeStruct((t.shape[1] // 2, t.shape[2]), F32) for t in terms],
+        scratch_shapes=scratch,
+        compiler_params=pltpu.CompilerParams(
+            collective_id=identity, has_side_effects=True, vmem_limit_bytes=66_000_000
+        ),
+    )(*terms)
 
 
 def dot(left, right):
@@ -83,7 +511,7 @@
         forward_kernel,
         name="attention_forward",
         grid=(seqs,),
-        in_specs=[row(width), whole(w_qkv.shape), whole(vectors.shape), tokens, tokens],
+        in_specs=[row(width), whole((width, 3 * width)), whole(vectors.shape), tokens, tokens],
         out_specs=[row(3 * width), row(width), pl.BlockSpec((1, 16, length), lambda i: (i, 0, 0))],
         out_shape=[
             jax.ShapeDtypeStruct((rows.shape[0], 3 * width), BF16),
@@ -220,8 +648,8 @@
 
 
 def backward_kernel(
-    scale_ref, x_ref, qkv_ref, datt_ref, lse_ref, seg_ref, pad_ref, sum_ref, w_ref,
-    gx_ref, gw_ref, gvec_ref, acc_ref, dqkv_ref, mask_ref,
+    scale_ref, x_ref, qkv_ref, datt_ref, lse_ref, seg_ref, pad_ref, sum_ref, w_ref, rest_ref,
+    gx_ref, gw_ref, acc_ref, gvec_ref, dqkv_ref, mask_ref,
 ):
     step = pl.program_id(0)
     width = x_ref.shape[1]
@@ -277,11 +705,14 @@
 
     @pl.when(step == pl.num_programs(0) - 1)
     def _():
-        gw_ref[...] = (acc_ref[...] * scale_ref[0]).astype(BF16)
-        gvec_ref[...] = gvec_ref[...] * scale_ref[0]
-
-
-def attention_backward(scale, rows, qkv, datt, lse, segments, pads, grad_sum, w_qkv):
+        gw_ref[:, : 3 * width] = (acc_ref[...] * scale_ref[0]).astype(BF16)
+        gvec_ref[:2] = gvec_ref[:2] * scale_ref[0]
+        gvec_ref[2:VECTORS] = rest_ref[2:VECTORS]
+        gw_ref[:, 3 * width : 3 * width + 128] = jnp.transpose(gvec_ref[...]).astype(BF16)
+        gw_ref[:, 3 * width + 128 :] = jnp.zeros((width, gw_ref.shape[1] - 3 * width - 128), BF16)
+
+
+def attention_backward(scale, rows, qkv, datt, lse, segments, pads, grad_sum, w_qkv, rest):
     seqs, _, length = segments.shape
     count, width = rows.shape
     whole = lambda shape: pl.BlockSpec(shape, lambda i: (0,) * len(shape), pipeline_mode=pl.Buffered(1))
@@ -301,18 +732,20 @@
             tokens,
             tokens,
             row(width),
-            whole(w_qkv.shape),
+            whole((width, 3 * width)),
+            whole(rest.shape),
         ],
-        out_specs=[row(width), whole(w_qkv.shape), whole((8, width))],
-        out_shape=[shape((count, width), F32), shape(w_qkv.shape, BF16), shape((8, width), F32)],
+        out_specs=[row(width), whole(w_qkv.shape)],
+        out_shape=[shape((count, width), F32), shape(w_qkv.shape, BF16)],
         scratch_shapes=[
-            pltpu.VMEM(w_qkv.shape, F32),
+            pltpu.VMEM((width, 3 * width), F32),
+            pltpu.VMEM((128, width), F32),
             pltpu.VMEM((length, 3 * width), BF16),
             pltpu.VMEM((length, length), F32),
         ],
         compiler_params=pltpu.CompilerParams(vmem_limit_bytes=VMEM_BYTES),
         cost_estimate=pl.CostEstimate(flops=31_000_000_000, bytes_accessed=35_000_000, transcendentals=12_000_000),
-    )(scale, rows, qkv, datt, lse, segments, pads, grad_sum, w_qkv)
+    )(scale, rows, qkv, datt, lse, segments, pads, grad_sum, w_qkv, rest)
 
 
 def body(
@@ -321,29 +754,39 @@
 ):
     seqs, length, width = hidden_in.shape
     mine = w_qkv.shape[0]
-    gather = partial(lax.all_gather, axis_name=AXES, axis=0, tiled=True)
-    scatter = partial(lax.psum_scatter, axis_name=AXES, scatter_dimension=0, tiled=True)
+    near = lax.axis_size("task") == 4 and lax.axis_size("batch") == 8 and mine % 8 == 0
     packed = jnp.stack([b_query, b_value, b_out, gain_one, shift_one, b_down, gain_two, shift_two], 1)
     packed = jnp.concatenate([packed, b_in.reshape(mine, -1)], 1)
-    packed = jnp.pad(packed, ((0, 0), (0, 128 - packed.shape[1])))
-    early = gather(jnp.concatenate([w_qkv, packed], 1))
-    qkv_full = early[:, : 3 * width]
+    packed = jnp.pad(packed, ((0, 0), (0, 256 - packed.shape[1])))
+    shards = [jnp.concatenate([w_qkv, packed], 1), w_out, w_in, w_down]
+    if near:
+        full = gather_all(shards[:1], 0) + gather_all(shards[1:], 1)
+        full = [f.reshape(-1, f.shape[-1]) for f in full]
+    else:
+        full = [lax.all_gather(s, AXES, axis=0, tiled=True) for s in shards]
+    early, wo_full, win_full, wd_full = full
     vectors = jnp.transpose(early[:, 3 * width : 3 * width + 8].astype(F32))
     bin_full = early[:, 3 * width + BIN : 3 * width + VECTORS].astype(F32).reshape(1, -1)
-    wo_full, win_full, wd_full = gather(w_out), gather(w_in), gather(w_down)
     rows = hidden_in.reshape(-1, width)
     segments = segment_ids.reshape(seqs, 1, length)
     pads = pad_mask.reshape(seqs, 1, length)
-    qkv, att, lse = attention_forward(rows, qkv_full, vectors, segments, pads)
+    qkv, att, lse = attention_forward(rows, early, vectors, segments, pads)
     hidden_out, grad_sum, datt, g_wo, g_win, g_wd, g_vec, g_bin = middle(
         task_weight, rows, att, out_grad.reshape(-1, width), wo_full, win_full, wd_full, vectors, bin_full
     )
-    grad_x, g_qkv, g_vec_b = attention_backward(
-        task_weight, rows, qkv, datt, lse, segments, pads, grad_sum, qkv_full
+    g_rest = jnp.concatenate([g_vec[:8], jnp.transpose(g_bin.reshape(width, -1)), g_vec[8:12]], 0)
+    grad_x, g_qkv = attention_backward(
+        task_weight, rows, qkv, datt, lse, segments, pads, grad_sum, early, g_rest
     )
-    g_packed = jnp.concatenate([jnp.transpose(g_vec_b[:2]), jnp.transpose(g_vec[2:8]), g_bin.reshape(width, -1)], 1)
-    g_packed = jnp.pad(g_packed, ((0, 0), (0, 128 - g_packed.shape[1]))).astype(BF16)
-    late = scatter(jnp.concatenate([g_qkv, g_packed], 1)).astype(F32)
+    terms = [g_qkv, g_wd, g_win, g_wo]
+    if near:
+        late, s_wd, s_win, s_wo = scatter_all([t.reshape(16, -1, t.shape[1]) for t in terms[:1]], 2) + scatter_all(
+            [t.reshape(16, -1, t.shape[1]) for t in terms[1:]], 3
+        )
+    else:
+        late, s_wd, s_win, s_wo = [
+            lax.psum_scatter(t, AXES, scatter_dimension=0, tiled=True).astype(F32) for t in terms
+        ]
     vector = lambda row: late[:, 3 * width + row]
     return (
         hidden_out.reshape(hidden_in.shape),
@@ -351,13 +794,13 @@
         late[:, : 3 * width],
         vector(BQ),
         vector(BV),
-        scatter(g_wo).astype(F32),
+        s_wo,
         vector(BO),
         vector(G1),
         vector(S1),
-        scatter(g_win).astype(F32),
+        s_win,
         late[:, 3 * width + BIN : 3 * width + VECTORS].reshape(-1),
-        scatter(g_wd).astype(F32),
+        s_wd,
         vector(BD),
         vector(G2),
         vector(S2),

time: 791 us -> 458 us (0.58)
  waiting for transfers between devices: 528 us -> 0 us
  Pallas kernels: 213 us -> 433 us
  between operations: 14.9 us -> 1.46 us
  other arithmetic: 13.5 us -> 4.87 us
    reduce_scatter x3 -> x0, waiting for transfers between devices: 230 us -> none  [the longest x1 111 us: body(): scatter(g_win).astype(F32)]
    pallas_call x0 -> x4, Pallas kernels: none -> 220 us  [the longest x2 126 us: scatter_all(): pl.pallas_call(partial(scatter_kernel, count), name='scatter', in_specs=[...]
    all_gather x4 -> x0, waiting for transfers between devices: 193 us -> none  [the longest x3 135 us: body(): wo_full, win_full, wd_full = (gather(w_out), gather(w_in), gather(w_down))]
    unnamed x9 -> x0, waiting for transfers between devices: 105 us -> none
  transfers between devices with their start and end apart: 8 -> 0, of which waited for: 8 -> 0; matrix products, arithmetic and copies ran while one was open for 3% -> 0% of each run, Pallas kernels for 15% -> 0%
where the time goes in v2:
time: 458 us; the launch traced here: 457 us
  Pallas kernels  433 us (95%)
  local copies, waits for them, and re-layouts  17.6 us (4%)
  other arithmetic  4.87 us (1%)
    pallas_call x2, Pallas kernels, scatter_all(): pl.pallas_call(partial(scatter_kernel, count), name='scatter', in_specs=[...  126 us
    pallas_call x2, Pallas kernels, gather_all(): pl.pallas_call(partial(gather_kernel, count), name='gather', in_specs=[pl...  93.9 us
    pallas_call x1, Pallas kernels, middle(): pl.pallas_call(middle_kernel, name='middle', grid=(count // tile,), in_sp...  93.8 us
    pallas_call x1, Pallas kernels, attention_backward(): pl.pallas_call(backward_kernel, name='attention_backward', grid=(seqs,),...  75.3 us
    pallas_call x1, Pallas kernels, attention_forward(): pl.pallas_call(forward_kernel, name='attention_forward', grid=(seqs,), in...  44.6 us

profile of v2, /device:TPU:0, one launch (start us, length us, event | category | flops | bytes accessed | tf_op | source)
XLA Modules:
  0.0 457.4 jit_solution(13060267100543027593)
XLA Ops:
  0.7 0.8 copy.43
  1.4 0.7 copy.44
  2.2 0.7 copy.45
  2.9 0.7 copy.46
  3.7 0.7 copy.47
  4.4 0.7 copy.48
  5.2 0.7 copy.49
  5.9 0.7 copy.50
  6.7 0.7 reshape.87
  7.5 1.6 fusion.1.refs_0_
  9.1 33.5 %gather.2 = bf16[32,24,2560]{2,1,0:T(8,128)(2,1)} custom-call(bf16[24,2560]{1,0:T(8,128)(2,1)} %fusion.1.refs_0_), custom_call_target="tpu_custom_call" | custom-call | tf_op jit(solution)/shard_map/gather/pallas_call | solution.py:219
  42.6 1.0 convert_bitcast_fusion
  43.6 0.7 copy.51.vec_ref
  45.5 44.6 %attention_forward.1 = (bf16[2048,2304]{1,0:T(8,128)(2,1)}, bf16[2048,768]{1,0:T(8,128)(2,1)}, f32[4,16,512]{2,1,0:T(8,128)}) custom-call(bf16[2048,768]{1,0:T(8,128)(2,1)} %bitcast.43, bf16[768,2560]{1,0:T(8,128)(2,1)} %bitcast.24, f32[8,768]{1,0:T(8,128)} %copy.51.vec_ref, s32[4,1,512]{2,1,0:T(1,128)} %reshape.89.seg_ref, s32[4,1,512]{2,1,0:T(1,128)} %reshape.90.pad_ref), custom_call_target="tpu_custom_call" | custom-call | flops 12000000000 | bytes 20000000 | tf_op jit(solution)/shard_map/attention_forward/pallas_call | solution.py:510
  90.1 1.0 slice_convert_fusion
  91.1 0.9 reshape.106.bin_ref
  92.0 60.3 %gather.3 = (bf16[32,24,768]{2,1,0:T(8,128)(2,1)}, bf16[32,24,3072]{2,1,0:T(8,128)(2,1)}, bf16[32,96,768]{2,1,0:T(8,128)(2,1)}) custom-call(bf16[24,768]{1,0:T(8,128)(2,1)} %refs_0_.1, bf16[24,3072]{1,0:T(8,128)(2,1)} %refs_1_.1, bf16[96,768]{1,0:T(8,128)(2,1)} %refs_2_.1), custom_call_target="tpu_custom_call" | custom-call | tf_op jit(solution)/shard_map/gather/pallas_call | solution.py:219
  153.0 93.8 %middle.1 = (bf16[2048,768]{1,0:T(8,128)(2,1)}, f32[2048,768]{1,0:T(8,128)}, bf16[2048,768]{1,0:T(8,128)(2,1)}, bf16[768,768]{1,0:T(8,128)(2,1)}, bf16[768,3072]...) custom-call(f32[1]{0:T(128)S(6)} %copy.57.scale_ref, ...), custom_call_target="tpu_custom_call" | custom-call | flops 65000001536 | bytes 60000000 | tf_op jit(solution)/shard_map/middle/pallas_call | solution.py:620
  246.8 90.2 %scatter.3 = (f32[96,768]{1,0:T(8,128)}, f32[24,3072]{1,0:T(8,128)}, f32[24,768]{1,0:T(8,128)}) custom-call(bf16[16,192,768]{2,1,0:T(8,128)(2,1)} %bitcast.28, bf16[16,48,3072]{2,1,0:T(8,128)(2,1)} %bitcast.27, bf16[16,48,768]{2,1,0:T(8,128)(2,1)} %bitcast.30), custom_call_target="tpu_custom_call" | custom-call | tf_op jit(solution)/shard_map/scatter/pallas_call | solution.py:434
  339.4 75.3 %attention_backward.1 = (f32[2048,768]{1,0:T(8,128)}, bf16[768,2560]{1,0:T(8,128)(2,1)}) custom-call(f32[1]{0:T(128)S(6)} %copy.57.scale_ref, bf16[2048,768]{1,0:T(8,128)(2,1)} %bitcast.45, bf16[2048,2304]{1,0:T(8,128)(2,1)} %get-tuple-element.39.qkv_ref, bf16[2048,768]{1,0:T(8,128)(2,1)} %get-tuple-element.40.datt_ref, ...), custom_call_target="tpu_custom_call" | custom-call | flops 31000000512 | bytes 35000000 | tf_op jit(solution)/shard_map/attention_backward/pallas_call | solution.py:722
  414.7 35.7 %scatter.2 = f32[24,2560]{1,0:T(8,128)} custom-call(bf16[16,48,2560]{2,1,0:T(8,128)(2,1)} %bitcast.29), custom_call_target="tpu_custom_call" | custom-call | tf_op jit(solution)/shard_map/scatter/pallas_call | solution.py:434
  450.5 1.6 slice.46
  452.1 0.8 slice.52
  453.5 1.8 slice_reduce_fusion
  (28 shorter events, 6.4 us)
Async XLA Ops:
  0.6 43.7 %copy-start.5 = (s32[4,512]{1,0:T(4,128)S(1)}, s32[4,512]{1,0:T(4,128)}, u32[]{:S(2)}) copy-start(s32[4,512]{1,0:T(4,128)} %param.20) | copy-start | bytes 24580
  0.7 44.3 %copy-start.6 = (s32[4,512]{1,0:T(4,128)S(1)}, s32[4,512]{1,0:T(4,128)}, u32[]{:S(2)}) copy-start(s32[4,512]{1,0:T(4,128)} %param.21) | copy-start | bytes 24580
  246.8 90.2 %copy-start.3 = (f32[16,768]{1,0:T(8,128)S(1)}, f32[16,768]{1,0:T(8,128)}, u32[]{:S(2)}) copy-start(f32[16,768]{1,0:T(8,128)} %get-tuple-element.43) | copy-start | bytes 147460
  246.8 90.8 %copy-start.4 = (f32[1,3072]{1,0:T(1,128)S(1)}, f32[1,3072]{1,0:T(1,128)}, u32[]{:S(2)}) copy-start(f32[1,3072]{1,0:T(1,128)} %get-tuple-element.44) | copy-start | bytes 36868
  414.7 40.6 %copy-start.2 = (f32[24,768]{1,0:T(8,128)S(1)}, f32[24,768]{1,0:T(8,128)}, u32[]{:S(2)}) copy-start(f32[24,768]{1,0:T(8,128)} %get-tuple-element.81) | copy-start | bytes 221188
  414.7 41.3 %copy-start.1 = (f32[24,3072]{1,0:T(8,128)S(1)}, f32[24,3072]{1,0:T(8,128)}, u32[]{:S(2)}) copy-start(f32[24,3072]{1,0:T(8,128)} %get-tuple-element.85) | copy-start | bytes 884740
  414.7 42.0 %copy-start = (f32[96,768]{1,0:T(8,128)S(1)}, f32[96,768]{1,0:T(8,128)}, u32[]{:S(2)}) copy-start(f32[96,768]{1,0:T(8,128)} %get-tuple-element.87) | copy-start | bytes 884740

commit v3 on v2

--- a/solution.py
+++ b/solution.py
@@ -192,6 +192,17 @@
                 def _():
                     self.to_z(task, place.z + far, index + 2, False, False)
 
+    def timed(self):
+        z, b = self.along_z, self.from_b
+        return [
+            (0, self.begin), (1, self.spread), (4, self.from_a), (5, partial(z, 1, 0)), (6, partial(b, 0)),
+            (9, partial(z, 1, 1)), (9, partial(b, 1)), (10, partial(b, 2)), (10, partial(b, 8)),
+            (13, partial(z, 2, 0)), (13, partial(b, 3)), (13, partial(b, 9)), (17, partial(z, 2, 1)),
+            (17, partial(b, 4)), (17, partial(b, 10)), (20, partial(b, 5)), (20, partial(b, 11)),
+            (21, partial(z, 3, 0)), (23, partial(b, 6)), (23, partial(b, 12)), (24, partial(z, 3, 1)),
+            (24, partial(b, 7)), (24, partial(b, 13)), (24, self.finish),
+        ]
+
     def events(self):
         out = [self.begin, self.spread, self.from_a]
         out += [partial(self.along_z, 1, 0), partial(self.along_z, 1, 1), partial(self.from_b, 0), partial(self.from_b, 1)]
@@ -338,13 +349,20 @@
         self.add(self.tasks[2 + which] * 4 + self.level(m), self.got_z, into)
 
     def step_far(self, which, m):
+        self.step_far_out(which, m)
+        self.step_far_on(which, m)
+
+    def step_far_out(self, which, m):
+        @pl.when(self.inner == 0)
+        def _():
+            self.along_z(which, m, True).start()
+
+    def step_far_on(self, which, m):
         @pl.when(self.inner == 1)
         def _():
             self.add_z(which, m, m - 1)
-
-        @pl.when(self.inner < m)
-        def _():
-            self.along_z(which, m, True).start()
+            if m > 1:
+                self.along_z(which, m, True).start()
 
     def step_near(self, which, m):
         @pl.when(self.inner >= m)
@@ -399,6 +417,19 @@
 
     def add_b_far(self, which, m):
         self.add_b(which, self.level(m))
+
+    def timed(self):
+        pair, b, send, relay, near = self.add_pair, self.add_b_far, self.step_far_out, self.step_far_on, self.step_near
+        return [
+            (0, self.begin), (2, partial(pair, 0)), (3, partial(pair, 1)), (4, partial(pair, 2)), (4, partial(pair, 3)),
+            (5, partial(b, 0, 3)), (5, partial(send, 0, 3)), (6, partial(b, 0, 2)), (6, partial(send, 0, 2)),
+            (8, partial(b, 0, 1)), (8, partial(send, 0, 1)), (8, partial(relay, 0, 3)), (9, partial(b, 0, 0)),
+            (10, partial(b, 1, 3)), (10, partial(send, 1, 3)), (11, partial(relay, 0, 2)), (11, partial(b, 1, 2)),
+            (11, partial(send, 1, 2)), (12, partial(near, 0, 0)), (13, partial(b, 1, 1)), (13, partial(send, 1, 1)),
+            (14, partial(relay, 0, 1)), (14, partial(b, 1, 0)), (15, partial(near, 0, 1)), (16, partial(relay, 1, 3)),
+            (16, self.to_a), (19, partial(relay, 1, 2)), (20, partial(near, 1, 0)), (22, partial(relay, 1, 1)),
+            (23, partial(near, 1, 1)), (24, self.add_a), (24, self.finish),
+        ]
 
     def events(self):
         out = [self.begin] + [partial(self.add_pair, i) for i in range(4)]
@@ -452,6 +483,30 @@
     return lax.dot_general(left, right, (((1,), (1,)), ((), ())), preferred_element_type=F32)
 
 
+def at_slot(slot, plan):
+    def choose(slots):
+        if len(slots) == 1:
+
+            @pl.when(slot == slots[0])
+            def _():
+                for event in plan[slots[0]]:
+                    event()
+
+            return
+        middle_slot = slots[len(slots) // 2]
+
+        @pl.when(slot < middle_slot)
+        def _():
+            choose(slots[: len(slots) // 2])
+
+        @pl.when(slot >= middle_slot)
+        def _():
+            choose(slots[len(slots) // 2 :])
+
+    if plan:
+        choose(sorted(plan))
+
+
 def fill_mask(seg_ref, pad_ref, mask_ref):
     length = mask_ref.shape[0]
     seg_row = seg_ref[0].astype(F32)
@@ -466,8 +521,22 @@
         mask_ref[:, 128 * block : 128 * block + 128] = jnp.where(same & seen, 0.0, -1e30)
 
 
-def forward_kernel(x_ref, w_ref, vec_ref, seg_ref, pad_ref, qkv_ref, att_ref, lse_ref, mask_ref):
+def forward_kernel(count, x_ref, w_ref, vec_ref, seg_ref, pad_ref, *refs):
+    shards, refs = refs[:count], refs[count:]
+    qkv_ref, att_ref, lse_ref = refs[:3]
+    fulls, mask_ref, sems = refs[3 : 3 + count], refs[3 + count], refs[4 + count :]
+    step = pl.program_id(0)
     width = x_ref.shape[1]
+    plan = {}
+    if count:
+        place = Place()
+        pl.when(step == 0)(place.meet)
+        for slot, index, event in sorted(
+            [(slot, i, e) for i in range(count) for slot, e in Gather(place, shards[i], fulls[i], sems[4 * i : 4 * i + 4]).timed()],
+            key=lambda item: item[0],
+        ):
+            plan.setdefault(slot, []).append(event)
+        ending = plan.pop(24)
     fill_mask(seg_ref, pad_ref, mask_ref)
     for part, row in enumerate((BQ, None, BV)):
         cols = slice(part * width, (part + 1) * width)
@@ -479,6 +548,7 @@
     first_half = lax.broadcasted_iota(jnp.int32, (1, 2 * half), 1) < half
 
     def pair(index, carry):
+        at_slot(step * (HEADS // 2) + index, plan)
         base = pl.multiple_of(index * 2 * half, 2 * half)
         queries = qkv_ref[:, pl.ds(base, 2 * half)]
         keys = qkv_ref[:, pl.ds(width + base, 2 * half)]
@@ -499,29 +569,38 @@
         return carry
 
     lax.fori_loop(0, HEADS // 2, pair, 0)
-
-
-def attention_forward(rows, w_qkv, vectors, segments, pads):
+    if count:
+
+        @pl.when(step == pl.num_programs(0) - 1)
+        def _():
+            for event in ending:
+                event()
+
+
+def attention_forward(rows, w_qkv, vectors, segments, pads, shards):
     seqs, _, length = segments.shape
     width = rows.shape[1]
     whole = lambda shape: pl.BlockSpec(shape, lambda i: (0,) * len(shape), pipeline_mode=pl.Buffered(1))
     row = lambda cols: pl.BlockSpec((length, cols), lambda i: (i, 0))
     tokens = pl.BlockSpec((1, 1, length), lambda i: (i, 0, 0))
+    anywhere = [pl.BlockSpec(memory_space=pl.ANY)] * len(shards)
+    remote = dict(collective_id=1, has_side_effects=True) if shards else {}
     return pl.pallas_call(
-        forward_kernel,
+        partial(forward_kernel, len(shards)),
         name="attention_forward",
         grid=(seqs,),
-        in_specs=[row(width), whole((width, 3 * width)), whole(vectors.shape), tokens, tokens],
-        out_specs=[row(3 * width), row(width), pl.BlockSpec((1, 16, length), lambda i: (i, 0, 0))],
+        in_specs=[row(width), whole((width, 3 * width)), whole(vectors.shape), tokens, tokens] + anywhere,
+        out_specs=[row(3 * width), row(width), pl.BlockSpec((1, 16, length), lambda i: (i, 0, 0))] + anywhere,
         out_shape=[
             jax.ShapeDtypeStruct((rows.shape[0], 3 * width), BF16),
             jax.ShapeDtypeStruct((rows.shape[0], width), BF16),
             jax.ShapeDtypeStruct((seqs, 16, length), F32),
-        ],
-        scratch_shapes=[pltpu.VMEM((length, length), F32)],
-        compiler_params=pltpu.CompilerParams(vmem_limit_bytes=VMEM_BYTES),
+        ]
+        + [jax.ShapeDtypeStruct((32, *s.shape), s.dtype) for s in shards],
+        scratch_shapes=[pltpu.VMEM((length, length), F32)] + GATHER_SEMS * len(shards),
+        compiler_params=pltpu.CompilerParams(vmem_limit_bytes=VMEM_BYTES, **remote),
         cost_estimate=pl.CostEstimate(flops=12_000_000_000, bytes_accessed=20_000_000, transcendentals=12_000_000),
-    )(rows, w_qkv, vectors, segments, pads)
+    )(rows, w_qkv, vectors, segments, pads, *shards)
 
 
 def norm_parts(arr):
@@ -648,10 +727,28 @@
 
 
 def backward_kernel(
-    scale_ref, x_ref, qkv_ref, datt_ref, lse_ref, seg_ref, pad_ref, sum_ref, w_ref, rest_ref,
-    gx_ref, gw_ref, acc_ref, gvec_ref, dqkv_ref, mask_ref,
+    count, scale_ref, x_ref, qkv_ref, datt_ref, lse_ref, seg_ref, pad_ref, sum_ref, w_ref, rest_ref, *refs
 ):
+    terms, refs = refs[:count], refs[count:]
+    gx_ref, gw_ref = refs[:2]
+    sums, refs = refs[2 : 2 + count], refs[2 + count :]
+    acc_ref, gvec_ref, dqkv_ref, mask_ref = refs[:4]
     step = pl.program_id(0)
+    plan = {}
+    if count:
+        place = Place()
+        pl.when(step == 0)(place.meet)
+        each = (len(refs) - 4) // count
+        for slot, index, event in sorted(
+            [
+                (slot, i, e)
+                for i in range(count)
+                for slot, e in Scatter(place, terms[i], sums[i], refs[4 + each * i : 4 + each * (i + 1)]).timed()
+            ],
+            key=lambda item: item[0],
+        ):
+            plan.setdefault(slot, []).append(event)
+        ending = plan.pop(24)
     width = x_ref.shape[1]
     half = width // HEADS
     fill_mask(seg_ref, pad_ref, mask_ref)
@@ -663,6 +760,7 @@
         gvec_ref[...] = jnp.zeros_like(gvec_ref)
 
     def pair(index, carry):
+        at_slot(step * (HEADS // 2) + index, plan)
         base = pl.multiple_of(index * 2 * half, 2 * half)
         queries = qkv_ref[:, pl.ds(base, 2 * half)]
         keys = qkv_ref[:, pl.ds(width + base, 2 * half)]
@@ -710,17 +808,24 @@
         gvec_ref[2:VECTORS] = rest_ref[2:VECTORS]
         gw_ref[:, 3 * width : 3 * width + 128] = jnp.transpose(gvec_ref[...]).astype(BF16)
         gw_ref[:, 3 * width + 128 :] = jnp.zeros((width, gw_ref.shape[1] - 3 * width - 128), BF16)
-
-
-def attention_backward(scale, rows, qkv, datt, lse, segments, pads, grad_sum, w_qkv, rest):
+        if count:
+            for event in ending:
+                event()
+
+
+def attention_backward(scale, rows, qkv, datt, lse, segments, pads, grad_sum, w_qkv, rest, terms):
     seqs, _, length = segments.shape
     count, width = rows.shape
     whole = lambda shape: pl.BlockSpec(shape, lambda i: (0,) * len(shape), pipeline_mode=pl.Buffered(1))
     row = lambda cols: pl.BlockSpec((length, cols), lambda i: (i, 0))
     tokens = pl.BlockSpec((1, 1, length), lambda i: (i, 0, 0))
     shape = jax.ShapeDtypeStruct
+    anywhere = [pl.BlockSpec(memory_space=pl.ANY)] * len(terms)
+    remote = dict(collective_id=3, has_side_effects=True) if terms else {}
+    sums = [(t.shape[1] // 2, t.shape[2]) for t in terms]
+    buffers = [b for t in terms for b in scatter_buffers(*t.shape[1:])]
     return pl.pallas_call(
-        backward_kernel,
+        partial(backward_kernel, len(terms)),
         name="attention_backward",
         grid=(seqs,),
         in_specs=[
@@ -734,18 +839,20 @@
             row(width),
             whole((width, 3 * width)),
             whole(rest.shape),
-        ],
-        out_specs=[row(width), whole(w_qkv.shape)],
-        out_shape=[shape((count, width), F32), shape(w_qkv.shape, BF16)],
+        ]
+        + anywhere,
+        out_specs=[row(width), whole(w_qkv.shape)] + [whole(s) for s in sums],
+        out_shape=[shape((count, width), F32), shape(w_qkv.shape, BF16)] + [shape(s, F32) for s in sums],
         scratch_shapes=[
             pltpu.VMEM((width, 3 * width), F32),
             pltpu.VMEM((128, width), F32),
             pltpu.VMEM((length, 3 * width), BF16),
             pltpu.VMEM((length, length), F32),
-        ],
-        compiler_params=pltpu.CompilerParams(vmem_limit_bytes=VMEM_BYTES),
+        ]
+        + buffers,
+        compiler_params=pltpu.CompilerParams(vmem_limit_bytes=VMEM_BYTES, **remote),
         cost_estimate=pl.CostEstimate(flops=31_000_000_000, bytes_accessed=35_000_000, transcendentals=12_000_000),
-    )(scale, rows, qkv, datt, lse, segments, pads, grad_sum, w_qkv, rest)
+    )(scale, rows, qkv, datt, lse, segments, pads, grad_sum, w_qkv, rest, *terms)
 
 
 def body(
@@ -759,34 +866,34 @@
     packed = jnp.concatenate([packed, b_in.reshape(mine, -1)], 1)
     packed = jnp.pad(packed, ((0, 0), (0, 256 - packed.shape[1])))
     shards = [jnp.concatenate([w_qkv, packed], 1), w_out, w_in, w_down]
+    flat = lambda arr: arr.reshape(-1, arr.shape[-1])
     if near:
-        full = gather_all(shards[:1], 0) + gather_all(shards[1:], 1)
-        full = [f.reshape(-1, f.shape[-1]) for f in full]
+        early, later = flat(gather_all(shards[:1], 0)[0]), []
     else:
-        full = [lax.all_gather(s, AXES, axis=0, tiled=True) for s in shards]
-    early, wo_full, win_full, wd_full = full
+        early, *later = [lax.all_gather(s, AXES, axis=0, tiled=True) for s in shards]
     vectors = jnp.transpose(early[:, 3 * width : 3 * width + 8].astype(F32))
     bin_full = early[:, 3 * width + BIN : 3 * width + VECTORS].astype(F32).reshape(1, -1)
     rows = hidden_in.reshape(-1, width)
     segments = segment_ids.reshape(seqs, 1, length)
     pads = pad_mask.reshape(seqs, 1, length)
-    qkv, att, lse = attention_forward(rows, early, vectors, segments, pads)
+    qkv, att, lse, *gathered = attention_forward(rows, early, vectors, segments, pads, shards[1:] if near else [])
+    wo_full, win_full, wd_full = later or map(flat, gathered)
     hidden_out, grad_sum, datt, g_wo, g_win, g_wd, g_vec, g_bin = middle(
         task_weight, rows, att, out_grad.reshape(-1, width), wo_full, win_full, wd_full, vectors, bin_full
     )
     g_rest = jnp.concatenate([g_vec[:8], jnp.transpose(g_bin.reshape(width, -1)), g_vec[8:12]], 0)
-    grad_x, g_qkv = attention_backward(
-        task_weight, rows, qkv, datt, lse, segments, pads, grad_sum, early, g_rest
+    blocks = lambda arr: arr.reshape(16, -1, arr.shape[1])
+    rest = (g_wd, g_win, g_wo)
+    grad_x, g_qkv, *sums = attention_backward(
+        task_weight, rows, qkv, datt, lse, segments, pads, grad_sum, early, g_rest, list(map(blocks, rest)) if near else []
     )
-    terms = [g_qkv, g_wd, g_win, g_wo]
     if near:
-        late, s_wd, s_win, s_wo = scatter_all([t.reshape(16, -1, t.shape[1]) for t in terms[:1]], 2) + scatter_all(
-            [t.reshape(16, -1, t.shape[1]) for t in terms[1:]], 3
-        )
+        (late,) = scatter_all([blocks(g_qkv)], 2)
     else:
-        late, s_wd, s_win, s_wo = [
-            lax.psum_scatter(t, AXES, scatter_dimension=0, tiled=True).astype(F32) for t in terms
+        late, *sums = [
+            lax.psum_scatter(t, AXES, scatter_dimension=0, tiled=True).astype(F32) for t in (g_qkv, *rest)
         ]
+    s_wd, s_win, s_wo = sums
     vector = lambda row: late[:, 3 * width + row]
     return (
         hidden_out.reshape(hidden_in.shape),

time: 458 us -> 379 us (0.83)
  Pallas kernels: 433 us -> 346 us
  local copies, waits for them, and re-layouts: 17.6 us -> 25.2 us
    pallas_call x2 -> x1, Pallas kernels: 126 us -> 35.1 us  [scatter_all(): pl.pallas_call(partial(scatter_kernel, count), name='scatter', in_specs=[...]
    pallas_call x2, Pallas kernels: 120 us -> 184 us  [the longest x1 103 us: attention_backward(): pl.pallas_call(partial(backward_kernel, len(terms)), name='attention_back...]
    pallas_call x2 -> x1, Pallas kernels: 93.9 us -> 33.5 us  [gather_all(): pl.pallas_call(partial(gather_kernel, count), name='gather', in_specs=[pl...]
    unnamed x17 -> x14, local copies, waits for them, and re-layouts: 2.09 us -> 8.23 us
where the time goes in v3:
time: 379 us; the launch traced here: 378 us
  Pallas kernels  346 us (91%)
  local copies, waits for them, and re-layouts  25.2 us (7%)
  other arithmetic  5.58 us (1%)
    pallas_call x1, Pallas kernels, attention_backward(): pl.pallas_call(partial(backward_kernel, len(terms)), name='attention_back...  103 us
    pallas_call x1, Pallas kernels, middle(): pl.pallas_call(middle_kernel, name='middle', grid=(count // tile,), in_sp...  93.8 us
    pallas_call x1, Pallas kernels, attention_forward(): pl.pallas_call(partial(forward_kernel, len(shards)), name='attention_forw...  80.8 us
    pallas_call x1, Pallas kernels, scatter_all(): pl.pallas_call(partial(scatter_kernel, count), name='scatter', in_specs=[...  35.1 us
    pallas_call x1, Pallas kernels, gather_all(): pl.pallas_call(partial(gather_kernel, count), name='gather', in_specs=[pl...  33.5 us
    unnamed x14, local copies, waits for them, and re-layouts  8.23 us

profile of v3, /device:TPU:0, one launch (start us, length us, event | category | flops | bytes accessed | tf_op | source)
XLA Modules:
  0.0 378.3 jit_solution(14288219231001570731)
XLA Ops:
  0.7 0.8 copy.43
  1.4 0.7 copy.44
  2.2 0.7 copy.45
  2.9 0.7 copy.46
  3.7 0.7 copy.47
  4.4 0.7 copy.48
  5.2 0.7 copy.49
  5.9 0.7 copy.50
  6.7 0.7 reshape.87
  7.5 1.6 fusion.1.refs_0_
  9.1 33.5 %gather.1 = bf16[32,24,2560]{2,1,0:T(8,128)(2,1)} custom-call(bf16[24,2560]{1,0:T(8,128)(2,1)} %fusion.1.refs_0_), custom_call_target="tpu_custom_call" | custom-call | tf_op jit(solution)/shard_map/gather/pallas_call | solution.py:230
  42.6 1.0 convert_bitcast_fusion
  43.6 0.7 copy.51.vec_ref
  45.5 80.8 %attention_forward.1 = (bf16[2048,2304]{1,0:T(8,128)(2,1)}, bf16[2048,768]{1,0:T(8,128)(2,1)}, f32[4,16,512]{2,1,0:T(8,128)}, bf16[32,24,768]{2,1,0:T(8,128)(2,1...) custom-call(bf16[2048,768]{1,0:T(8,128)(2,1)} %bitcast.39, bf16[768,2560]{1,0:T(8,128)(2,1)} %bitcast.25, ...), custom_call_target="tpu_custom_call" | custom-call | flops 12000000000 | bytes 20000000 | tf_op jit(solution)/shard_map/attention_forward/pallas_call | solution.py:588
  126.4 1.0 slice_convert_fusion
  127.4 0.9 reshape.106.bin_ref
  128.9 93.8 %middle.1 = (bf16[2048,768]{1,0:T(8,128)(2,1)}, f32[2048,768]{1,0:T(8,128)}, bf16[2048,768]{1,0:T(8,128)(2,1)}, bf16[768,768]{1,0:T(8,128)(2,1)}, bf16[768,3072]...) custom-call(f32[1]{0:T(128)S(6)} %copy.58.scale_ref, ...), custom_call_target="tpu_custom_call" | custom-call | flops 65000001536 | bytes 60000000 | tf_op jit(solution)/shard_map/middle/pallas_call | solution.py:699
  224.8 1.4 reduce.19
  227.3 102.7 %attention_backward.1 = (f32[2048,768]{1,0:T(8,128)}, bf16[768,2560]{1,0:T(8,128)(2,1)}, f32[96,768]{1,0:T(8,128)}, f32[24,3072]{1,0:T(8,128)}, f32[24,768]{1,0:T(8,128)}) custom-call(f32[1]{0:T(128)S(6)} %copy.58.scale_ref, bf16[2048,768]{1,0:T(8,128)(2,1)} %bitcast.41, bf16[2048,2304]{1,0:T(8,128)(2,1)} %get-tuple-element.39.qkv_ref, ...), custom_call_target="tpu_custom_call" | custom-call | flops 31000000512 | bytes 35000000 | tf_op jit(solution)/shard_map/attention_backward/pallas_call | solution.py:827
  330.1 35.1 %scatter.1 = f32[24,2560]{1,0:T(8,128)} custom-call(bf16[16,48,2560]{2,1,0:T(8,128)(2,1)} %bitcast.28), custom_call_target="tpu_custom_call" | custom-call | tf_op jit(solution)/shard_map/scatter/pallas_call | solution.py:465
  365.2 1.6 slice.46
  366.8 0.8 slice.52
  368.2 1.8 slice_reduce_fusion
  370.0 6.2 %copy.59 = f32[4,512,768]{2,1,0:T(8,128)} copy(f32[4,512,768]{2,1,0:T(8,128)} %bitcast.23) | data formatting | bytes 12582912
  (23 shorter events, 7.2 us)
Async XLA Ops:
  0.6 43.7 %copy-start.3 = (s32[4,512]{1,0:T(4,128)S(1)}, s32[4,512]{1,0:T(4,128)}, u32[]{:S(2)}) copy-start(s32[4,512]{1,0:T(4,128)} %param.20) | copy-start | bytes 24580
  0.7 44.3 %copy-start.4 = (s32[4,512]{1,0:T(4,128)S(1)}, s32[4,512]{1,0:T(4,128)}, u32[]{:S(2)}) copy-start(s32[4,512]{1,0:T(4,128)} %param.21) | copy-start | bytes 24580
  370.0 6.2 %copy-start.2 = (f32[24,768]{1,0:T(8,128)S(1)}, f32[24,768]{1,0:T(8,128)}, u32[]{:S(2)}) copy-start(f32[24,768]{1,0:T(8,128)} %get-tuple-element.81) | copy-start | bytes 221188
  370.0 6.8 %copy-start.1 = (f32[24,3072]{1,0:T(8,128)S(1)}, f32[24,3072]{1,0:T(8,128)}, u32[]{:S(2)}) copy-start(f32[24,3072]{1,0:T(8,128)} %get-tuple-element.85) | copy-start | bytes 884740
  370.0 7.5 %copy-start = (f32[96,768]{1,0:T(8,128)S(1)}, f32[96,768]{1,0:T(8,128)}, u32[]{:S(2)}) copy-start(f32[96,768]{1,0:T(8,128)} %get-tuple-element.87) | copy-start | bytes 884740

commit v4 on v1

v4 whole, which is shorter than its diff:
```python
from functools import partial

import jax
import jax.numpy as jnp
from jax import lax
from jax.experimental import pallas as pl
from jax.experimental.pallas import tpu as pltpu
from jax.sharding import PartitionSpec as P

HEADS = 12
GROUPS = 3
AXES = ("task", "batch")
F32 = jnp.float32
BF16 = jnp.bfloat16
VMEM_BYTES = 66_900_000
BQ, BV, BO, G1, S1, BD, G2, S2, BIN = range(9)
VECTORS = 12

GATHER_TABLE = [
    (0, 0, 0), (0, 1, 0), (0, 0, 1), (0, 1, 1), (0, 0, 2), (0, 0, 3), (0, 0, 4), (0, 0, 5), (0, 1, 2), (0, 1, 3),
    (0, 1, 4), (0, 1, 5), (0, 0, 6), (0, 0, 7), (0, 0, 8), (0, 0, 9), (0, 0, 10), (0, 0, 11), (0, 2, 0), (0, 0, 14),
    (0, 0, 12), (0, 0, 13), (0, 1, 6), (0, 1, 7), (0, 1, 8), (0, 1, 10), (0, 2, 1), (0, 3, 0), (0, 0, 15), (0, 0, 16),
    (0, 0, 17), (0, 0, 18), (0, 0, 21), (0, 0, 22), (0, 1, 9), (0, 1, 11), (0, 1, 14), (0, 0, 19), (0, 0, 20),
    (0, 0, 23), (0, 0, 24), (0, 3, 1), (0, 4, 0), (0, 5, 0), (0, 6, 0), (0, 1, 12), (0, 1, 13), (0, 1, 15),
    (0, 1, 16), (0, 1, 17), (0, 1, 18), (0, 1, 21), (0, 0, 26), (0, 2, 2), (0, 2, 3), (0, 4, 1), (0, 5, 1),
    (0, 0, 25), (0, 2, 4), (0, 2, 5), (0, 6, 1), (0, 0, 27), (0, 0, 28), (0, 1, 22), (0, 0, 29), (0, 3, 2), (0, 3, 3),
    (0, 3, 4), (0, 3, 5), (0, 1, 23), (0, 1, 24), (0, 1, 19), (0, 1, 20), (0, 1, 25), (0, 1, 26), (0, 2, 6),
    (0, 2, 7), (0, 1, 27), (0, 1, 28), (0, 2, 8), (0, 2, 9), (0, 2, 10), (0, 2, 11), (0, 2, 12), (0, 2, 13),
    (0, 2, 14), (0, 3, 6), (0, 3, 7), (0, 3, 8), (0, 3, 10), (0, 3, 11), (0, 4, 2), (0, 4, 3), (0, 4, 4), (0, 4, 5),
    (0, 5, 2), (0, 5, 3), (0, 5, 4), (0, 5, 5), (0, 6, 2), (0, 6, 3), (0, 6, 4), (0, 6, 5), (0, 1, 29), (0, 3, 9),
    (0, 3, 14), (1, 2, 15), (1, 2, 16), (1, 2, 17), (1, 2, 18), (1, 2, 21), (1, 2, 22), (1, 3, 12), (1, 3, 13),
    (2, 2, 19), (2, 2, 20), (2, 2, 23), (2, 2, 24), (2, 3, 15), (2, 3, 16), (2, 3, 17), (2, 3, 18), (2, 4, 7),
    (2, 4, 8), (3, 3, 21), (3, 4, 6), (3, 4, 9), (3, 4, 10), (3, 4, 11), (3, 4, 12), (4, 5, 6), (5, 5, 7), (5, 5, 8),
    (6, 5, 9), (7, 5, 10), (7, 5, 11), (7, 5, 12), (8, 6, 6), (9, 2, 27), (9, 2, 28), (9, 3, 19), (9, 3, 20),
    (9, 3, 23), (9, 3, 24), (9, 6, 9), (10, 6, 7), (10, 6, 8), (10, 6, 10), (11, 2, 25), (11, 2, 26), (11, 3, 22),
    (11, 3, 25), (11, 3, 26), (11, 4, 13), (12, 2, 29), (12, 4, 14), (12, 4, 17), (12, 4, 18), (12, 6, 11),
    (12, 6, 12), (13, 3, 27), (13, 3, 28), (13, 4, 15), (13, 4, 16), (13, 4, 19), (13, 4, 20), (13, 5, 13),
    (14, 3, 29), (14, 5, 14), (16, 4, 25), (16, 4, 26), (16, 5, 15), (16, 5, 16), (16, 5, 17), (16, 5, 18),
    (17, 6, 13), (18, 5, 19), (18, 5, 20), (18, 6, 14), (19, 4, 21), (19, 4, 22), (19, 6, 17), (19, 6, 18),
    (20, 6, 15), (20, 6, 16), (21, 5, 21), (21, 5, 22), (21, 5, 25), (21, 5, 26), (23, 4, 23), (23, 4, 24),
    (23, 6, 19), (23, 6, 20), (23, 6, 21), (23, 6, 22), (25, 4, 27), (25, 4, 28), (26, 4, 29), (26, 5, 23),
    (26, 5, 24), (26, 6, 25), (26, 6, 26), (28, 6, 23), (28, 6, 24), (29, 5, 27), (29, 5, 28), (30, 5, 29),
    (31, 6, 27), (31, 6, 28), (32, 6, 29),
]
SCATTER_TABLE = [
    (0, 0, 0), (0, 1, 0), (0, 2, 0), (1, 0, 1), (2, 0, 2), (2, 0, 3), (3, 0, 4), (3, 0, 5), (3, 0, 6), (3, 0, 7),
    (3, 0, 8), (3, 1, 1), (4, 0, 9), (4, 0, 10), (4, 1, 2), (4, 1, 3), (5, 0, 11), (5, 0, 12), (5, 0, 15), (5, 0, 16),
    (5, 1, 4), (5, 2, 1), (5, 2, 2), (5, 2, 3), (5, 2, 4), (6, 0, 17), (6, 0, 18), (7, 0, 13), (7, 0, 19), (7, 0, 20),
    (7, 0, 21), (7, 0, 25), (8, 3, 0), (8, 0, 14), (8, 0, 22), (8, 0, 26), (8, 0, 27), (8, 0, 28), (8, 1, 5),
    (8, 1, 6), (8, 1, 7), (8, 1, 8), (8, 1, 9), (8, 1, 10), (9, 3, 1), (9, 3, 2), (9, 3, 3), (9, 3, 4), (9, 0, 23),
    (9, 1, 11), (9, 1, 15), (9, 1, 16), (10, 0, 29), (10, 1, 17), (10, 1, 18), (11, 0, 24), (11, 1, 19), (11, 1, 20),
    (11, 1, 21), (11, 2, 5), (11, 2, 6), (12, 0, 30), (12, 0, 31), (12, 1, 12), (12, 2, 7), (12, 2, 8), (12, 2, 9),
    (12, 2, 10), (12, 2, 11), (12, 2, 15), (12, 2, 16), (12, 2, 17), (12, 2, 18), (12, 2, 19), (12, 2, 20),
    (13, 3, 5), (13, 3, 6), (13, 0, 32), (13, 1, 13), (13, 2, 21), (14, 3, 7), (14, 3, 8), (14, 3, 9), (14, 3, 10),
    (14, 3, 11), (14, 3, 15), (14, 3, 16), (14, 3, 17), (14, 3, 18), (14, 3, 19), (14, 3, 20), (14, 0, 33),
    (14, 1, 25), (15, 3, 21), (15, 1, 14), (16, 4, 0), (16, 1, 22), (16, 1, 23), (16, 1, 26), (16, 1, 27),
    (16, 1, 28), (17, 4, 1), (17, 4, 2), (17, 4, 3), (17, 4, 4), (17, 1, 24), (17, 2, 12), (18, 4, 5), (18, 4, 6),
    (18, 4, 7), (18, 4, 8), (18, 1, 29), (18, 2, 13), (18, 2, 14), (18, 2, 22), (19, 3, 12), (19, 4, 9), (19, 4, 10),
    (19, 4, 11), (19, 4, 15), (19, 4, 16), (19, 4, 17), (19, 4, 18), (19, 4, 19), (19, 4, 20), (19, 4, 21),
    (19, 2, 23), (19, 2, 24), (20, 3, 13), (20, 3, 14), (20, 3, 22), (20, 1, 30), (20, 1, 31), (20, 1, 32),
    (20, 2, 25), (20, 2, 26), (21, 3, 23), (21, 3, 24), (21, 3, 25), (21, 4, 12), (21, 1, 33), (21, 2, 27),
    (21, 2, 28), (21, 2, 29), (21, 2, 30), (22, 3, 26), (22, 3, 27), (22, 3, 28), (22, 3, 29), (22, 3, 30),
    (22, 4, 13), (22, 4, 14), (22, 4, 22), (23, 3, 31), (23, 3, 32), (23, 4, 23), (23, 4, 24), (23, 4, 25),
    (23, 4, 26), (23, 2, 31), (23, 2, 32), (24, 3, 33), (24, 4, 27), (24, 4, 28), (24, 4, 29), (24, 4, 30),
    (24, 5, 0), (24, 6, 0), (24, 2, 33), (25, 4, 31), (25, 4, 32), (25, 5, 1), (25, 5, 2), (25, 5, 3), (25, 5, 4),
    (25, 6, 1), (25, 6, 2), (25, 6, 3), (25, 6, 4), (27, 4, 33), (27, 5, 5), (27, 5, 6), (27, 5, 7), (27, 5, 8),
    (29, 5, 9), (29, 5, 10), (29, 5, 11), (29, 5, 12), (29, 5, 15), (29, 5, 16), (29, 5, 17), (29, 5, 18),
    (29, 5, 19), (29, 5, 20), (29, 5, 21), (29, 6, 5), (29, 6, 6), (29, 6, 7), (29, 6, 8), (29, 6, 9), (29, 6, 10),
    (29, 6, 11), (31, 5, 13), (31, 5, 14), (31, 5, 25), (31, 6, 15), (31, 6, 16), (31, 6, 17), (31, 6, 18),
    (31, 6, 19), (31, 6, 20), (31, 6, 21), (32, 5, 22), (32, 5, 23), (32, 5, 24), (32, 5, 26), (32, 5, 27),
    (32, 5, 28), (32, 6, 12), (32, 6, 13), (32, 6, 14), (32, 5, 29), (32, 6, 22), (32, 6, 23), (32, 6, 24),
    (32, 5, 30), (32, 6, 25), (32, 6, 26), (32, 6, 29), (32, 6, 30), (32, 5, 31), (32, 5, 32), (32, 6, 27),
    (32, 6, 28), (32, 5, 33), (32, 6, 31), (32, 6, 32), (32, 6, 33),
]
GATHER_LINE_FIRST = [True, True, True, True, False, False, False]
SCATTER_LINE_LAST = [False, False, False, False, False, False, False]


MESH = pl.DeviceIdType.MESH


class Place:
    def __init__(self):
        self.task = lax.axis_index("task")
        self.batch = lax.axis_index("batch")
        self.core = self.batch % 2
        self.z = self.batch // 2
        x, y = self.task % 2, self.task // 2
        flip_x, flip_y = self.task + 1 - 2 * x, self.task + 2 - 4 * y
        self.task_a = (1 - self.core) * flip_x + self.core * flip_y
        self.task_b = (1 - self.core) * flip_y + self.core * flip_x
        self.task_ab = 3 - self.task
        self.partner = (self.task, self.batch + 1 - 2 * self.core)
        self.peer_a = (self.task_a, self.batch)
        self.peer_b = (self.task_b, self.batch)
        self.above = (self.task, self.batch + 2)
        self.below = (self.task, self.batch - 2)
        self.low = 1 - self.z // 2
        self.inner = self.low * self.z + (1 - self.low) * (3 - self.z)
        self.far = (self.task, self.batch + 4 * self.low - 2)
        self.near = (self.task, self.batch + 2 - 4 * self.low)

    def meet(self):
        barrier = pltpu.get_barrier_semaphore()
        for peer in (self.partner, self.peer_a, self.peer_b):
            pl.semaphore_signal(barrier, inc=1, device_id=peer, device_id_type=MESH)

        @pl.when(self.z < 3)
        def _():
            pl.semaphore_signal(barrier, inc=1, device_id=self.above, device_id_type=MESH)

        @pl.when(self.z > 0)
        def _():
            pl.semaphore_signal(barrier, inc=1, device_id=self.below, device_id_type=MESH)

        pl.semaphore_wait(barrier, 4 + self.z * (3 - self.z) // 2)


def remote(src, dst, send, recv, peer):
    return pltpu.make_async_remote_copy(src, dst, send, recv, device_id=peer, device_id_type=MESH)


GATHER_SEMS = [
    pltpu.SemaphoreType.DMA((12,)),
    pltpu.SemaphoreType.DMA((7,)),
    pltpu.SemaphoreType.DMA((14,)),
    pltpu.SemaphoreType.DMA((14,)),
    pltpu.SemaphoreType.DMA((6,)),
]


class Gather:
    def __init__(self, place, windows, full, sems, line_first=False):
        self.place, self.windows, self.full, self.line_first = place, windows, full, line_first
        self.send_z, self.send_a, self.recv, self.recv_b, self.misc = sems
        self.half = full.shape[1] // 2
        self.r = full.shape[0] // 32

    def rows(self, task, batch, count):
        return pl.ds(pl.multiple_of((task * 8 + batch) * self.r, 8), count * self.r)

    def cols(self, core):
        return pl.ds(pl.multiple_of(core * self.half, 128), self.half)

    def task(self, which):
        return self.place.task if which == 0 else self.place.task_a

    def level(self, spot):
        return self.place.z - spot if spot < 4 else self.place.z + spot - 3

    def here(self, spot):
        return self.place.z >= spot if spot < 4 else self.place.z + spot <= 6

    def chunk(self, task, spot):
        return self.full.at[self.rows(task, 2 * self.level(spot), 2), self.cols(self.place.core)]

    def begin(self):
        place, at = self.place, 0
        for window in self.windows:
            into = self.full.at[self.rows(place.task, place.batch, 1), pl.ds(at, window.shape[1])]
            pltpu.make_async_copy(window, into, self.misc.at[0]).start()
            remote(window, into, self.misc.at[1], self.misc.at[2], place.partner).start()
            at += window.shape[1]

    def along_z(self, which, spot, up):
        step = spot if up else max(spot - 3, 0)
        slot = which * 6 + step + (0 if up else 3)
        chunk = self.chunk(self.task(which), spot)
        into = which * 7 + step + (1 if up else 4)
        return remote(chunk, chunk, self.send_z.at[slot], self.recv.at[into], self.place.above if up else self.place.below)

    def along_a(self, spot):
        chunk = self.chunk(self.place.task, spot)
        return remote(chunk, chunk, self.send_a.at[spot], self.recv.at[7 + spot], self.place.peer_a)

    def along_b(self, which, spot):
        chunk = self.chunk(self.task(which), spot)
        return remote(chunk, chunk, self.misc.at[3], self.recv_b.at[which * 7 + spot], self.place.peer_b)

    def hand_over(self, task, spot):
        chunk = self.chunk(task, spot)
        remote(chunk, chunk, self.misc.at[4], self.misc.at[5], self.place.partner).start()

    def arrived(self, task, spot, sem):
        chunk = self.chunk(task, spot)
        remote(chunk, chunk, self.misc.at[1], sem, self.place.partner).wait_recv()

    def onward(self, which, spot):
        place = self.place
        if which == 0 or not self.line_first:
            for up in (True, False):
                if spot == 0 or (spot < 3 if up else 3 < spot < 6):
                    more = place.z < 3 if up else place.z > 0

                    @pl.when(more)
                    def _():
                        self.along_z(which, spot, up).start()

        if which == 0 and (spot == 0 or self.line_first):
            self.along_a(spot).start()
        self.along_b(which, spot).start()
        if which or spot:
            self.hand_over(self.task(which), spot)

    def spread(self):
        place = self.place
        mine = self.full.at[self.rows(place.task, place.batch, 1), :]
        pltpu.make_async_copy(mine, mine, self.misc.at[0]).wait()
        other = self.full.at[self.rows(place.task, place.partner[1], 1), :]
        remote(other, other, self.misc.at[1], self.misc.at[2], place.partner).wait_recv()
        self.onward(0, 0)

    def line(self, which, spot):
        @pl.when(self.here(spot))
        def _():
            self.arrived(self.task(which), spot, self.recv.at[which * 7 + spot])
            self.onward(which, spot)

    def from_b(self, which, spot):
        task = self.place.task_b if which == 0 else self.place.task_ab

        @pl.when(self.here(spot))
        def _():
            self.arrived(task, spot, self.recv_b.at[which * 7 + spot])
            self.hand_over(task, spot)

    def finish(self):
        place, full, r = self.place, self.full, self.r
        rest = full.at[pl.ds(0, 30 * r), self.cols(1 - place.core)]
        remote(rest, rest, self.misc.at[4], self.misc.at[5], place.partner).wait_recv()
        mine = full.at[pl.ds(0, 30 * r), self.cols(place.core)]
        remote(mine, mine, self.misc.at[4], self.misc.at[5], place.partner).wait_send()
        eight = full.at[pl.ds(0, 16 * r), self.cols(place.core)]
        remote(eight, eight, self.misc.at[3], self.recv_b.at[0], place.peer_b).wait_send()
        own = full.at[self.rows(place.task, place.batch, 1), :]
        remote(own, own, self.misc.at[1], self.misc.at[2], place.partner).wait_send()
        for spot in range(7 if self.line_first else 1):

            @pl.when(self.here(spot))
            def _():
                self.along_a(spot).wait_send()

        for which in range(1 if self.line_first else 2):
            for spot in (0, 1, 2):

                @pl.when(self.here(spot) & (place.z < 3))
                def _():
                    self.along_z(which, spot, True).wait_send()

            for spot in (0, 4, 5):

                @pl.when(self.here(spot) & (place.z > 0))
                def _():
                    self.along_z(which, spot, False).wait_send()

    def events(self):
        line, b = self.line, self.from_b
        out = [self.begin, self.spread]
        if self.line_first:
            out += [partial(line, 0, 1), partial(line, 0, 4), partial(line, 1, 0), partial(b, 0, 0)]
            out += [partial(line, 0, 2), partial(line, 0, 5), partial(line, 1, 1), partial(line, 1, 4)]
            out += [partial(b, 0, 1), partial(b, 0, 4), partial(line, 0, 3), partial(line, 0, 6), partial(b, 1, 0)]
            out += [partial(line, 1, 2), partial(line, 1, 5), partial(b, 0, 2), partial(b, 0, 5)]
            out += [partial(line, 1, 3), partial(line, 1, 6), partial(b, 1, 1), partial(b, 1, 4)]
            out += [partial(b, w, s) for w, s in ((0, 3), (0, 6), (1, 2), (1, 5), (1, 3), (1, 6))]
        else:
            out += [partial(line, 1, 0), partial(line, 0, 1), partial(line, 0, 4), partial(b, 0, 0), partial(b, 1, 0)]
            out += [partial(line, 1, 1), partial(line, 1, 4), partial(b, 0, 1), partial(b, 0, 4)]
            out += [partial(line, 0, 2), partial(line, 0, 5), partial(b, 1, 1), partial(b, 1, 4)]
            out += [partial(line, 1, 2), partial(line, 1, 5), partial(b, 0, 2), partial(b, 0, 5)]
            out += [partial(line, 0, 3), partial(line, 0, 6), partial(b, 1, 2), partial(b, 1, 5)]
            out += [partial(line, 1, 3), partial(line, 1, 6), partial(b, 0, 3), partial(b, 0, 6)]
            out += [partial(b, 1, 3), partial(b, 1, 6)]
        return out + [self.finish]


SCATTER_SEMS = [
    pltpu.SemaphoreType.DMA((4,)),
    pltpu.SemaphoreType.DMA((4,)),
    pltpu.SemaphoreType.DMA((4,)),
    pltpu.SemaphoreType.DMA((8,)),
    pltpu.SemaphoreType.DMA((8,)),
    pltpu.SemaphoreType.DMA((8,)),
    pltpu.SemaphoreType.DMA((10,)),
    pltpu.SemaphoreType.DMA((4,)),
    pltpu.SemaphoreType.DMA((4,)),
    pltpu.SemaphoreType.DMA((2,)),
]


def scatter_buffers(rows, cols, line_last=False):
    half = cols // 2
    return [
        pltpu.VMEM((16, rows, half), BF16),
        pltpu.VMEM((16, rows, half), BF16),
        pltpu.VMEM((8, rows, half), BF16),
        pltpu.VMEM((5 if line_last else 10, rows, half), BF16),
        pltpu.VMEM((4 if line_last else 1, rows, half), BF16),
        pltpu.VMEM((rows, half), F32),
        pltpu.VMEM((rows // 2, half), F32),
    ] + SCATTER_SEMS


class Scatter:
    def __init__(self, place, terms, out, buffers, line_last=False):
        self.place, self.terms, self.out, self.line_last = place, terms, out, line_last
        (self.own, self.other, self.got_b, self.got_z, self.got_a, self.total, self.got_f) = buffers[:7]
        (
            self.s_load, self.s_pair, self.r_pair, self.s_b, self.r_b, self.s_z, self.r_z, self.s_a, self.r_a, self.misc
        ) = buffers[7:]
        self.half = self.own.shape[2]
        self.tasks = (place.task_ab, place.task_b, place.task_a, place.task)
        self.tasks_partner = (place.task_ab, place.task_a, place.task_b, place.task)

    def cols(self, core):
        return pl.ds(pl.multiple_of(core * self.half, 128), self.half)

    def level(self, m):
        return self.place.low * m + (1 - self.place.low) * (3 - m)

    def load(self, index):
        first = self.tasks[index] * 4
        return pltpu.make_async_copy(
            self.terms.at[pl.ds(first, 4), :, self.cols(self.place.core)],
            self.own.at[pl.ds(first, 4)],
            self.s_load.at[index],
        )

    def pair(self, index, sent=True):
        first = (self.tasks_partner if sent else self.tasks)[index] * 4
        return remote(
            self.terms.at[pl.ds(first, 4), :, self.cols(1 - self.place.core)],
            self.other.at[pl.ds(first, 4)],
            self.s_pair.at[index],
            self.r_pair.at[index],
            self.place.partner,
        )

    def begin(self):
        for index in range(4):
            self.load(index).start()
            self.pair(index).start()

    def add(self, at, ref, where):
        self.own[at] = (self.own[at].astype(F32) + ref[where].astype(F32)).astype(BF16)

    def along_b(self, which, z):
        slot = which * 4 + z
        return remote(
            self.own.at[self.tasks[which] * 4 + z], self.got_b.at[slot], self.s_b.at[slot], self.r_b.at[slot],
            self.place.peer_b,
        )

    def add_pair(self, index):
        self.load(index).wait()
        self.pair(index, False).wait_recv()
        first = self.tasks[index] * 4
        for m in (3, 2, 1, 0):
            z = self.level(m)
            self.add(first + z, self.other, first + z)
            if index < 2:
                self.along_b(index, z).start()

    def add_b(self, which, m):
        z = self.level(m)
        self.along_b(which, z).wait_recv()
        self.add(self.tasks[2 + which] * 4 + z, self.got_b, which * 4 + z)
        if which == 0 and self.line_last:
            self.along_a(z).start()

    def along_z(self, which, m, far):
        place = self.place
        at = self.tasks[2 + which] * 4 + self.level(m)
        line = 0 if self.line_last else 5 * which
        into = line + ((1 - place.inner) * (m - 1) + place.inner * (6 - m) if far else 3 + m)
        peer = place.far if far else place.near
        return remote(self.own.at[at], self.got_z.at[into], self.s_z.at[which * 4 + m], self.r_z.at[into], peer)

    def add_z(self, which, m, slot):
        into = slot + (0 if self.line_last else 5 * which)
        got = self.got_z.at[into]
        remote(got, got, self.s_z.at[0], self.r_z.at[into], self.place.partner).wait_recv()
        self.add(self.tasks[2 + which] * 4 + self.level(m), self.got_z, into)

    def far_out(self, which, m):
        @pl.when(self.place.inner == 0)
        def _():
            self.along_z(which, m, True).start()

    def far_on(self, which, m):
        @pl.when(self.place.inner == 1)
        def _():
            self.add_z(which, m, m - 1)
            if m > 1:
                self.along_z(which, m, True).start()

    def near_on(self, which, m):
        @pl.when(self.place.inner == 1)
        def _():
            self.add_z(which, m, 3 + m)
            if m == 0:
                self.along_z(which, m, False).start()

    def near_in(self, which):
        @pl.when(self.place.inner == 0)
        def _():
            self.add_z(which, 0, 3)

    def along_a(self, z):
        slot = z if self.line_last else 0
        return remote(
            self.own.at[self.tasks[2] * 4 + z], self.got_a.at[slot], self.s_a.at[slot], self.r_a.at[slot],
            self.place.peer_a,
        )

    def to_a(self):
        self.along_a(self.place.z).start()

    def add_a(self, m):
        z = self.level(m)
        self.along_a(z).wait_recv()
        self.add(self.tasks[3] * 4 + z, self.got_a, z)

    def last(self):
        rows = self.got_f.shape[0]
        away = pl.multiple_of((1 - self.place.core) * rows, rows)
        return remote(
            self.total.at[pl.ds(away, rows)], self.got_f, self.misc.at[0], self.misc.at[1], self.place.partner
        )

    def close(self):
        total = self.own[self.tasks[3] * 4 + self.place.z].astype(F32)
        if not self.line_last:
            self.along_a(self.place.z).wait_recv()
            total = total + self.got_a[0].astype(F32)
        self.total[...] = total
        self.last().start()

    def finish(self):
        rows = self.got_f.shape[0]
        core = self.place.core
        self.last().wait_recv()
        self.out[:, self.cols(core)] = self.total[pl.ds(pl.multiple_of(core * rows, rows), rows), :]
        self.out[:, self.cols(1 - core)] = self.got_f[...]
        for index in range(4):
            self.pair(index).wait_send()
        for which in range(2):
            for z in range(4):
                self.along_b(which, z).wait_send()
        for which in range(1 if self.line_last else 0, 2):
            for m in range(4):

                @pl.when(self.place.inner < m)
                def _():
                    self.along_z(which, m, True).wait_send()

                @pl.when(self.place.inner > m)
                def _():
                    self.along_z(which, m, False).wait_send()

        for z in range(4 if self.line_last else 1):
            self.along_a(z if self.line_last else self.place.z).wait_send()
        self.last().wait_send()

    def events(self):
        out = [self.begin] + [partial(self.add_pair, i) for i in range(4)]
        if self.line_last:
            out += [partial(self.add_b, which, m) for which in range(2) for m in (3, 2, 1, 0)]
            for m in (3, 2, 1):
                out += [partial(self.add_a, m), partial(self.far_out, 1, m)]
            out.append(partial(self.add_a, 0))
            out += [partial(self.far_on, 1, m) for m in (3, 2, 1)]
            out += [partial(self.near_on, 1, 0), partial(self.near_on, 1, 1), partial(self.near_in, 1)]
        else:
            for which in range(2):
                for m in (3, 2, 1):
                    out += [partial(self.add_b, which, m), partial(self.far_out, which, m)]
                out.append(partial(self.add_b, which, 0))
                out += [partial(self.far_on, which, m) for m in (3, 2, 1)]
            for which in range(2):
                out += [partial(self.near_on, which, 0), partial(self.near_on, which, 1), partial(self.near_in, which)]
                if which == 0:
                    out.append(self.to_a)
        return out + [self.close, self.finish]


def dot(left, right):
    return lax.dot_general(left, right, (((1,), (0,)), ((), ())), preferred_element_type=F32)


def dot_right(left, right):
    return lax.dot_general(left, right, (((1,), (1,)), ((), ())), preferred_element_type=F32)


def at_slot(slot, plan):
    def choose(slots):
        if len(slots) == 1:

            @pl.when(slot == slots[0])
            def _():
                for event in plan[slots[0]]:
                    event()

            return
        middle_slot = slots[len(slots) // 2]

        @pl.when(slot < middle_slot)
        def _():
            choose(slots[: len(slots) // 2])

        @pl.when(slot >= middle_slot)
        def _():
            choose(slots[len(slots) // 2 :])

    if plan:
        choose(sorted(plan))


def fill_mask(seg_ref, pad_ref, mask_ref):
    length = mask_ref.shape[0]
    seg_row = seg_ref[0].astype(F32)
    pad_row = pad_ref[0].astype(F32)
    seg_col = jnp.transpose(jnp.broadcast_to(seg_row, (128, length)))
    pad_col = jnp.transpose(jnp.broadcast_to(pad_row, (128, length)))
    key_at = lax.broadcasted_iota(jnp.int32, (length, 128), 0)
    lane = lax.broadcasted_iota(jnp.int32, (length, 128), 1)
    for block in range(length // 128):
        same = seg_col == seg_row[:, 128 * block : 128 * block + 128]
        seen = (pad_col == 1.0) | (key_at == lane + 128 * block)
        mask_ref[:, 128 * block : 128 * block + 128] = jnp.where(same & seen, 0.0, -1e30)


def planned(table, jobs):
    plan = {}
    events = [job.events() for job in jobs]
    for slot, job, event in table:
        plan.setdefault(slot, []).append(events[job][event])
    return plan


def run_now(plan, slot):
    for event in plan.get(slot, []):
        event()


def every(plan, per_step, part, last):
    return {slot // per_step: e for slot, e in plan.items() if slot % per_step == part and slot < last}


def forward_kernel(near, x_ref, seg_ref, pad_ref, *refs):
    if near:
        rows_ref, wqkv_ref, wo_ref, win_ref, wd_ref = refs[:5]
        qkv_ref, att_ref, lse_ref, vec_ref = refs[5:9]
        fulls = refs[9:16]
        mask_ref, w_ref, small_ref, load_sem, shard_ref = refs[16:21]
        sems = refs[21:]
    else:
        fulls = refs[:4]
        qkv_ref, att_ref, lse_ref, vec_ref = refs[4:8]
        mask_ref, w_ref, small_ref, load_sem = refs[8:]
    step = pl.program_id(0)
    length, width = x_ref.shape
    part = width // GROUPS
    half = width // HEADS
    steps = GROUPS * SEQS
    plan = {}
    if near:
        place = Place()
        windows = [[shard_ref]]
        for group in range(GROUPS):
            windows.append([wqkv_ref.at[:, pl.ds(third * width + group * part, part)] for third in range(3)])
        windows += [[wo_ref], [win_ref], [wd_ref]]
        jobs = [
            Gather(place, windows[i], fulls[i], sems[5 * i : 5 * i + 5], GATHER_LINE_FIRST[i]) for i in range(7)
        ]
        plan = planned(GATHER_TABLE, jobs)

    @pl.when(step == 0)
    def _():
        if near:
            rows = rows_ref[...].astype(F32)
            rows = jnp.concatenate([rows, jnp.zeros((128 - rows.shape[0], 128), F32)], 0)
            shard_ref[:, :128] = jnp.transpose(rows)[: shard_ref.shape[0]].astype(BF16)
            shard_ref[:, 128:] = jnp.zeros((shard_ref.shape[0], 128), BF16)
            place.meet()
            run_now(plan, 0)
        copy = pltpu.make_async_copy(fulls[0].at[:, pl.ds(0, 128)], small_ref, load_sem.at[0])
        copy.start()
        copy.wait()
        vec_ref[...] = jnp.transpose(small_ref[...].astype(F32))[:16]

    if near:
        at_slot(step, {k: v for k, v in every(plan, 3, 0, 3 * steps).items() if k})
    for group in range(GROUPS):

        @pl.when(step == group * SEQS)
        def _():
            copy = pltpu.make_async_copy(fulls[1 + group], w_ref, load_sem.at[1])
            copy.start()
            copy.wait()

    fill_mask(seg_ref, pad_ref, mask_ref)
    at = pl.multiple_of(step // SEQS * part, part)
    for third, row in enumerate((BQ, None, BV)):
        cols = slice(third * part, (third + 1) * part)
        product = dot(x_ref[...], w_ref[:, cols])
        if row is not None:
            product = product + vec_ref[row : row + 1, pl.ds(at, part)]
        qkv_ref[:, cols] = product.astype(BF16)
    first_half = lax.broadcasted_iota(jnp.int32, (1, 2 * half), 1) < half
    for pair in range(part // (2 * half)):
        if near:
            at_slot(step, every(plan, 3, 1 + pair, 3 * steps))
        cols = slice(pair * 2 * half, (pair + 1) * 2 * half)
        queries = qkv_ref[:, cols]
        keys = qkv_ref[:, part + cols.start : part + cols.stop] * jnp.asarray(0.125, BF16)
        values_t = jnp.transpose(qkv_ref[:, 2 * part + cols.start : 2 * part + cols.stop])
        outs = []
        for head in range(2):
            mine = first_half if head == 0 else ~first_half
            scores = dot_right(jnp.where(mine, keys, jnp.zeros_like(keys)), queries) + mask_ref[...]
            top = jnp.max(scores, 0, keepdims=True)
            expo = jnp.exp(scores - top)
            total = jnp.sum(expo, 0, keepdims=True)
            probs = (expo * (1.0 / total)).astype(BF16)
            outs.append(dot(values_t[head * half : (head + 1) * half], probs))
            row = 2 * pair + head
            lse_ref[0, row : row + 1, :] = top + jnp.log(total)
        att_ref[:, cols] = jnp.transpose(jnp.concatenate(outs, 0)).astype(BF16)
    if near:

        @pl.when(step == steps - 1)
        def _():
            run_now(plan, 3 * steps)


SEQS = 4


def attention_forward(near, rows, segments, pads, weights):
    seqs, _, length = segments.shape
    width = rows.shape[1]
    part = width // GROUPS
    anywhere = lambda count: [pl.BlockSpec(memory_space=pl.ANY)] * count
    tokens = pl.BlockSpec((1, 1, length), lambda i: (i % seqs, 0, 0))
    shape = jax.ShapeDtypeStruct
    out_specs = [
        pl.BlockSpec((length, width), lambda i: (i % seqs, i // seqs)),
        pl.BlockSpec((length, part), lambda i: (i % seqs, i // seqs)),
        pl.BlockSpec((1, 8, length), lambda i: (i, 0, 0)),
        pl.BlockSpec((16, width), lambda i: (0, 0)),
    ]
    out_shape = [
        shape((rows.shape[0], 3 * width), BF16),
        shape((rows.shape[0], width), BF16),
        shape((GROUPS * seqs, 8, length), F32),
        shape((16, width), F32),
    ]
    in_specs = [pl.BlockSpec((length, width), lambda i: (i % seqs, 0)), tokens, tokens]
    scratch = [
        pltpu.VMEM((length, length), F32),
        pltpu.VMEM((width, width), BF16),
        pltpu.VMEM((width, 128), BF16),
        pltpu.SemaphoreType.DMA((2,)),
    ]
    remotely = {}
    if near:
        packed, w_qkv, w_out, w_in, w_down = weights
        in_specs += [pl.BlockSpec(packed.shape, lambda i: (0, 0))] + anywhere(4)
        mine = w_qkv.shape[0]
        fulls = [(mine, 256)] + [(mine, width)] * GROUPS + [w.shape for w in (w_out, w_in, w_down)]
        out_specs += anywhere(7)
        out_shape += [shape((32 * r, c), BF16) for r, c in fulls]
        scratch += [pltpu.VMEM((mine, 256), BF16)] + GATHER_SEMS * 7
        remotely = dict(collective_id=0, has_side_effects=True)
    else:
        in_specs += anywhere(4)
    return pl.pallas_call(
        partial(forward_kernel, near),
        name="attention_forward",
        grid=(GROUPS * seqs,),
        in_specs=in_specs,
        out_specs=out_specs,
        out_shape=out_shape,
        scratch_shapes=scratch,
        compiler_params=pltpu.CompilerParams(vmem_limit_bytes=VMEM_BYTES, **remotely),
    )(rows, segments, pads, *weights)


def norm_parts(arr):
    centre = arr - jnp.mean(arr, -1, keepdims=True)
    scale = lax.rsqrt(jnp.mean(centre * centre, -1, keepdims=True) + 1e-12)
    return centre * scale, scale


def norm_back(grad_normal, normal, scale):
    return scale * (
        grad_normal
        - jnp.mean(grad_normal, -1, keepdims=True)
        - normal * jnp.mean(grad_normal * normal, -1, keepdims=True)
    )


def column_sum(arr):
    return jnp.sum(arr.astype(F32), 0, keepdims=True)


def middle_kernel(
    scale_ref, x_ref, att_ref, cot_ref, wo_ref, win_ref, wd_ref, vec_ref, bin_ref,
    out_ref, sum_ref, datt_ref, gwo_ref, gwin_ref, gwd_ref, gvec_ref, gbin_ref,
    acc_wo, acc_win, acc_wd, act_ref, slope_ref,
):
    step = pl.program_id(0)
    width = x_ref.shape[1]
    hidden = win_ref.shape[1]
    chunks = hidden // width

    @pl.when(step == 0)
    def _():
        acc_wo[...] = jnp.zeros_like(acc_wo)
        acc_win[...] = jnp.zeros_like(acc_win)
        acc_wd[...] = jnp.zeros_like(acc_wd)
        gvec_ref[...] = jnp.zeros_like(gvec_ref)
        gbin_ref[...] = jnp.zeros_like(gbin_ref)

    vec = lambda row: vec_ref[row : row + 1, :]
    branch = dot(att_ref[...], wo_ref[...]) + vec(BO)
    normal_one, scale_one = norm_parts(x_ref[...].astype(F32) + branch)
    first = normal_one * vec(G1) + vec(S1)
    first_low = first.astype(BF16)
    second = first + vec(BD)
    for chunk in range(chunks):
        cols = slice(chunk * width, (chunk + 1) * width)
        pre = dot(first_low, win_ref[:, cols]) + bin_ref[:, cols]
        below = 0.5 + 0.5 * lax.erf(pre * 0.7071067811865476)
        act = (pre * below).astype(BF16)
        act_ref[:, cols] = act
        slope_ref[:, cols] = below + pre * (jnp.exp(pre * pre * -0.5) * 0.3989422804014327)
        second = second + dot(act, wd_ref[cols, :])
    normal_two, scale_two = norm_parts(second)
    out_ref[...] = (normal_two * vec(G2) + vec(S2)).astype(BF16)
    cot = cot_ref[...].astype(F32)
    gvec_ref[G2 : G2 + 1, :] += column_sum(cot * normal_two)
    gvec_ref[S2 : S2 + 1, :] += column_sum(cot)
    grad_second = norm_back(cot * vec(G2), normal_two, scale_two)
    grad_low = grad_second.astype(BF16)
    gvec_ref[BD : BD + 1, :] += column_sum(grad_low)
    first_t = jnp.transpose(first_low)
    grad_first = grad_second
    for chunk in range(chunks):
        cols = slice(chunk * width, (chunk + 1) * width)
        grad_pre = (slope_ref[:, cols] * dot_right(grad_low, wd_ref[cols, :])).astype(BF16)
        gbin_ref[:, cols] += column_sum(grad_pre)
        acc_wd[cols, :] += dot(jnp.transpose(act_ref[:, cols]), grad_low)
        acc_win[:, cols] += dot(first_t, grad_pre)
        grad_first = grad_first + dot_right(grad_pre, win_ref[:, cols])
    gvec_ref[G1 : G1 + 1, :] += column_sum(grad_first * normal_one)
    gvec_ref[S1 : S1 + 1, :] += column_sum(grad_first)
    grad_sum = norm_back(grad_first * vec(G1), normal_one, scale_one)
    sum_ref[...] = grad_sum
    grad_one = grad_sum.astype(BF16)
    gvec_ref[BO : BO + 1, :] += column_sum(grad_one)
    acc_wo[...] += dot(jnp.transpose(att_ref[...]), grad_one)
    datt_ref[...] = dot_right(grad_one, wo_ref[...]).astype(BF16)

    @pl.when(step == pl.num_programs(0) - 1)
    def _():
        weight = scale_ref[0]
        gwo_ref[...] = (acc_wo[...] * weight).astype(BF16)
        gwin_ref[...] = (acc_win[...] * weight).astype(BF16)
        gwd_ref[...] = (acc_wd[...] * weight).astype(BF16)
        gvec_ref[...] = gvec_ref[...] * weight
        gbin_ref[...] = gbin_ref[...] * weight


def middle(scale, rows, att, cot, w_out, w_in, w_down, vectors, b_in):
    count, width = rows.shape
    hidden = w_in.shape[1]
    tile = 256
    whole = lambda shape: pl.BlockSpec(shape, lambda i: (0,) * len(shape), pipeline_mode=pl.Buffered(1))
    row = pl.BlockSpec((tile, width), lambda i: (i, 0))
    shape = jax.ShapeDtypeStruct
    return pl.pallas_call(
        middle_kernel,
        name="middle",
        grid=(count // tile,),
        in_specs=[pl.BlockSpec(memory_space=pltpu.SMEM), row, row, row]
        + [whole(a.shape) for a in (w_out, w_in, w_down, vectors, b_in)],
        out_specs=[row, row, row]
        + [whole(s) for s in (w_out.shape, w_in.shape, w_down.shape, (16, width), (1, hidden))],
        out_shape=[
            shape((count, width), BF16),
            shape((count, width), F32),
            shape((count, width), BF16),
            shape(w_out.shape, BF16),
            shape(w_in.shape, BF16),
            shape(w_down.shape, BF16),
            shape((16, width), F32),
            shape((1, hidden), F32),
        ],
        scratch_shapes=[
            pltpu.VMEM(w_out.shape, F32),
            pltpu.VMEM(w_in.shape, F32),
            pltpu.VMEM(w_down.shape, F32),
            pltpu.VMEM((tile, hidden), BF16),
            pltpu.VMEM((tile, hidden), F32),
        ],
        compiler_params=pltpu.CompilerParams(vmem_limit_bytes=VMEM_BYTES),
        cost_estimate=pl.CostEstimate(flops=65_000_000_000, bytes_accessed=60_000_000, transcendentals=12_000_000),
    )(scale, rows, att, cot, w_out, w_in, w_down, vectors, b_in)


def backward_kernel(near, scale_ref, x_ref, qkv_ref, datt_ref, lse_ref, seg_ref, pad_ref, sum_ref, rest_ref, *refs):
    w_refs, refs = refs[:GROUPS], refs[GROUPS:]
    step = pl.program_id(0)
    length, width = x_ref.shape
    part = width // GROUPS
    half = width // HEADS
    steps = GROUPS * SEQS
    plan = {}
    if near:
        given, gx_ref, sums, refs = refs[:3], refs[3], refs[4:11], refs[11:]
        xt_ref, dqkv_ref, gvec_ref, mask_ref = refs[:4]
        terms = refs[4 : 5 + GROUPS]
        refs = refs[5 + GROUPS :]
        each = len(refs) // 7
        place = Place()
        jobs = [
            Scatter(place, t, sums[i], refs[each * i : each * (i + 1)], SCATTER_LINE_LAST[i])
            for i, t in enumerate(given + terms)
        ]
        plan = planned(SCATTER_TABLE, jobs)
        put = lambda ref, value: ref.__setitem__(..., value.reshape(ref.shape))
    else:
        gx_ref, terms, refs = refs[0], refs[1 : 2 + GROUPS], refs[2 + GROUPS :]
        xt_ref, dqkv_ref, gvec_ref, mask_ref = refs
        put = lambda ref, value: ref.__setitem__(..., value)

    @pl.when(step == 0)
    def _():
        if near:
            place.meet()
        gvec_ref[...] = jnp.zeros_like(gvec_ref)

    @pl.when(step < SEQS)
    def _():
        xt_ref[:, pl.ds(pl.multiple_of(step * length, length), length)] = jnp.transpose(x_ref[...])

    at = pl.multiple_of(step % SEQS * length, length)

    @pl.when(step < steps)
    def _():
        group = step // SEQS
        fill_mask(seg_ref, pad_ref, mask_ref)
        first_half = lax.broadcasted_iota(jnp.int32, (1, 2 * half), 1) < half
        for pair in range(part // (2 * half)):
            if near:
                at_slot(step, every(plan, 2, pair, 2 * steps))
            cols = slice(pair * 2 * half, (pair + 1) * 2 * half)
            queries = qkv_ref[:, cols]
            keys = qkv_ref[:, part + cols.start : part + cols.stop]
            values = qkv_ref[:, 2 * part + cols.start : 2 * part + cols.stop]
            grads = datt_ref[:, cols]
            keys_t = jnp.transpose(keys)
            keys = keys * jnp.asarray(0.125, BF16)
            grad_k = jnp.zeros(keys.shape, F32)
            grad_v = jnp.zeros(keys.shape, F32)
            grad_q = []
            for head in range(2):
                mine = first_half if head == 0 else ~first_half
                only = lambda arr: jnp.where(mine, arr, jnp.zeros_like(arr))
                scores = dot_right(only(keys), queries) + mask_ref[...]
                row = 2 * pair + head
                probs = jnp.exp(scores - lse_ref[0, row : row + 1, :])
                grad_probs = dot_right(only(values), grads)
                inner = jnp.sum(probs * grad_probs, 0, keepdims=True)
                grad_scores = (probs * (grad_probs - inner)).astype(BF16)
                grad_v = grad_v + dot(probs.astype(BF16), only(grads))
                grad_k = grad_k + dot(grad_scores, only(queries))
                grad_q.append(dot(keys_t[head * half : (head + 1) * half], grad_scores))
            grad_q = jnp.transpose(jnp.concatenate(grad_q, 0))
            for third, value in enumerate((grad_q * 0.125, grad_k * 0.125, grad_v)):
                to = slice(third * part + cols.start, third * part + cols.stop)
                dqkv_ref[group, pl.ds(at, length), to] = value.astype(BF16)
                if third != 1:
                    row = BQ if third == 0 else BV
                    into = pl.ds(pl.multiple_of(group * part + cols.start, 2 * half), 2 * half)
                    gvec_ref[row : row + 1, into] += column_sum(value.astype(BF16))

    for group in range(GROUPS):

        @pl.when(step == group * SEQS + SEQS - 1)
        def _():
            for third in range(3):
                cols = slice(third * part, (third + 1) * part)
                grad = dot(xt_ref[...], dqkv_ref[group, :, cols]) * scale_ref[0]
                if near:
                    terms[group][:, :, cols] = grad.astype(BF16).reshape(*terms[group].shape[:2], part)
                else:
                    terms[group][:, cols] = grad.astype(BF16)

    @pl.when(step == steps - 1)
    def _():
        gvec_ref[:2] = gvec_ref[:2] * scale_ref[0]
        gvec_ref[2:VECTORS] = rest_ref[2:VECTORS]
        packed = jnp.transpose(gvec_ref[...]).astype(BF16)
        put(terms[GROUPS], jnp.concatenate([packed, jnp.zeros_like(packed)], 1))

    @pl.when(step >= steps)
    def _():
        if near:
            at_slot(step, {k: v for k, v in every(plan, 2, 0, 2 * (steps + SEQS)).items() if k >= steps})
        grad_x = sum_ref[...]
        for group in range(GROUPS):
            grad_x = grad_x + dot_right(dqkv_ref[group, pl.ds(at, length), :], w_refs[group][...])
        gx_ref[...] = grad_x
        if near:
            at_slot(step, {k: v for k, v in every(plan, 2, 1, 2 * (steps + SEQS)).items() if k >= steps})

    if near:

        @pl.when(step == steps + SEQS - 1)
        def _():
            run_now(plan, 2 * (steps + SEQS))


def attention_backward(near, scale, rows, qkv, datt, lse, segments, pads, grad_sum, rest, w_groups, given):
    seqs, _, length = segments.shape
    count, width = rows.shape
    part = width // GROUPS
    steps = GROUPS * seqs
    whole = lambda shape: pl.BlockSpec(shape, lambda i: (0,) * len(shape), pipeline_mode=pl.Buffered(1))
    now = lambda i: jnp.minimum(i, steps - 1)
    tokens = pl.BlockSpec((1, 1, length), lambda i: (now(i) % seqs, 0, 0))
    late = pl.BlockSpec((length, width), lambda i: (jnp.maximum(i - steps, 0), 0))
    shape = jax.ShapeDtypeStruct
    in_specs = [
        pl.BlockSpec(memory_space=pltpu.SMEM),
        pl.BlockSpec((length, width), lambda i: (jnp.minimum(i, seqs - 1), 0)),
        pl.BlockSpec((length, width), lambda i: (now(i) % seqs, now(i) // seqs)),
        pl.BlockSpec((length, part), lambda i: (now(i) % seqs, now(i) // seqs)),
        pl.BlockSpec((1, 8, length), lambda i: (now(i), 0, 0)),
        tokens,
        tokens,
        late,
        whole(rest.shape),
    ] + [whole(w.shape) for w in w_groups]
    scratch = [
        pltpu.VMEM((width, count), BF16),
        pltpu.VMEM((GROUPS, count, width), BF16),
        pltpu.VMEM((128, width), F32),
        pltpu.VMEM((length, length), F32),
    ]
    out_shape = [shape((count, width), F32)]
    remotely = {}
    if near:
        in_specs += [pl.BlockSpec(memory_space=pl.ANY)] * 3
        made = [(16, width // 16, width)] * GROUPS + [(16, width // 16, 256)]
        scratch += [pltpu.VMEM(m, BF16) for m in made]
        every_shape = [g.shape for g in given] + made
        out_shape += [shape((s[1] // 2, s[2]), F32) for s in every_shape]
        for s, line_last in zip(every_shape, SCATTER_LINE_LAST):
            scratch += scatter_buffers(s[1], s[2], line_last)
        remotely = dict(collective_id=1, has_side_effects=True)
    else:
        out_shape += [shape((width, width), BF16)] * GROUPS + [shape((width, 256), BF16)]
    return pl.pallas_call(
        partial(backward_kernel, near),
        name="attention_backward",
        grid=(steps + seqs,),
        in_specs=in_specs,
        out_specs=[late] + [whole(s.shape) for s in out_shape[1:]],
        out_shape=out_shape,
        scratch_shapes=scratch,
        compiler_params=pltpu.CompilerParams(vmem_limit_bytes=VMEM_BYTES, **remotely),
    )(scale, rows, qkv, datt, lse, segments, pads, grad_sum, rest, *w_groups, *given)


def join_groups(parts, width):
    part = width // GROUPS
    cut = [p[:, third * part : (third + 1) * part] for third in range(3) for p in parts]
    return jnp.concatenate(cut, 1)


def finish_kernel(wd_ref, win_ref, wo_ref, *refs):
    parts, small_ref, outs = refs[:GROUPS], refs[GROUPS], refs[GROUPS + 1 :]
    qkv_ref, o_wd, o_win, o_wo = outs[:4]
    width = parts[0].shape[1]
    part = width // GROUPS
    for third in range(3):
        for group in range(GROUPS):
            cols = slice(third * width + group * part, third * width + (group + 1) * part)
            qkv_ref[:, cols] = parts[group][:, third * part : (third + 1) * part]
    o_wd[...] = wd_ref[...]
    o_win[...] = win_ref[...]
    o_wo[...] = wo_ref[...]
    mine = small_ref.shape[0]
    square = jnp.concatenate([small_ref[:, :128], jnp.zeros((128 - mine, 128), F32)], 0)
    vectors = jnp.transpose(square)
    for row in range(BIN):
        outs[4 + row][...] = vectors[row : row + 1, :mine]
    outs[4 + BIN][...] = vectors[BIN:VECTORS, :mine]


def finish(sums):
    wd, win, wo, *rest = sums
    mine, width = rest[0].shape
    shape = jax.ShapeDtypeStruct
    vmem = pl.BlockSpec(memory_space=pltpu.VMEM)
    outs = pl.pallas_call(
        finish_kernel,
        name="finish",
        in_specs=[vmem] * 7,
        out_specs=[vmem] * (5 + BIN),
        out_shape=[shape((mine, 3 * width), F32)]
        + [shape(a.shape, F32) for a in (wd, win, wo)]
        + [shape((1, mine), F32)] * BIN
        + [shape((VECTORS - BIN, mine), F32)],
    )(*sums)
    return outs[0], outs[1:4], [v.reshape(-1) for v in outs[4:]]


def body(
    hidden_in, out_grad, segment_ids, pad_mask, task_weight, w_qkv, b_query, b_value, w_out, b_out,
    gain_one, shift_one, w_in, b_in, w_down, b_down, gain_two, shift_two,
):
    seqs, length, width = hidden_in.shape
    mine = w_qkv.shape[0]
    part = width // GROUPS
    near = lax.axis_size("task") == 4 and lax.axis_size("batch") == 8 and mine % 8 == 0
    packed = jnp.concatenate([b_query, b_value, b_out, gain_one, shift_one, b_down, gain_two, shift_two, b_in])
    packed = packed.reshape(VECTORS, mine)
    rows = hidden_in.reshape(-1, width)
    segments = segment_ids.reshape(seqs, 1, length)
    pads = pad_mask.reshape(seqs, 1, length)
    if near:
        weights = [jnp.pad(packed, ((0, 16 - VECTORS), (0, 128 - mine))), w_qkv, w_out, w_in, w_down]
        qkv, att, lse, vectors, _, *full = attention_forward(True, rows, segments, pads, weights)
    else:
        packed = jnp.pad(jnp.transpose(packed), ((0, 0), (0, 256 - VECTORS)))
        cut = w_qkv.reshape(mine, 3, GROUPS, part)
        groups = [cut[:, :, g].reshape(mine, width) for g in range(GROUPS)]
        full = [lax.all_gather(w, AXES, axis=0, tiled=True) for w in (packed, *groups, w_out, w_in, w_down)]
        qkv, att, lse, vectors = attention_forward(False, rows, segments, pads, full[:4])
        full = full[1:]
    *w_groups, wo_full, win_full, wd_full = full
    bin_full = jnp.swapaxes(vectors[BIN:VECTORS].reshape(VECTORS - BIN, -1, mine), 0, 1).reshape(1, -1)
    hidden_out, grad_sum, datt, g_wo, g_win, g_wd, g_vec, g_bin = middle(
        task_weight, rows, att, out_grad.reshape(-1, width), wo_full, win_full, wd_full, vectors, bin_full
    )
    g_bin = jnp.swapaxes(g_bin.reshape(-1, VECTORS - BIN, mine), 0, 1).reshape(VECTORS - BIN, -1)
    g_rest = jnp.concatenate([g_vec[:BIN], g_bin, g_vec[VECTORS:]], 0)
    given = [g.reshape(16, -1, g.shape[1]) for g in (g_wd, g_win, g_wo)] if near else []
    grad_x, *terms = attention_backward(
        near, task_weight, rows, qkv, datt, lse, segments, pads, grad_sum, g_rest, w_groups, given
    )
    if near:
        s_qkv, (s_wd, s_win, s_wo), s_vec = finish(terms)
    else:
        s_wd, s_win, s_wo, *parts, small = [
            lax.psum_scatter(t, AXES, scatter_dimension=0, tiled=True).astype(F32) for t in (g_wd, g_win, g_wo, *terms)
        ]
        s_qkv = join_groups(parts, width)
        s_vec = [small[:, row] for row in range(BIN)] + [jnp.transpose(small[:, BIN:VECTORS]).reshape(-1)]
    return (
        hidden_out.reshape(hidden_in.shape),
        grad_x.reshape(hidden_in.shape),
        s_qkv,
        s_vec[BQ],
        s_vec[BV],
        s_wo,
        s_vec[BO],
        s_vec[G1],
        s_vec[S1],
        s_win,
        s_vec[BIN],
        s_wd,
        s_vec[BD],
        s_vec[G2],
        s_vec[S2],
    )


def solution(mesh):
    seq, mat, vec = P(AXES, None, None), P(AXES, None), P(AXES)
    weights = (mat, vec, vec, mat, vec, vec, vec, mat, vec, mat, vec, vec, vec)
    return jax.shard_map(
        body,
        mesh=mesh,
        in_specs=(seq, seq, mat, mat, P("task")) + weights,
        out_specs=(seq, seq) + weights,
        check_vma=False,
    )
```

time: 791 us -> 340 us (0.43)
  waiting for transfers between devices: 528 us -> 0 us
  Pallas kernels: 213 us -> 314 us
  between operations: 14.9 us -> 1.55 us
  other arithmetic: 13.5 us -> 2.01 us
    reduce_scatter x3 -> x0, waiting for transfers between devices: 230 us -> none  [the longest x1 111 us: body(): scatter(g_win).astype(F32)]
    all_gather x4 -> x0, waiting for transfers between devices: 193 us -> none  [the longest x3 135 us: body(): wo_full, win_full, wd_full = (gather(w_out), gather(w_in), gather(w_down))]
    unnamed x9 -> x0, waiting for transfers between devices: 105 us -> none
    pallas_call x2 -> x3, Pallas kernels: 119 us -> 220 us  [the longest x1 120 us: attention_backward(): pl.pallas_call(partial(backward_kernel, near), name='attention_backward',...]
  transfers between devices with their start and end apart: 8 -> 0, of which waited for: 8 -> 0; matrix products, arithmetic and copies ran while one was open for 3% -> 0% of each run, Pallas kernels for 15% -> 0%
where the time goes in v4:
time: 340 us; the launch traced here: 338 us
  Pallas kernels  314 us (92%)
  local copies, waits for them, and re-layouts  20.6 us (6%)
    pallas_call x1, Pallas kernels, attention_backward(): pl.pallas_call(partial(backward_kernel, near), name='attention_backward',...  120 us
    pallas_call x1, Pallas kernels, attention_forward(): pl.pallas_call(partial(forward_kernel, near), name='attention_forward', g...  98.3 us
    pallas_call x1, Pallas kernels, middle(): pl.pallas_call(middle_kernel, name='middle', grid=(count // tile,), in_sp...  93.9 us

profile of v4, /device:TPU:0, one launch (start us, length us, event | category | flops | bytes accessed | tf_op | source)
XLA Modules:
  0.0 338.3 jit_solution(14999099725307122341)
XLA Ops:
  0.6 1.3 reshape.100.seg_ref
  1.9 1.3 reshape.101.pad_ref
  3.2 6.1 %concatenate.6 = bf16[288]{0:T(512)(128)(2,1)S(1)} concatenate(bf16[24]{0:T(256)(128)(2,1)} %param.24, bf16[24]{0:T(256)(128)(2,1)} %param.25, bf16[24]{0:T(256)(128)(2,1)} %param.27, bf16[24]{0:T(256)(128)(2,1)} %param.28, bf16[24]{0:T(256)(128)(2,1)} %param.29, bf16[24]{0:T(256)(128)(2,1)} %param.33, bf16[24]{0:T(256)(128)(2,1)} %param.34, bf16[24]{0:T(256)(128)(2,1)} %param.35, ...), dimensions={0} | concatenate | bytes 1152 | tf_op jit(solution)/shard_map/concatenate | solution.py:1031
  9.3 0.1 reshape.102
  9.4 0.6 pad.4.refs_0_
  10.0 98.3 %attention_forward.1 = (bf16[2048,2304]{1,0:T(8,128)(2,1)}, bf16[2048,768]{1,0:T(8,128)(2,1)}, f32[12,8,512]{2,1,0:T(8,128)}, f32[16,768]{1,0:T(8,128)}, bf16[76...) custom-call(bf16[2048,768]{1,0:T(8,128)(2,1)} %bitcast.17, ...), custom_call_target="tpu_custom_call" | custom-call | tf_op jit(solution)/shard_map/attention_forward/pallas_call | solution.py:678
  108.4 0.7 slice.9
  109.1 0.1 reshape.104
  109.3 0.7 reshape.105.bin_ref
  110.7 93.9 %middle.1 = (bf16[2048,768]{1,0:T(8,128)(2,1)}, f32[2048,768]{1,0:T(8,128)}, bf16[2048,768]{1,0:T(8,128)(2,1)}, bf16[768,768]{1,0:T(8,128)(2,1)}, bf16[768,3072]...) custom-call(f32[1]{0:T(128)S(6)} %copy.38.scale_ref, ...), custom_call_target="tpu_custom_call" | custom-call | flops 65000001536 | bytes 60000000 | tf_op jit(solution)/shard_map/middle/pallas_call | solution.py:783
  204.6 0.7 slice.10
  205.3 0.7 slice.11
  206.0 0.5 broadcast.5
  206.6 1.4 reduce.3
  207.9 0.1 reshape.107
  208.1 0.1 reshape.108
  208.2 0.6 pad_maximum_fusion.rest_ref
  208.8 119.8 %attention_backward.1 = (f32[2048,768]{1,0:T(8,128)}, f32[96,768]{1,0:T(8,128)}, f32[24,3072]{1,0:T(8,128)}, f32[24,768]{1,0:T(8,128)}, f32[24,768]{1,0:T(8,128)...) custom-call(f32[1]{0:T(128)S(6)} %copy.38.scale_ref, bf16[2048,768]{1,0:T(8,128)(2,1)} %bitcast.19, ...), custom_call_target="tpu_custom_call" | custom-call | tf_op jit(solution)/shard_map/attention_backward/pallas_call | solution.py:967
  328.6 2.1 finish.1
  330.7 1.3 reshape.118
  332.0 6.1 %copy.39 = f32[4,512,768]{2,1,0:T(8,128)} copy(f32[4,512,768]{2,1,0:T(8,128)} %bitcast.20) | data formatting | bytes 12582912
  (2 shorter events, 0.1 us)

commit v5 on v4

--- a/solution.py
+++ b/solution.py
@@ -9,6 +9,7 @@
 
 HEADS = 12
 GROUPS = 3
+SEQS = 4
 AXES = ("task", "batch")
 F32 = jnp.float32
 BF16 = jnp.bfloat16
@@ -17,63 +18,58 @@
 VECTORS = 12
 
 GATHER_TABLE = [
-    (0, 0, 0), (0, 1, 0), (0, 0, 1), (0, 1, 1), (0, 0, 2), (0, 0, 3), (0, 0, 4), (0, 0, 5), (0, 1, 2), (0, 1, 3),
-    (0, 1, 4), (0, 1, 5), (0, 0, 6), (0, 0, 7), (0, 0, 8), (0, 0, 9), (0, 0, 10), (0, 0, 11), (0, 2, 0), (0, 0, 14),
-    (0, 0, 12), (0, 0, 13), (0, 1, 6), (0, 1, 7), (0, 1, 8), (0, 1, 10), (0, 2, 1), (0, 3, 0), (0, 0, 15), (0, 0, 16),
-    (0, 0, 17), (0, 0, 18), (0, 0, 21), (0, 0, 22), (0, 1, 9), (0, 1, 11), (0, 1, 14), (0, 0, 19), (0, 0, 20),
-    (0, 0, 23), (0, 0, 24), (0, 3, 1), (0, 4, 0), (0, 5, 0), (0, 6, 0), (0, 1, 12), (0, 1, 13), (0, 1, 15),
-    (0, 1, 16), (0, 1, 17), (0, 1, 18), (0, 1, 21), (0, 0, 26), (0, 2, 2), (0, 2, 3), (0, 4, 1), (0, 5, 1),
-    (0, 0, 25), (0, 2, 4), (0, 2, 5), (0, 6, 1), (0, 0, 27), (0, 0, 28), (0, 1, 22), (0, 0, 29), (0, 3, 2), (0, 3, 3),
-    (0, 3, 4), (0, 3, 5), (0, 1, 23), (0, 1, 24), (0, 1, 19), (0, 1, 20), (0, 1, 25), (0, 1, 26), (0, 2, 6),
-    (0, 2, 7), (0, 1, 27), (0, 1, 28), (0, 2, 8), (0, 2, 9), (0, 2, 10), (0, 2, 11), (0, 2, 12), (0, 2, 13),
-    (0, 2, 14), (0, 3, 6), (0, 3, 7), (0, 3, 8), (0, 3, 10), (0, 3, 11), (0, 4, 2), (0, 4, 3), (0, 4, 4), (0, 4, 5),
-    (0, 5, 2), (0, 5, 3), (0, 5, 4), (0, 5, 5), (0, 6, 2), (0, 6, 3), (0, 6, 4), (0, 6, 5), (0, 1, 29), (0, 3, 9),
-    (0, 3, 14), (1, 2, 15), (1, 2, 16), (1, 2, 17), (1, 2, 18), (1, 2, 21), (1, 2, 22), (1, 3, 12), (1, 3, 13),
-    (2, 2, 19), (2, 2, 20), (2, 2, 23), (2, 2, 24), (2, 3, 15), (2, 3, 16), (2, 3, 17), (2, 3, 18), (2, 4, 7),
-    (2, 4, 8), (3, 3, 21), (3, 4, 6), (3, 4, 9), (3, 4, 10), (3, 4, 11), (3, 4, 12), (4, 5, 6), (5, 5, 7), (5, 5, 8),
-    (6, 5, 9), (7, 5, 10), (7, 5, 11), (7, 5, 12), (8, 6, 6), (9, 2, 27), (9, 2, 28), (9, 3, 19), (9, 3, 20),
-    (9, 3, 23), (9, 3, 24), (9, 6, 9), (10, 6, 7), (10, 6, 8), (10, 6, 10), (11, 2, 25), (11, 2, 26), (11, 3, 22),
-    (11, 3, 25), (11, 3, 26), (11, 4, 13), (12, 2, 29), (12, 4, 14), (12, 4, 17), (12, 4, 18), (12, 6, 11),
-    (12, 6, 12), (13, 3, 27), (13, 3, 28), (13, 4, 15), (13, 4, 16), (13, 4, 19), (13, 4, 20), (13, 5, 13),
-    (14, 3, 29), (14, 5, 14), (16, 4, 25), (16, 4, 26), (16, 5, 15), (16, 5, 16), (16, 5, 17), (16, 5, 18),
-    (17, 6, 13), (18, 5, 19), (18, 5, 20), (18, 6, 14), (19, 4, 21), (19, 4, 22), (19, 6, 17), (19, 6, 18),
-    (20, 6, 15), (20, 6, 16), (21, 5, 21), (21, 5, 22), (21, 5, 25), (21, 5, 26), (23, 4, 23), (23, 4, 24),
-    (23, 6, 19), (23, 6, 20), (23, 6, 21), (23, 6, 22), (25, 4, 27), (25, 4, 28), (26, 4, 29), (26, 5, 23),
-    (26, 5, 24), (26, 6, 25), (26, 6, 26), (28, 6, 23), (28, 6, 24), (29, 5, 27), (29, 5, 28), (30, 5, 29),
-    (31, 6, 27), (31, 6, 28), (32, 6, 29),
+    (0, 0, 0), (0, 1, 0), (0, 2, 0), (0, 0, 1), (0, 1, 1), (0, 2, 1), (0, 3, 0), (0, 0, 3), (0, 0, 4), (0, 0, 5),
+    (0, 3, 1), (0, 0, 2), (0, 1, 2), (0, 1, 3), (0, 1, 4), (0, 1, 5), (0, 0, 9), (0, 0, 10), (0, 0, 11), (0, 0, 12),
+    (0, 2, 2), (0, 2, 3), (0, 2, 4), (0, 2, 5), (0, 6, 0), (0, 0, 6), (0, 0, 7), (0, 0, 8), (0, 3, 2), (0, 3, 3),
+    (0, 3, 4), (0, 3, 5), (0, 1, 6), (0, 0, 17), (0, 0, 18), (0, 1, 7), (0, 1, 8), (0, 1, 9), (0, 1, 10), (0, 1, 11),
+    (0, 1, 12), (0, 6, 1), (0, 0, 19), (0, 0, 20), (0, 2, 6), (0, 2, 7), (0, 2, 8), (0, 2, 9), (0, 2, 10), (0, 4, 0),
+    (0, 0, 13), (0, 0, 14), (0, 0, 15), (0, 0, 16), (0, 2, 11), (0, 2, 12), (0, 3, 6), (0, 3, 9), (0, 1, 13),
+    (0, 3, 7), (0, 3, 8), (0, 3, 10), (0, 3, 11), (0, 3, 12), (0, 4, 1), (0, 1, 14), (0, 1, 15), (0, 1, 16),
+    (0, 1, 17), (0, 1, 18), (0, 5, 0), (0, 1, 19), (0, 1, 20), (0, 0, 25), (0, 0, 26), (0, 5, 1), (0, 0, 21),
+    (0, 0, 22), (0, 2, 13), (0, 2, 14), (0, 6, 2), (0, 6, 3), (0, 6, 4), (0, 6, 5), (0, 0, 23), (0, 2, 15),
+    (0, 2, 16), (0, 2, 17), (0, 2, 18), (0, 0, 24), (0, 1, 25), (0, 3, 13), (0, 3, 14), (0, 1, 26), (0, 1, 21),
+    (0, 1, 22), (0, 2, 19), (0, 2, 20), (0, 3, 15), (0, 3, 16), (0, 3, 17), (0, 3, 18), (0, 3, 19), (0, 3, 20),
+    (0, 4, 4), (0, 4, 5), (0, 1, 23), (0, 4, 2), (0, 4, 3), (0, 1, 24), (0, 0, 27), (0, 6, 8), (0, 6, 10), (0, 5, 2),
+    (0, 5, 3), (0, 5, 4), (0, 5, 5), (0, 0, 28), (0, 0, 29), (0, 2, 23), (0, 2, 24), (0, 2, 25), (0, 2, 26),
+    (0, 3, 23), (0, 3, 24), (0, 3, 25), (0, 3, 26), (0, 6, 6), (0, 6, 7), (0, 1, 27), (0, 1, 28), (0, 6, 9),
+    (0, 6, 11), (0, 4, 6), (0, 4, 7), (0, 1, 29), (1, 2, 21), (1, 2, 22), (1, 2, 28), (1, 3, 21), (1, 3, 22),
+    (1, 6, 14), (1, 4, 8), (1, 4, 10), (1, 4, 14), (1, 5, 7), (1, 5, 8), (1, 3, 28), (2, 2, 27), (2, 3, 27),
+    (2, 6, 21), (2, 4, 9), (2, 4, 11), (2, 5, 6), (2, 5, 11), (2, 5, 12), (3, 2, 29), (3, 3, 29), (3, 6, 12),
+    (3, 6, 13), (3, 4, 12), (3, 4, 13), (3, 5, 9), (3, 5, 10), (4, 6, 15), (4, 6, 16), (4, 6, 17), (4, 6, 18),
+    (4, 5, 15), (4, 5, 16), (4, 5, 19), (4, 5, 20), (5, 6, 19), (5, 6, 20), (5, 6, 22), (5, 6, 23), (5, 6, 24),
+    (5, 4, 15), (5, 4, 16), (5, 4, 17), (5, 4, 18), (5, 4, 19), (5, 4, 20), (5, 4, 21), (5, 4, 23), (5, 4, 24),
+    (6, 4, 22), (6, 5, 13), (6, 5, 14), (6, 5, 23), (6, 5, 24), (7, 6, 25), (7, 6, 26), (7, 6, 27), (7, 6, 28),
+    (7, 4, 27), (7, 4, 28), (7, 5, 17), (7, 5, 18), (7, 5, 21), (7, 5, 22), (7, 5, 25), (7, 5, 26), (8, 6, 29),
+    (8, 4, 25), (8, 4, 26), (8, 5, 27), (8, 5, 28), (9, 4, 29), (9, 5, 29),
 ]
 SCATTER_TABLE = [
-    (0, 0, 0), (0, 1, 0), (0, 2, 0), (1, 0, 1), (2, 0, 2), (2, 0, 3), (3, 0, 4), (3, 0, 5), (3, 0, 6), (3, 0, 7),
-    (3, 0, 8), (3, 1, 1), (4, 0, 9), (4, 0, 10), (4, 1, 2), (4, 1, 3), (5, 0, 11), (5, 0, 12), (5, 0, 15), (5, 0, 16),
-    (5, 1, 4), (5, 2, 1), (5, 2, 2), (5, 2, 3), (5, 2, 4), (6, 0, 17), (6, 0, 18), (7, 0, 13), (7, 0, 19), (7, 0, 20),
-    (7, 0, 21), (7, 0, 25), (8, 3, 0), (8, 0, 14), (8, 0, 22), (8, 0, 26), (8, 0, 27), (8, 0, 28), (8, 1, 5),
-    (8, 1, 6), (8, 1, 7), (8, 1, 8), (8, 1, 9), (8, 1, 10), (9, 3, 1), (9, 3, 2), (9, 3, 3), (9, 3, 4), (9, 0, 23),
-    (9, 1, 11), (9, 1, 15), (9, 1, 16), (10, 0, 29), (10, 1, 17), (10, 1, 18), (11, 0, 24), (11, 1, 19), (11, 1, 20),
-    (11, 1, 21), (11, 2, 5), (11, 2, 6), (12, 0, 30), (12, 0, 31), (12, 1, 12), (12, 2, 7), (12, 2, 8), (12, 2, 9),
-    (12, 2, 10), (12, 2, 11), (12, 2, 15), (12, 2, 16), (12, 2, 17), (12, 2, 18), (12, 2, 19), (12, 2, 20),
-    (13, 3, 5), (13, 3, 6), (13, 0, 32), (13, 1, 13), (13, 2, 21), (14, 3, 7), (14, 3, 8), (14, 3, 9), (14, 3, 10),
-    (14, 3, 11), (14, 3, 15), (14, 3, 16), (14, 3, 17), (14, 3, 18), (14, 3, 19), (14, 3, 20), (14, 0, 33),
-    (14, 1, 25), (15, 3, 21), (15, 1, 14), (16, 4, 0), (16, 1, 22), (16, 1, 23), (16, 1, 26), (16, 1, 27),
-    (16, 1, 28), (17, 4, 1), (17, 4, 2), (17, 4, 3), (17, 4, 4), (17, 1, 24), (17, 2, 12), (18, 4, 5), (18, 4, 6),
-    (18, 4, 7), (18, 4, 8), (18, 1, 29), (18, 2, 13), (18, 2, 14), (18, 2, 22), (19, 3, 12), (19, 4, 9), (19, 4, 10),
-    (19, 4, 11), (19, 4, 15), (19, 4, 16), (19, 4, 17), (19, 4, 18), (19, 4, 19), (19, 4, 20), (19, 4, 21),
-    (19, 2, 23), (19, 2, 24), (20, 3, 13), (20, 3, 14), (20, 3, 22), (20, 1, 30), (20, 1, 31), (20, 1, 32),
-    (20, 2, 25), (20, 2, 26), (21, 3, 23), (21, 3, 24), (21, 3, 25), (21, 4, 12), (21, 1, 33), (21, 2, 27),
-    (21, 2, 28), (21, 2, 29), (21, 2, 30), (22, 3, 26), (22, 3, 27), (22, 3, 28), (22, 3, 29), (22, 3, 30),
-    (22, 4, 13), (22, 4, 14), (22, 4, 22), (23, 3, 31), (23, 3, 32), (23, 4, 23), (23, 4, 24), (23, 4, 25),
-    (23, 4, 26), (23, 2, 31), (23, 2, 32), (24, 3, 33), (24, 4, 27), (24, 4, 28), (24, 4, 29), (24, 4, 30),
-    (24, 5, 0), (24, 6, 0), (24, 2, 33), (25, 4, 31), (25, 4, 32), (25, 5, 1), (25, 5, 2), (25, 5, 3), (25, 5, 4),
-    (25, 6, 1), (25, 6, 2), (25, 6, 3), (25, 6, 4), (27, 4, 33), (27, 5, 5), (27, 5, 6), (27, 5, 7), (27, 5, 8),
-    (29, 5, 9), (29, 5, 10), (29, 5, 11), (29, 5, 12), (29, 5, 15), (29, 5, 16), (29, 5, 17), (29, 5, 18),
-    (29, 5, 19), (29, 5, 20), (29, 5, 21), (29, 6, 5), (29, 6, 6), (29, 6, 7), (29, 6, 8), (29, 6, 9), (29, 6, 10),
-    (29, 6, 11), (31, 5, 13), (31, 5, 14), (31, 5, 25), (31, 6, 15), (31, 6, 16), (31, 6, 17), (31, 6, 18),
-    (31, 6, 19), (31, 6, 20), (31, 6, 21), (32, 5, 22), (32, 5, 23), (32, 5, 24), (32, 5, 26), (32, 5, 27),
-    (32, 5, 28), (32, 6, 12), (32, 6, 13), (32, 6, 14), (32, 5, 29), (32, 6, 22), (32, 6, 23), (32, 6, 24),
-    (32, 5, 30), (32, 6, 25), (32, 6, 26), (32, 6, 29), (32, 6, 30), (32, 5, 31), (32, 5, 32), (32, 6, 27),
-    (32, 6, 28), (32, 5, 33), (32, 6, 31), (32, 6, 32), (32, 6, 33),
+    (0, 0, 0), (0, 1, 0), (1, 0, 1), (1, 0, 2), (2, 0, 3), (2, 0, 4), (2, 0, 5), (2, 1, 1), (2, 2, 0), (3, 0, 6),
+    (3, 0, 7), (3, 1, 2), (3, 1, 3), (3, 1, 4), (3, 2, 1), (3, 2, 2), (3, 2, 3), (3, 2, 4), (4, 3, 0), (4, 0, 8),
+    (4, 0, 9), (4, 0, 10), (4, 0, 11), (4, 0, 12), (5, 3, 1), (5, 3, 2), (5, 3, 3), (5, 3, 4), (5, 0, 13), (5, 0, 14),
+    (5, 1, 5), (6, 1, 6), (6, 1, 7), (6, 1, 8), (7, 0, 15), (7, 0, 16), (7, 0, 17), (7, 0, 18), (7, 0, 20), (8, 4, 0),
+    (8, 0, 21), (8, 1, 9), (8, 1, 10), (8, 1, 11), (8, 1, 12), (8, 2, 5), (8, 2, 6), (8, 2, 7), (8, 2, 8), (8, 2, 9),
+    (9, 4, 1), (9, 4, 2), (9, 4, 3), (9, 4, 4), (9, 3, 5), (9, 3, 6), (9, 3, 7), (9, 3, 8), (9, 0, 19), (9, 0, 22),
+    (9, 0, 23), (9, 2, 10), (9, 2, 11), (9, 2, 12), (9, 3, 9), (9, 0, 24), (10, 3, 10), (10, 3, 11), (10, 3, 12),
+    (10, 1, 13), (10, 1, 14), (11, 0, 25), (11, 0, 26), (11, 1, 15), (11, 1, 16), (11, 1, 17), (11, 1, 18),
+    (11, 1, 19), (11, 2, 13), (11, 2, 14), (12, 5, 0), (12, 6, 0), (12, 4, 5), (12, 4, 6), (12, 4, 7), (12, 4, 8),
+    (12, 4, 9), (12, 4, 10), (12, 4, 11), (12, 4, 12), (12, 3, 13), (12, 3, 14), (12, 3, 15), (12, 3, 16),
+    (12, 3, 17), (12, 3, 18), (12, 3, 19), (12, 0, 27), (12, 1, 20), (12, 1, 21), (12, 1, 22), (12, 2, 15),
+    (12, 2, 16), (12, 2, 17), (12, 2, 18), (12, 2, 19), (12, 2, 20), (13, 5, 1), (13, 5, 2), (13, 5, 3), (13, 5, 4),
+    (13, 6, 1), (13, 6, 2), (13, 6, 3), (13, 6, 4), (13, 4, 13), (13, 4, 14), (13, 4, 15), (13, 4, 16), (13, 4, 17),
+    (13, 4, 18), (13, 4, 19), (13, 3, 20), (13, 3, 21), (14, 5, 5), (14, 5, 6), (14, 5, 7), (14, 4, 20), (14, 3, 22),
+    (14, 1, 23), (14, 2, 21), (14, 2, 22), (14, 5, 8), (15, 5, 9), (15, 5, 10), (15, 5, 11), (15, 5, 12), (15, 6, 5),
+    (15, 6, 6), (15, 6, 7), (15, 6, 8), (15, 6, 9), (15, 6, 10), (15, 6, 11), (15, 6, 15), (15, 6, 16), (15, 6, 17),
+    (15, 6, 18), (15, 6, 19), (15, 6, 20), (15, 6, 21), (15, 4, 21), (15, 4, 22), (15, 3, 23), (15, 3, 24),
+    (15, 1, 24), (15, 2, 23), (15, 5, 13), (15, 5, 14), (15, 5, 15), (15, 5, 16), (16, 5, 17), (16, 5, 18),
+    (16, 5, 19), (16, 6, 12), (16, 6, 13), (16, 6, 14), (16, 6, 22), (16, 6, 23), (16, 6, 24), (16, 4, 23),
+    (16, 4, 24), (16, 3, 25), (16, 3, 26), (16, 1, 25), (16, 1, 26), (16, 2, 24), (16, 2, 25), (16, 2, 26),
+    (16, 5, 20), (16, 5, 21), (16, 3, 27), (16, 6, 25), (16, 1, 27), (16, 2, 27), (16, 6, 26), (16, 5, 22),
+    (16, 6, 29), (16, 6, 30), (16, 4, 25), (16, 4, 26), (16, 5, 23), (16, 6, 27), (16, 6, 28), (16, 4, 27),
+    (16, 5, 24), (16, 6, 31), (16, 6, 32), (16, 5, 25), (16, 5, 26), (16, 6, 33), (16, 5, 27),
 ]
-GATHER_LINE_FIRST = [True, True, True, True, False, False, False]
-SCATTER_LINE_LAST = [False, False, False, False, False, False, False]
+GATHER_LINE_FIRST = [False, False, False, False, True, False, True]
+SCATTER_LINE_LAST = [True, True, True, True, True, True, False]
+GATHER_SLOTS, SCATTER_SLOTS = 1, 1
 
 
 MESH = pl.DeviceIdType.MESH
@@ -342,7 +338,14 @@
             self.pair(index).start()
 
     def add(self, at, ref, where):
-        self.own[at] = (self.own[at].astype(F32) + ref[where].astype(F32)).astype(BF16)
+        size = 48 if self.half <= 512 else 16
+
+        def some(index, carry):
+            rows = pl.ds(pl.multiple_of(index * size, size), size)
+            self.own[at, rows] = self.own[at, rows] + ref[where, rows]
+            return carry
+
+        lax.fori_loop(0, self.own.shape[1] // size, some, 0)
 
     def along_b(self, which, z):
         slot = which * 4 + z
@@ -355,11 +358,15 @@
         self.load(index).wait()
         self.pair(index, False).wait_recv()
         first = self.tasks[index] * 4
-        for m in (3, 2, 1, 0):
-            z = self.level(m)
+
+        def chunk(count, carry):
+            z = self.level(3 - count)
             self.add(first + z, self.other, first + z)
             if index < 2:
                 self.along_b(index, z).start()
+            return carry
+
+        lax.fori_loop(0, 4, chunk, 0)
 
     def add_b(self, which, m):
         z = self.level(m)
@@ -516,10 +523,10 @@
         choose(sorted(plan))
 
 
-def fill_mask(seg_ref, pad_ref, mask_ref):
+def fill_mask(seg_ref, pad_ref, row, mask_ref):
     length = mask_ref.shape[0]
-    seg_row = seg_ref[0].astype(F32)
-    pad_row = pad_ref[0].astype(F32)
+    seg_row = seg_ref[pl.ds(row, 1), :].astype(F32)
+    pad_row = pad_ref[pl.ds(row, 1), :].astype(F32)
     seg_col = jnp.transpose(jnp.broadcast_to(seg_row, (128, length)))
     pad_col = jnp.transpose(jnp.broadcast_to(pad_row, (128, length)))
     key_at = lax.broadcasted_iota(jnp.int32, (length, 128), 0)
@@ -543,26 +550,25 @@
         event()
 
 
-def every(plan, per_step, part, last):
-    return {slot // per_step: e for slot, e in plan.items() if slot % per_step == part and slot < last}
-
-
-def forward_kernel(near, x_ref, seg_ref, pad_ref, *refs):
+def forward_kernel(near, devices, x_ref, seg_ref, pad_ref, *refs):
     if near:
-        rows_ref, wqkv_ref, wo_ref, win_ref, wd_ref = refs[:5]
-        qkv_ref, att_ref, lse_ref, vec_ref = refs[5:9]
+        vector_refs, refs = refs[: BIN + 1], refs[BIN + 1 :]
+        wqkv_ref, wo_ref, win_ref, wd_ref = refs[:4]
+        qkv_ref, att_ref, lse_ref, vec_ref, bin_ref = refs[4:9]
         fulls = refs[9:16]
-        mask_ref, w_ref, small_ref, load_sem, shard_ref = refs[16:21]
-        sems = refs[21:]
+        mask_ref, w_ref, small_ref, load_sem, shard_ref, square_ref = refs[16:22]
+        sems = refs[22:]
     else:
         fulls = refs[:4]
-        qkv_ref, att_ref, lse_ref, vec_ref = refs[4:8]
-        mask_ref, w_ref, small_ref, load_sem = refs[8:]
+        qkv_ref, att_ref, lse_ref, vec_ref, bin_ref = refs[4:9]
+        mask_ref, w_ref, small_ref, load_sem = refs[9:]
     step = pl.program_id(0)
     length, width = x_ref.shape
     part = width // GROUPS
     half = width // HEADS
     steps = GROUPS * SEQS
+    per = GATHER_SLOTS
+    last = per * steps
     plan = {}
     if near:
         place = Place()
@@ -578,9 +584,13 @@
     @pl.when(step == 0)
     def _():
         if near:
-            rows = rows_ref[...].astype(F32)
-            rows = jnp.concatenate([rows, jnp.zeros((128 - rows.shape[0], 128), F32)], 0)
-            shard_ref[:, :128] = jnp.transpose(rows)[: shard_ref.shape[0]].astype(BF16)
+            mine = shard_ref.shape[0]
+            square_ref[...] = jnp.zeros_like(square_ref)
+            for row, ref in enumerate(vector_refs):
+                vector = ref[...].astype(F32).reshape(1, ref.shape[0])
+                for j in range(ref.shape[0] // mine):
+                    square_ref[row + j : row + j + 1, :mine] = vector[:, j * mine : (j + 1) * mine]
+            shard_ref[:, :128] = jnp.transpose(square_ref[...])[:mine].astype(BF16)
             shard_ref[:, 128:] = jnp.zeros((shard_ref.shape[0], 128), BF16)
             place.meet()
             run_now(plan, 0)
@@ -588,9 +598,14 @@
         copy.start()
         copy.wait()
         vec_ref[...] = jnp.transpose(small_ref[...].astype(F32))[:16]
+        mine = small_ref.shape[0] // devices
+        for d in range(devices):
+            for j in range(VECTORS - BIN):
+                start = (d * (VECTORS - BIN) + j) * mine
+                bin_ref[:, start : start + mine] = vec_ref[BIN + j : BIN + j + 1, d * mine : (d + 1) * mine]
 
     if near:
-        at_slot(step, {k: v for k, v in every(plan, 3, 0, 3 * steps).items() if k})
+        at_slot(per * step, {s: e for s, e in plan.items() if s % per == 0 and 0 < s < last})
     for group in range(GROUPS):
 
         @pl.when(step == group * SEQS)
@@ -599,7 +614,7 @@
             copy.start()
             copy.wait()
 
-    fill_mask(seg_ref, pad_ref, mask_ref)
+    fill_mask(seg_ref, pad_ref, step % SEQS, mask_ref)
     at = pl.multiple_of(step // SEQS * part, part)
     for third, row in enumerate((BQ, None, BV)):
         cols = slice(third * part, (third + 1) * part)
@@ -608,13 +623,15 @@
             product = product + vec_ref[row : row + 1, pl.ds(at, part)]
         qkv_ref[:, cols] = product.astype(BF16)
     first_half = lax.broadcasted_iota(jnp.int32, (1, 2 * half), 1) < half
-    for pair in range(part // (2 * half)):
-        if near:
-            at_slot(step, every(plan, 3, 1 + pair, 3 * steps))
-        cols = slice(pair * 2 * half, (pair + 1) * 2 * half)
-        queries = qkv_ref[:, cols]
-        keys = qkv_ref[:, part + cols.start : part + cols.stop] * jnp.asarray(0.125, BF16)
-        values_t = jnp.transpose(qkv_ref[:, 2 * part + cols.start : 2 * part + cols.stop])
+    pairs = part // (2 * half)
+
+    def attend(pair):
+        if near and 0 < pair < per:
+            at_slot(per * step + pair, {s: e for s, e in plan.items() if s % per == pair and s < last})
+        base = pair * 2 * half
+        queries = qkv_ref[:, pl.ds(base, 2 * half)]
+        keys = qkv_ref[:, pl.ds(part + base, 2 * half)] * jnp.asarray(0.125, BF16)
+        values_t = jnp.transpose(qkv_ref[:, pl.ds(2 * part + base, 2 * half)])
         outs = []
         for head in range(2):
             mine = first_half if head == 0 else ~first_half
@@ -624,37 +641,38 @@
             total = jnp.sum(expo, 0, keepdims=True)
             probs = (expo * (1.0 / total)).astype(BF16)
             outs.append(dot(values_t[head * half : (head + 1) * half], probs))
-            row = 2 * pair + head
-            lse_ref[0, row : row + 1, :] = top + jnp.log(total)
-        att_ref[:, cols] = jnp.transpose(jnp.concatenate(outs, 0)).astype(BF16)
+            lse_ref[0, pl.ds(2 * pair + head, 1), :] = top + jnp.log(total)
+        att_ref[:, pl.ds(base, 2 * half)] = jnp.transpose(jnp.concatenate(outs, 0)).astype(BF16)
+
+    for pair in range(pairs):
+        attend(pair)
     if near:
 
         @pl.when(step == steps - 1)
         def _():
-            run_now(plan, 3 * steps)
-
-
-SEQS = 4
+            run_now(plan, last)
 
 
 def attention_forward(near, rows, segments, pads, weights):
-    seqs, _, length = segments.shape
+    seqs, length = segments.shape
     width = rows.shape[1]
     part = width // GROUPS
     anywhere = lambda count: [pl.BlockSpec(memory_space=pl.ANY)] * count
-    tokens = pl.BlockSpec((1, 1, length), lambda i: (i % seqs, 0, 0))
+    tokens = pl.BlockSpec((seqs, length), lambda i: (0, 0))
     shape = jax.ShapeDtypeStruct
     out_specs = [
         pl.BlockSpec((length, width), lambda i: (i % seqs, i // seqs)),
         pl.BlockSpec((length, part), lambda i: (i % seqs, i // seqs)),
         pl.BlockSpec((1, 8, length), lambda i: (i, 0, 0)),
         pl.BlockSpec((16, width), lambda i: (0, 0)),
+        pl.BlockSpec((1, (VECTORS - BIN) * width), lambda i: (0, 0)),
     ]
     out_shape = [
         shape((rows.shape[0], 3 * width), BF16),
         shape((rows.shape[0], width), BF16),
         shape((GROUPS * seqs, 8, length), F32),
         shape((16, width), F32),
+        shape((1, (VECTORS - BIN) * width), F32),
     ]
     in_specs = [pl.BlockSpec((length, width), lambda i: (i % seqs, 0)), tokens, tokens]
     scratch = [
@@ -665,18 +683,19 @@
     ]
     remotely = {}
     if near:
-        packed, w_qkv, w_out, w_in, w_down = weights
-        in_specs += [pl.BlockSpec(packed.shape, lambda i: (0, 0))] + anywhere(4)
+        *vectors, w_qkv, w_out, w_in, w_down = weights
+        in_specs += [pl.BlockSpec(v.shape, lambda i: (0,)) for v in vectors]
+        in_specs += [pl.BlockSpec(w.shape, lambda i: (0, 0)) for w in (w_qkv, w_out, w_in, w_down)]
         mine = w_qkv.shape[0]
         fulls = [(mine, 256)] + [(mine, width)] * GROUPS + [w.shape for w in (w_out, w_in, w_down)]
         out_specs += anywhere(7)
         out_shape += [shape((32 * r, c), BF16) for r, c in fulls]
-        scratch += [pltpu.VMEM((mine, 256), BF16)] + GATHER_SEMS * 7
+        scratch += [pltpu.VMEM((mine, 256), BF16), pltpu.VMEM((128, 128), F32)] + GATHER_SEMS * 7
         remotely = dict(collective_id=0, has_side_effects=True)
     else:
         in_specs += anywhere(4)
     return pl.pallas_call(
-        partial(forward_kernel, near),
+        partial(forward_kernel, near, lax.axis_size(AXES)),
         name="attention_forward",
         grid=(GROUPS * seqs,),
         in_specs=in_specs,
@@ -706,9 +725,9 @@
 
 
 def middle_kernel(
-    scale_ref, x_ref, att_ref, cot_ref, wo_ref, win_ref, wd_ref, vec_ref, bin_ref,
-    out_ref, sum_ref, datt_ref, gwo_ref, gwin_ref, gwd_ref, gvec_ref, gbin_ref,
-    acc_wo, acc_win, acc_wd, act_ref, slope_ref,
+    mine, scale_ref, x_ref, att_ref, cot_ref, wo_ref, win_ref, wd_ref, vec_ref, bin_ref,
+    out_ref, sum_ref, datt_ref, gwo_ref, gwin_ref, gwd_ref, gvec_ref,
+    gbin_ref, acc_wo, acc_win, acc_wd, act_ref, slope_ref,
 ):
     step = pl.program_id(0)
     width = x_ref.shape[1]
@@ -766,14 +785,24 @@
     @pl.when(step == pl.num_programs(0) - 1)
     def _():
         weight = scale_ref[0]
-        gwo_ref[...] = (acc_wo[...] * weight).astype(BF16)
-        gwin_ref[...] = (acc_win[...] * weight).astype(BF16)
-        gwd_ref[...] = (acc_wd[...] * weight).astype(BF16)
+
+        def cast(index, carry):
+            for ref, acc in ((gwo_ref, acc_wo), (gwin_ref, acc_win), (gwd_ref, acc_wd)):
+                size = acc.shape[0] // 24
+                some = pl.ds(pl.multiple_of(index * size, size), size)
+                ref[some, :] = (acc[some, :] * weight).astype(BF16)
+            return carry
+
+        lax.fori_loop(0, 24, cast, 0)
         gvec_ref[...] = gvec_ref[...] * weight
-        gbin_ref[...] = gbin_ref[...] * weight
-
-
-def middle(scale, rows, att, cot, w_out, w_in, w_down, vectors, b_in):
+        for row in range(VECTORS - BIN):
+            for d in range(width // mine):
+                start = (d * (VECTORS - BIN) + row) * mine
+                piece = gbin_ref[:, start : start + mine] * weight
+                gvec_ref[BIN + row : BIN + row + 1, d * mine : (d + 1) * mine] = piece
+
+
+def middle(scale, rows, att, cot, w_out, w_in, w_down, vectors, b_in, mine):
     count, width = rows.shape
     hidden = w_in.shape[1]
     tile = 256
@@ -781,13 +810,13 @@
     row = pl.BlockSpec((tile, width), lambda i: (i, 0))
     shape = jax.ShapeDtypeStruct
     return pl.pallas_call(
-        middle_kernel,
+        partial(middle_kernel, mine),
         name="middle",
         grid=(count // tile,),
         in_specs=[pl.BlockSpec(memory_space=pltpu.SMEM), row, row, row]
         + [whole(a.shape) for a in (w_out, w_in, w_down, vectors, b_in)],
         out_specs=[row, row, row]
-        + [whole(s) for s in (w_out.shape, w_in.shape, w_down.shape, (16, width), (1, hidden))],
+        + [whole(s) for s in (w_out.shape, w_in.shape, w_down.shape, (16, width))],
         out_shape=[
             shape((count, width), BF16),
             shape((count, width), F32),
@@ -796,9 +825,9 @@
             shape(w_in.shape, BF16),
             shape(w_down.shape, BF16),
             shape((16, width), F32),
-            shape((1, hidden), F32),
         ],
         scratch_shapes=[
+            pltpu.VMEM((1, hidden), F32),
             pltpu.VMEM(w_out.shape, F32),
             pltpu.VMEM(w_in.shape, F32),
             pltpu.VMEM(w_down.shape, F32),
@@ -817,6 +846,8 @@
     part = width // GROUPS
     half = width // HEADS
     steps = GROUPS * SEQS
+    per = SCATTER_SLOTS
+    last = per * (steps + SEQS)
     plan = {}
     if near:
         given, gx_ref, sums, refs = refs[:3], refs[3], refs[4:11], refs[11:]
@@ -851,16 +882,17 @@
     @pl.when(step < steps)
     def _():
         group = step // SEQS
-        fill_mask(seg_ref, pad_ref, mask_ref)
+        fill_mask(seg_ref, pad_ref, step % SEQS, mask_ref)
         first_half = lax.broadcasted_iota(jnp.int32, (1, 2 * half), 1) < half
-        for pair in range(part // (2 * half)):
-            if near:
-                at_slot(step, every(plan, 2, pair, 2 * steps))
-            cols = slice(pair * 2 * half, (pair + 1) * 2 * half)
-            queries = qkv_ref[:, cols]
-            keys = qkv_ref[:, part + cols.start : part + cols.stop]
-            values = qkv_ref[:, 2 * part + cols.start : 2 * part + cols.stop]
-            grads = datt_ref[:, cols]
+        pairs = part // (2 * half)
+
+        def back(pair):
+            if near and pair < per:
+                at_slot(per * step + pair, {s: e for s, e in plan.items() if s % per == pair and s < per * steps})
+            base = pair * 2 * half
+            pick = lambda ref, start: ref[:, pl.ds(start + base, 2 * half)]
+            queries, keys, values = (pick(qkv_ref, third * part) for third in range(3))
+            grads = pick(datt_ref, 0)
             keys_t = jnp.transpose(keys)
             keys = keys * jnp.asarray(0.125, BF16)
             grad_k = jnp.zeros(keys.shape, F32)
@@ -870,8 +902,7 @@
                 mine = first_half if head == 0 else ~first_half
                 only = lambda arr: jnp.where(mine, arr, jnp.zeros_like(arr))
                 scores = dot_right(only(keys), queries) + mask_ref[...]
-                row = 2 * pair + head
-                probs = jnp.exp(scores - lse_ref[0, row : row + 1, :])
+                probs = jnp.exp(scores - lse_ref[0, pl.ds(2 * pair + head, 1), :])
                 grad_probs = dot_right(only(values), grads)
                 inner = jnp.sum(probs * grad_probs, 0, keepdims=True)
                 grad_scores = (probs * (grad_probs - inner)).astype(BF16)
@@ -880,12 +911,14 @@
                 grad_q.append(dot(keys_t[head * half : (head + 1) * half], grad_scores))
             grad_q = jnp.transpose(jnp.concatenate(grad_q, 0))
             for third, value in enumerate((grad_q * 0.125, grad_k * 0.125, grad_v)):
-                to = slice(third * part + cols.start, third * part + cols.stop)
-                dqkv_ref[group, pl.ds(at, length), to] = value.astype(BF16)
+                dqkv_ref[group, pl.ds(at, length), pl.ds(third * part + base, 2 * half)] = value.astype(BF16)
                 if third != 1:
                     row = BQ if third == 0 else BV
-                    into = pl.ds(pl.multiple_of(group * part + cols.start, 2 * half), 2 * half)
+                    into = pl.ds(pl.multiple_of(group * part + base, 2 * half), 2 * half)
                     gvec_ref[row : row + 1, into] += column_sum(value.astype(BF16))
+
+        for pair in range(pairs):
+            back(pair)
 
     for group in range(GROUPS):
 
@@ -909,29 +942,29 @@
     @pl.when(step >= steps)
     def _():
         if near:
-            at_slot(step, {k: v for k, v in every(plan, 2, 0, 2 * (steps + SEQS)).items() if k >= steps})
+            at_slot(per * step, {s: e for s, e in plan.items() if s % per == 0 and per * steps <= s < last})
         grad_x = sum_ref[...]
         for group in range(GROUPS):
             grad_x = grad_x + dot_right(dqkv_ref[group, pl.ds(at, length), :], w_refs[group][...])
         gx_ref[...] = grad_x
-        if near:
-            at_slot(step, {k: v for k, v in every(plan, 2, 1, 2 * (steps + SEQS)).items() if k >= steps})
+        if near and per > 1:
+            at_slot(per * step, {s - 1: e for s, e in plan.items() if s % per and per * steps < s < last})
 
     if near:
 
         @pl.when(step == steps + SEQS - 1)
         def _():
-            run_now(plan, 2 * (steps + SEQS))
+            run_now(plan, last)
 
 
 def attention_backward(near, scale, rows, qkv, datt, lse, segments, pads, grad_sum, rest, w_groups, given):
-    seqs, _, length = segments.shape
+    seqs, length = segments.shape
     count, width = rows.shape
     part = width // GROUPS
     steps = GROUPS * seqs
     whole = lambda shape: pl.BlockSpec(shape, lambda i: (0,) * len(shape), pipeline_mode=pl.Buffered(1))
     now = lambda i: jnp.minimum(i, steps - 1)
-    tokens = pl.BlockSpec((1, 1, length), lambda i: (now(i) % seqs, 0, 0))
+    tokens = whole((seqs, length))
     late = pl.BlockSpec((length, width), lambda i: (jnp.maximum(i - steps, 0), 0))
     shape = jax.ShapeDtypeStruct
     in_specs = [
@@ -999,7 +1032,7 @@
     vectors = jnp.transpose(square)
     for row in range(BIN):
         outs[4 + row][...] = vectors[row : row + 1, :mine]
-    outs[4 + BIN][...] = vectors[BIN:VECTORS, :mine]
+    outs[4 + BIN][...] = jnp.concatenate([vectors[row : row + 1, :mine] for row in range(BIN, VECTORS)], 1)
 
 
 def finish(sums):
@@ -1015,7 +1048,7 @@
         out_shape=[shape((mine, 3 * width), F32)]
         + [shape(a.shape, F32) for a in (wd, win, wo)]
         + [shape((1, mine), F32)] * BIN
-        + [shape((VECTORS - BIN, mine), F32)],
+        + [shape((1, (VECTORS - BIN) * mine), F32)],
     )(*sums)
     return outs[0], outs[1:4], [v.reshape(-1) for v in outs[4:]]
 
@@ -1028,31 +1061,26 @@
     mine = w_qkv.shape[0]
     part = width // GROUPS
     near = lax.axis_size("task") == 4 and lax.axis_size("batch") == 8 and mine % 8 == 0
-    packed = jnp.concatenate([b_query, b_value, b_out, gain_one, shift_one, b_down, gain_two, shift_two, b_in])
-    packed = packed.reshape(VECTORS, mine)
+    vectors = [b_query, b_value, b_out, gain_one, shift_one, b_down, gain_two, shift_two, b_in]
     rows = hidden_in.reshape(-1, width)
-    segments = segment_ids.reshape(seqs, 1, length)
-    pads = pad_mask.reshape(seqs, 1, length)
     if near:
-        weights = [jnp.pad(packed, ((0, 16 - VECTORS), (0, 128 - mine))), w_qkv, w_out, w_in, w_down]
-        qkv, att, lse, vectors, _, *full = attention_forward(True, rows, segments, pads, weights)
+        weights = [*vectors, w_qkv, w_out, w_in, w_down]
+        qkv, att, lse, vectors, bin_full, _, *full = attention_forward(True, rows, segment_ids, pad_mask, weights)
     else:
-        packed = jnp.pad(jnp.transpose(packed), ((0, 0), (0, 256 - VECTORS)))
+        packed = jnp.transpose(jnp.concatenate(vectors).reshape(VECTORS, mine))
+        packed = jnp.pad(packed, ((0, 0), (0, 256 - VECTORS)))
         cut = w_qkv.reshape(mine, 3, GROUPS, part)
         groups = [cut[:, :, g].reshape(mine, width) for g in range(GROUPS)]
         full = [lax.all_gather(w, AXES, axis=0, tiled=True) for w in (packed, *groups, w_out, w_in, w_down)]
-        qkv, att, lse, vectors = attention_forward(False, rows, segments, pads, full[:4])
+        qkv, att, lse, vectors, bin_full = attention_forward(False, rows, segment_ids, pad_mask, full[:4])
         full = full[1:]
     *w_groups, wo_full, win_full, wd_full = full
-    bin_full = jnp.swapaxes(vectors[BIN:VECTORS].reshape(VECTORS - BIN, -1, mine), 0, 1).reshape(1, -1)
-    hidden_out, grad_sum, datt, g_wo, g_win, g_wd, g_vec, g_bin = middle(
-        task_weight, rows, att, out_grad.reshape(-1, width), wo_full, win_full, wd_full, vectors, bin_full
+    hidden_out, grad_sum, datt, g_wo, g_win, g_wd, g_rest = middle(
+        task_weight, rows, att, out_grad.reshape(-1, width), wo_full, win_full, wd_full, vectors, bin_full, mine
     )
-    g_bin = jnp.swapaxes(g_bin.reshape(-1, VECTORS - BIN, mine), 0, 1).reshape(VECTORS - BIN, -1)
-    g_rest = jnp.concatenate([g_vec[:BIN], g_bin, g_vec[VECTORS:]], 0)
     given = [g.reshape(16, -1, g.shape[1]) for g in (g_wd, g_win, g_wo)] if near else []
     grad_x, *terms = attention_backward(
-        near, task_weight, rows, qkv, datt, lse, segments, pads, grad_sum, g_rest, w_groups, given
+        near, task_weight, rows, qkv, datt, lse, segment_ids, pad_mask, grad_sum, g_rest, w_groups, given
     )
     if near:
         s_qkv, (s_wd, s_win, s_wo), s_vec = finish(terms)

time: 340 us -> 294 us (0.86)
  Pallas kernels: 314 us -> 286 us
  local copies, waits for them, and re-layouts: 20.6 us -> 6.09 us
    pallas_call x1, Pallas kernels: 120 us -> 102 us  [attention_backward(): pl.pallas_call(partial(backward_kernel, near), name='attention_backward',...]
    pallas_call x2, Pallas kernels: 192 us -> 182 us  [the longest x1 94.2 us: middle(): pl.pallas_call(partial(middle_kernel, mine), name='middle', grid=(count /...]
    concatenate x1 -> x0, local copies, waits for them, and re-layouts: 6.1 us -> none  [body(): jnp.concatenate([b_query, b_value, b_out, gain_one, shift_one, b_down, ga...]
    reshape x8 -> x0, local copies, waits for them, and re-layouts: 4.99 us -> none  [the longest x1 1.3 us: body(): segments = segment_ids.reshape(seqs, 1, length)]
where the time goes in v5:
time: 294 us; the launch traced here: 293 us
  Pallas kernels  286 us (97%)
  local copies, waits for them, and re-layouts  6.09 us (2%)
    pallas_call x1, Pallas kernels, attention_backward(): pl.pallas_call(partial(backward_kernel, near), name='attention_backward',...  102 us
    pallas_call x1, Pallas kernels, middle(): pl.pallas_call(partial(middle_kernel, mine), name='middle', grid=(count /...  94.2 us
    pallas_call x1, Pallas kernels, attention_forward(): pl.pallas_call(partial(forward_kernel, near, lax.axis_size(AXES)), name='...  87.9 us
    unnamed x1, local copies, waits for them, and re-layouts  6.09 us

profile of v5, /device:TPU:0, one launch (start us, length us, event | category | flops | bytes accessed | tf_op | source)
XLA Modules:
  0.0 293.4 jit_solution(3235379261409897916)
XLA Ops:
  1.3 87.9 %attention_forward.1 = (bf16[2048,2304]{1,0:T(8,128)(2,1)}, bf16[2048,768]{1,0:T(8,128)(2,1)}, f32[12,8,512]{2,1,0:T(8,128)}, f32[16,768]{1,0:T(8,128)}, f32[1,3...) custom-call(bf16[2048,768]{1,0:T(8,128)(2,1)} %bitcast.16, ...), custom_call_target="tpu_custom_call" | custom-call | tf_op jit(solution)/shard_map/attention_forward/pallas_call | solution.py:697
  89.2 94.2 %middle.1 = (bf16[2048,768]{1,0:T(8,128)(2,1)}, f32[2048,768]{1,0:T(8,128)}, bf16[2048,768]{1,0:T(8,128)(2,1)}, bf16[768,768]{1,0:T(8,128)(2,1)}, bf16[768,3072]...) custom-call(f32[1]{0:T(128)S(6)} %copy.34.scale_ref, bf16[2048,768]{1,0:T(8,128)(2,1)} %bitcast.17, ...), custom_call_target="tpu_custom_call" | custom-call | flops 65000001536 | bytes 60000000 | tf_op jit(solution)/shard_map/middle/pallas_call | solution.py:812
  183.4 101.7 %attention_backward.1 = (f32[2048,768]{1,0:T(8,128)}, f32[96,768]{1,0:T(8,128)}, f32[24,3072]{1,0:T(8,128)}, f32[24,768]{1,0:T(8,128)}, f32[24,768]{1,0:T(8,128)...) custom-call(f32[1]{0:T(128)S(6)} %copy.34.scale_ref, bf16[2048,768]{1,0:T(8,128)(2,1)} %bitcast.18, ...), custom_call_target="tpu_custom_call" | custom-call | tf_op jit(solution)/shard_map/attention_backward/pallas_call | solution.py:1000
  285.1 2.2 finish.1
  287.4 6.1 %copy.35 = f32[4,512,768]{2,1,0:T(8,128)} copy(f32[4,512,768]{2,1,0:T(8,128)} %bitcast.19) | data formatting | bytes 12582912

commit v6 on v5

--- a/solution.py
+++ b/solution.py
@@ -18,57 +18,45 @@
 VECTORS = 12
 
 GATHER_TABLE = [
-    (0, 0, 0), (0, 1, 0), (0, 2, 0), (0, 0, 1), (0, 1, 1), (0, 2, 1), (0, 3, 0), (0, 0, 3), (0, 0, 4), (0, 0, 5),
-    (0, 3, 1), (0, 0, 2), (0, 1, 2), (0, 1, 3), (0, 1, 4), (0, 1, 5), (0, 0, 9), (0, 0, 10), (0, 0, 11), (0, 0, 12),
-    (0, 2, 2), (0, 2, 3), (0, 2, 4), (0, 2, 5), (0, 6, 0), (0, 0, 6), (0, 0, 7), (0, 0, 8), (0, 3, 2), (0, 3, 3),
-    (0, 3, 4), (0, 3, 5), (0, 1, 6), (0, 0, 17), (0, 0, 18), (0, 1, 7), (0, 1, 8), (0, 1, 9), (0, 1, 10), (0, 1, 11),
-    (0, 1, 12), (0, 6, 1), (0, 0, 19), (0, 0, 20), (0, 2, 6), (0, 2, 7), (0, 2, 8), (0, 2, 9), (0, 2, 10), (0, 4, 0),
-    (0, 0, 13), (0, 0, 14), (0, 0, 15), (0, 0, 16), (0, 2, 11), (0, 2, 12), (0, 3, 6), (0, 3, 9), (0, 1, 13),
-    (0, 3, 7), (0, 3, 8), (0, 3, 10), (0, 3, 11), (0, 3, 12), (0, 4, 1), (0, 1, 14), (0, 1, 15), (0, 1, 16),
-    (0, 1, 17), (0, 1, 18), (0, 5, 0), (0, 1, 19), (0, 1, 20), (0, 0, 25), (0, 0, 26), (0, 5, 1), (0, 0, 21),
-    (0, 0, 22), (0, 2, 13), (0, 2, 14), (0, 6, 2), (0, 6, 3), (0, 6, 4), (0, 6, 5), (0, 0, 23), (0, 2, 15),
-    (0, 2, 16), (0, 2, 17), (0, 2, 18), (0, 0, 24), (0, 1, 25), (0, 3, 13), (0, 3, 14), (0, 1, 26), (0, 1, 21),
-    (0, 1, 22), (0, 2, 19), (0, 2, 20), (0, 3, 15), (0, 3, 16), (0, 3, 17), (0, 3, 18), (0, 3, 19), (0, 3, 20),
-    (0, 4, 4), (0, 4, 5), (0, 1, 23), (0, 4, 2), (0, 4, 3), (0, 1, 24), (0, 0, 27), (0, 6, 8), (0, 6, 10), (0, 5, 2),
-    (0, 5, 3), (0, 5, 4), (0, 5, 5), (0, 0, 28), (0, 0, 29), (0, 2, 23), (0, 2, 24), (0, 2, 25), (0, 2, 26),
-    (0, 3, 23), (0, 3, 24), (0, 3, 25), (0, 3, 26), (0, 6, 6), (0, 6, 7), (0, 1, 27), (0, 1, 28), (0, 6, 9),
-    (0, 6, 11), (0, 4, 6), (0, 4, 7), (0, 1, 29), (1, 2, 21), (1, 2, 22), (1, 2, 28), (1, 3, 21), (1, 3, 22),
-    (1, 6, 14), (1, 4, 8), (1, 4, 10), (1, 4, 14), (1, 5, 7), (1, 5, 8), (1, 3, 28), (2, 2, 27), (2, 3, 27),
-    (2, 6, 21), (2, 4, 9), (2, 4, 11), (2, 5, 6), (2, 5, 11), (2, 5, 12), (3, 2, 29), (3, 3, 29), (3, 6, 12),
-    (3, 6, 13), (3, 4, 12), (3, 4, 13), (3, 5, 9), (3, 5, 10), (4, 6, 15), (4, 6, 16), (4, 6, 17), (4, 6, 18),
-    (4, 5, 15), (4, 5, 16), (4, 5, 19), (4, 5, 20), (5, 6, 19), (5, 6, 20), (5, 6, 22), (5, 6, 23), (5, 6, 24),
-    (5, 4, 15), (5, 4, 16), (5, 4, 17), (5, 4, 18), (5, 4, 19), (5, 4, 20), (5, 4, 21), (5, 4, 23), (5, 4, 24),
-    (6, 4, 22), (6, 5, 13), (6, 5, 14), (6, 5, 23), (6, 5, 24), (7, 6, 25), (7, 6, 26), (7, 6, 27), (7, 6, 28),
-    (7, 4, 27), (7, 4, 28), (7, 5, 17), (7, 5, 18), (7, 5, 21), (7, 5, 22), (7, 5, 25), (7, 5, 26), (8, 6, 29),
-    (8, 4, 25), (8, 4, 26), (8, 5, 27), (8, 5, 28), (9, 4, 29), (9, 5, 29),
+    (0, 0, 0), (0, 0, 1), (0, 1, 0), (0, 1, 1), (0, 0, 2), (0, 0, 3), (0, 0, 4), (0, 0, 5), (0, 2, 0), (0, 3, 0),
+    (0, 1, 2), (0, 1, 3), (0, 1, 4), (0, 1, 5), (0, 0, 6), (0, 0, 7), (0, 0, 8), (0, 0, 9), (0, 2, 1), (0, 3, 1),
+    (0, 0, 10), (0, 0, 11), (0, 0, 12), (0, 1, 6), (0, 4, 0), (0, 1, 7), (0, 1, 8), (0, 1, 9), (0, 1, 10), (0, 1, 11),
+    (0, 1, 12), (0, 0, 13), (0, 0, 14), (0, 0, 15), (0, 0, 16), (0, 4, 1), (0, 2, 2), (0, 2, 3), (0, 2, 4), (0, 2, 5),
+    (0, 0, 19), (0, 3, 2), (0, 3, 3), (0, 3, 4), (0, 3, 5), (0, 0, 17), (0, 0, 18), (0, 0, 20), (0, 0, 21),
+    (0, 0, 22), (0, 1, 13), (0, 1, 14), (0, 1, 15), (0, 1, 16), (0, 1, 17), (0, 1, 18), (0, 1, 19), (0, 1, 20),
+    (0, 0, 23), (0, 0, 24), (0, 0, 25), (0, 4, 2), (0, 4, 5), (0, 0, 26), (0, 1, 23), (0, 1, 24), (0, 2, 6),
+    (0, 2, 7), (0, 2, 8), (0, 2, 9), (0, 2, 10), (0, 2, 11), (0, 2, 12), (0, 4, 3), (0, 4, 4), (0, 3, 6), (0, 3, 7),
+    (0, 3, 8), (0, 3, 10), (0, 0, 27), (0, 1, 25), (0, 1, 26), (0, 0, 28), (0, 0, 29), (0, 4, 7), (0, 4, 8),
+    (1, 1, 21), (1, 1, 22), (1, 1, 27), (1, 1, 28), (1, 2, 15), (1, 2, 16), (1, 2, 19), (1, 2, 20), (1, 3, 9),
+    (1, 3, 11), (1, 3, 14), (2, 1, 29), (2, 2, 13), (2, 2, 14), (2, 2, 17), (2, 2, 18), (2, 4, 6), (2, 4, 11),
+    (2, 4, 12), (3, 2, 26), (3, 4, 9), (3, 4, 10), (3, 3, 12), (3, 3, 13), (4, 2, 23), (4, 2, 24), (4, 2, 25),
+    (4, 4, 15), (4, 4, 16), (4, 3, 15), (4, 3, 16), (4, 3, 17), (4, 3, 18), (5, 4, 13), (5, 4, 19), (5, 4, 20),
+    (5, 3, 21), (6, 2, 21), (6, 2, 22), (6, 2, 27), (6, 2, 28), (6, 4, 14), (6, 4, 23), (6, 4, 24), (6, 3, 19),
+    (6, 3, 20), (6, 3, 22), (6, 3, 23), (6, 3, 24), (7, 2, 29), (7, 4, 17), (7, 4, 18), (7, 4, 21), (7, 4, 22),
+    (7, 4, 25), (7, 4, 26), (8, 4, 27), (8, 4, 28), (8, 3, 25), (8, 3, 26), (8, 3, 27), (8, 3, 28), (9, 4, 29),
+    (9, 3, 29),
 ]
 SCATTER_TABLE = [
-    (0, 0, 0), (0, 1, 0), (1, 0, 1), (1, 0, 2), (2, 0, 3), (2, 0, 4), (2, 0, 5), (2, 1, 1), (2, 2, 0), (3, 0, 6),
-    (3, 0, 7), (3, 1, 2), (3, 1, 3), (3, 1, 4), (3, 2, 1), (3, 2, 2), (3, 2, 3), (3, 2, 4), (4, 3, 0), (4, 0, 8),
-    (4, 0, 9), (4, 0, 10), (4, 0, 11), (4, 0, 12), (5, 3, 1), (5, 3, 2), (5, 3, 3), (5, 3, 4), (5, 0, 13), (5, 0, 14),
-    (5, 1, 5), (6, 1, 6), (6, 1, 7), (6, 1, 8), (7, 0, 15), (7, 0, 16), (7, 0, 17), (7, 0, 18), (7, 0, 20), (8, 4, 0),
-    (8, 0, 21), (8, 1, 9), (8, 1, 10), (8, 1, 11), (8, 1, 12), (8, 2, 5), (8, 2, 6), (8, 2, 7), (8, 2, 8), (8, 2, 9),
-    (9, 4, 1), (9, 4, 2), (9, 4, 3), (9, 4, 4), (9, 3, 5), (9, 3, 6), (9, 3, 7), (9, 3, 8), (9, 0, 19), (9, 0, 22),
-    (9, 0, 23), (9, 2, 10), (9, 2, 11), (9, 2, 12), (9, 3, 9), (9, 0, 24), (10, 3, 10), (10, 3, 11), (10, 3, 12),
-    (10, 1, 13), (10, 1, 14), (11, 0, 25), (11, 0, 26), (11, 1, 15), (11, 1, 16), (11, 1, 17), (11, 1, 18),
-    (11, 1, 19), (11, 2, 13), (11, 2, 14), (12, 5, 0), (12, 6, 0), (12, 4, 5), (12, 4, 6), (12, 4, 7), (12, 4, 8),
-    (12, 4, 9), (12, 4, 10), (12, 4, 11), (12, 4, 12), (12, 3, 13), (12, 3, 14), (12, 3, 15), (12, 3, 16),
-    (12, 3, 17), (12, 3, 18), (12, 3, 19), (12, 0, 27), (12, 1, 20), (12, 1, 21), (12, 1, 22), (12, 2, 15),
-    (12, 2, 16), (12, 2, 17), (12, 2, 18), (12, 2, 19), (12, 2, 20), (13, 5, 1), (13, 5, 2), (13, 5, 3), (13, 5, 4),
-    (13, 6, 1), (13, 6, 2), (13, 6, 3), (13, 6, 4), (13, 4, 13), (13, 4, 14), (13, 4, 15), (13, 4, 16), (13, 4, 17),
-    (13, 4, 18), (13, 4, 19), (13, 3, 20), (13, 3, 21), (14, 5, 5), (14, 5, 6), (14, 5, 7), (14, 4, 20), (14, 3, 22),
-    (14, 1, 23), (14, 2, 21), (14, 2, 22), (14, 5, 8), (15, 5, 9), (15, 5, 10), (15, 5, 11), (15, 5, 12), (15, 6, 5),
-    (15, 6, 6), (15, 6, 7), (15, 6, 8), (15, 6, 9), (15, 6, 10), (15, 6, 11), (15, 6, 15), (15, 6, 16), (15, 6, 17),
-    (15, 6, 18), (15, 6, 19), (15, 6, 20), (15, 6, 21), (15, 4, 21), (15, 4, 22), (15, 3, 23), (15, 3, 24),
-    (15, 1, 24), (15, 2, 23), (15, 5, 13), (15, 5, 14), (15, 5, 15), (15, 5, 16), (16, 5, 17), (16, 5, 18),
-    (16, 5, 19), (16, 6, 12), (16, 6, 13), (16, 6, 14), (16, 6, 22), (16, 6, 23), (16, 6, 24), (16, 4, 23),
-    (16, 4, 24), (16, 3, 25), (16, 3, 26), (16, 1, 25), (16, 1, 26), (16, 2, 24), (16, 2, 25), (16, 2, 26),
-    (16, 5, 20), (16, 5, 21), (16, 3, 27), (16, 6, 25), (16, 1, 27), (16, 2, 27), (16, 6, 26), (16, 5, 22),
-    (16, 6, 29), (16, 6, 30), (16, 4, 25), (16, 4, 26), (16, 5, 23), (16, 6, 27), (16, 6, 28), (16, 4, 27),
-    (16, 5, 24), (16, 6, 31), (16, 6, 32), (16, 5, 25), (16, 5, 26), (16, 6, 33), (16, 5, 27),
+    (0, 1, 0), (1, 1, 1), (1, 0, 0), (2, 1, 2), (2, 1, 3), (2, 1, 4), (3, 1, 5), (3, 1, 6), (3, 1, 7), (3, 1, 8),
+    (3, 0, 1), (3, 0, 2), (3, 0, 3), (3, 0, 4), (3, 1, 9), (3, 1, 10), (4, 2, 0), (4, 1, 11), (4, 1, 12), (4, 1, 15),
+    (4, 1, 16), (4, 1, 17), (4, 1, 18), (5, 2, 1), (5, 2, 2), (5, 2, 3), (5, 2, 4), (5, 1, 13), (5, 1, 19),
+    (5, 1, 20), (5, 1, 21), (5, 0, 5), (5, 0, 6), (6, 1, 14), (6, 1, 25), (6, 0, 7), (6, 0, 8), (6, 0, 9), (6, 0, 10),
+    (7, 1, 22), (7, 1, 23), (7, 1, 26), (7, 0, 11), (7, 0, 15), (7, 0, 16), (7, 0, 17), (7, 0, 18), (8, 3, 0),
+    (8, 2, 5), (8, 2, 6), (8, 2, 7), (8, 2, 8), (8, 2, 9), (8, 2, 10), (8, 2, 11), (8, 2, 12), (8, 1, 24), (8, 1, 27),
+    (8, 1, 28), (8, 1, 29), (8, 0, 12), (8, 0, 19), (8, 0, 20), (8, 0, 21), (9, 3, 1), (9, 3, 2), (9, 3, 3),
+    (9, 3, 4), (9, 2, 13), (9, 2, 14), (9, 2, 15), (9, 2, 16), (9, 2, 17), (9, 2, 18), (9, 2, 19), (9, 1, 30),
+    (9, 0, 13), (9, 0, 14), (10, 3, 5), (10, 3, 6), (10, 3, 7), (10, 3, 8), (10, 3, 9), (10, 3, 10), (10, 3, 11),
+    (10, 1, 31), (10, 1, 32), (10, 0, 22), (10, 0, 25), (10, 3, 12), (11, 3, 13), (11, 3, 14), (11, 3, 15),
+    (11, 3, 16), (11, 3, 17), (11, 3, 18), (11, 3, 19), (11, 2, 20), (11, 1, 33), (11, 0, 23), (11, 0, 24),
+    (11, 0, 26), (12, 4, 0), (12, 3, 20), (12, 3, 21), (12, 3, 22), (12, 2, 21), (12, 2, 22), (12, 2, 23),
+    (12, 0, 27), (12, 0, 28), (12, 0, 29), (12, 0, 30), (14, 4, 1), (14, 4, 2), (15, 4, 3), (15, 4, 4), (15, 3, 23),
+    (15, 2, 25), (16, 3, 24), (16, 2, 24), (16, 2, 26), (17, 4, 5), (18, 4, 6), (18, 4, 7), (18, 2, 27), (18, 0, 31),
+    (18, 0, 32), (19, 4, 8), (19, 4, 9), (19, 3, 25), (19, 3, 26), (20, 4, 10), (20, 4, 11), (20, 0, 33), (21, 4, 12),
+    (21, 4, 13), (21, 4, 14), (21, 3, 27), (22, 4, 15), (22, 4, 16), (22, 4, 17), (22, 4, 18), (23, 4, 19),
+    (24, 4, 20), (24, 4, 21), (24, 4, 22), (24, 4, 23), (24, 4, 24), (24, 4, 25), (24, 4, 26), (24, 4, 27),
 ]
-GATHER_LINE_FIRST = [False, False, False, False, True, False, True]
-SCATTER_LINE_LAST = [True, True, True, True, True, True, False]
+GATHER_LINE_FIRST = [False, False, False, True, False]
+SCATTER_LINE_LAST = [False, False, True, True, True]
 GATHER_SLOTS, SCATTER_SLOTS = 1, 1
 
 
@@ -555,11 +543,11 @@
         vector_refs, refs = refs[: BIN + 1], refs[BIN + 1 :]
         wqkv_ref, wo_ref, win_ref, wd_ref = refs[:4]
         qkv_ref, att_ref, lse_ref, vec_ref, bin_ref = refs[4:9]
-        fulls = refs[9:16]
-        mask_ref, w_ref, small_ref, load_sem, shard_ref, square_ref = refs[16:22]
-        sems = refs[22:]
+        fulls = refs[9:14]
+        mask_ref, w_ref, small_ref, load_sem, shard_ref, square_ref = refs[14:20]
+        sems = refs[20:]
     else:
-        fulls = refs[:4]
+        small, *groups = [ref.at[:, pl.ds(0, size)] for ref, size in zip(refs[:4], (128, 768, 768, 768))]
         qkv_ref, att_ref, lse_ref, vec_ref, bin_ref = refs[4:9]
         mask_ref, w_ref, small_ref, load_sem = refs[9:]
     step = pl.program_id(0)
@@ -571,13 +559,16 @@
     last = per * steps
     plan = {}
     if near:
+        groups = [fulls[0].at[:, pl.ds(0, width)], *fulls[1:GROUPS]]
+        small = fulls[0].at[:, pl.ds(width, 128)]
         place = Place()
-        windows = [[shard_ref]]
+        windows = []
         for group in range(GROUPS):
             windows.append([wqkv_ref.at[:, pl.ds(third * width + group * part, part)] for third in range(3)])
-        windows += [[wo_ref], [win_ref], [wd_ref]]
+        windows[0].append(shard_ref)
+        windows += [[win_ref, wo_ref], [wd_ref]]
         jobs = [
-            Gather(place, windows[i], fulls[i], sems[5 * i : 5 * i + 5], GATHER_LINE_FIRST[i]) for i in range(7)
+            Gather(place, w, fulls[i], sems[5 * i : 5 * i + 5], GATHER_LINE_FIRST[i]) for i, w in enumerate(windows)
         ]
         plan = planned(GATHER_TABLE, jobs)
 
@@ -594,7 +585,7 @@
             shard_ref[:, 128:] = jnp.zeros((shard_ref.shape[0], 128), BF16)
             place.meet()
             run_now(plan, 0)
-        copy = pltpu.make_async_copy(fulls[0].at[:, pl.ds(0, 128)], small_ref, load_sem.at[0])
+        copy = pltpu.make_async_copy(small, small_ref, load_sem.at[0])
         copy.start()
         copy.wait()
         vec_ref[...] = jnp.transpose(small_ref[...].astype(F32))[:16]
@@ -610,7 +601,7 @@
 
         @pl.when(step == group * SEQS)
         def _():
-            copy = pltpu.make_async_copy(fulls[1 + group], w_ref, load_sem.at[1])
+            copy = pltpu.make_async_copy(groups[group], w_ref, load_sem.at[1])
             copy.start()
             copy.wait()
 
@@ -687,10 +678,11 @@
         in_specs += [pl.BlockSpec(v.shape, lambda i: (0,)) for v in vectors]
         in_specs += [pl.BlockSpec(w.shape, lambda i: (0, 0)) for w in (w_qkv, w_out, w_in, w_down)]
         mine = w_qkv.shape[0]
-        fulls = [(mine, 256)] + [(mine, width)] * GROUPS + [w.shape for w in (w_out, w_in, w_down)]
-        out_specs += anywhere(7)
+        fulls = [(mine, width + 256)] + [(mine, width)] * (GROUPS - 1)
+        fulls += [(mine, w_in.shape[1] + w_out.shape[1]), w_down.shape]
+        out_specs += anywhere(5)
         out_shape += [shape((32 * r, c), BF16) for r, c in fulls]
-        scratch += [pltpu.VMEM((mine, 256), BF16), pltpu.VMEM((128, 128), F32)] + GATHER_SEMS * 7
+        scratch += [pltpu.VMEM((mine, 256), BF16), pltpu.VMEM((128, 128), F32)] + GATHER_SEMS * 5
         remotely = dict(collective_id=0, has_side_effects=True)
     else:
         in_specs += anywhere(4)
@@ -726,7 +718,7 @@
 
 def middle_kernel(
     mine, scale_ref, x_ref, att_ref, cot_ref, wo_ref, win_ref, wd_ref, vec_ref, bin_ref,
-    out_ref, sum_ref, datt_ref, gwo_ref, gwin_ref, gwd_ref, gvec_ref,
+    out_ref, sum_ref, datt_ref, gboth_ref, gwd_ref, gvec_ref,
     gbin_ref, acc_wo, acc_win, acc_wd, act_ref, slope_ref,
 ):
     step = pl.program_id(0)
@@ -787,10 +779,13 @@
         weight = scale_ref[0]
 
         def cast(index, carry):
-            for ref, acc in ((gwo_ref, acc_wo), (gwin_ref, acc_win), (gwd_ref, acc_wd)):
+            here = pl.ds(0, hidden)
+            for ref, acc, cols in (
+                (gboth_ref, acc_win, here), (gboth_ref, acc_wo, pl.ds(hidden, width)), (gwd_ref, acc_wd, pl.ds(0, width)),
+            ):
                 size = acc.shape[0] // 24
                 some = pl.ds(pl.multiple_of(index * size, size), size)
-                ref[some, :] = (acc[some, :] * weight).astype(BF16)
+                ref[some, cols] = (acc[some, :] * weight).astype(BF16)
             return carry
 
         lax.fori_loop(0, 24, cast, 0)
@@ -804,8 +799,9 @@
 
 def middle(scale, rows, att, cot, w_out, w_in, w_down, vectors, b_in, mine):
     count, width = rows.shape
-    hidden = w_in.shape[1]
+    hidden = w_down.shape[0]
     tile = 256
+    last = w_out.shape[1] // width - 1
     whole = lambda shape: pl.BlockSpec(shape, lambda i: (0,) * len(shape), pipeline_mode=pl.Buffered(1))
     row = pl.BlockSpec((tile, width), lambda i: (i, 0))
     shape = jax.ShapeDtypeStruct
@@ -814,22 +810,22 @@
         name="middle",
         grid=(count // tile,),
         in_specs=[pl.BlockSpec(memory_space=pltpu.SMEM), row, row, row]
-        + [whole(a.shape) for a in (w_out, w_in, w_down, vectors, b_in)],
+        + [pl.BlockSpec((width, width), lambda i: (0, last), pipeline_mode=pl.Buffered(1)), whole((width, hidden))]
+        + [whole(a.shape) for a in (w_down, vectors, b_in)],
         out_specs=[row, row, row]
-        + [whole(s) for s in (w_out.shape, w_in.shape, w_down.shape, (16, width))],
+        + [whole(s) for s in ((width, hidden + width), w_down.shape, (16, width))],
         out_shape=[
             shape((count, width), BF16),
             shape((count, width), F32),
             shape((count, width), BF16),
-            shape(w_out.shape, BF16),
-            shape(w_in.shape, BF16),
+            shape((width, hidden + width), BF16),
             shape(w_down.shape, BF16),
             shape((16, width), F32),
         ],
         scratch_shapes=[
             pltpu.VMEM((1, hidden), F32),
-            pltpu.VMEM(w_out.shape, F32),
-            pltpu.VMEM(w_in.shape, F32),
+            pltpu.VMEM((width, width), F32),
+            pltpu.VMEM((width, hidden), F32),
             pltpu.VMEM(w_down.shape, F32),
             pltpu.VMEM((tile, hidden), BF16),
             pltpu.VMEM((tile, hidden), F32),
@@ -847,25 +843,23 @@
     half = width // HEADS
     steps = GROUPS * SEQS
     per = SCATTER_SLOTS
-    last = per * (steps + SEQS)
+    last = per * steps + GROUPS * SEQS
     plan = {}
     if near:
-        given, gx_ref, sums, refs = refs[:3], refs[3], refs[4:11], refs[11:]
+        given, gx_ref, sums, refs = refs[:2], refs[2], refs[3:8], refs[8:]
         xt_ref, dqkv_ref, gvec_ref, mask_ref = refs[:4]
-        terms = refs[4 : 5 + GROUPS]
-        refs = refs[5 + GROUPS :]
-        each = len(refs) // 7
+        terms = refs[4 : 4 + GROUPS]
+        refs = refs[4 + GROUPS :]
+        each = len(refs) // 5
         place = Place()
         jobs = [
             Scatter(place, t, sums[i], refs[each * i : each * (i + 1)], SCATTER_LINE_LAST[i])
             for i, t in enumerate(given + terms)
         ]
         plan = planned(SCATTER_TABLE, jobs)
-        put = lambda ref, value: ref.__setitem__(..., value.reshape(ref.shape))
     else:
-        gx_ref, terms, refs = refs[0], refs[1 : 2 + GROUPS], refs[2 + GROUPS :]
+        gx_ref, terms, refs = refs[0], refs[1 : 1 + GROUPS], refs[1 + GROUPS :]
         xt_ref, dqkv_ref, gvec_ref, mask_ref = refs
-        put = lambda ref, value: ref.__setitem__(..., value)
 
     @pl.when(step == 0)
     def _():
@@ -937,18 +931,24 @@
         gvec_ref[:2] = gvec_ref[:2] * scale_ref[0]
         gvec_ref[2:VECTORS] = rest_ref[2:VECTORS]
         packed = jnp.transpose(gvec_ref[...]).astype(BF16)
-        put(terms[GROUPS], jnp.concatenate([packed, jnp.zeros_like(packed)], 1))
+        for start, value in ((width, packed), (width + 128, jnp.zeros_like(packed))):
+            if near:
+                blocks = value.reshape(*terms[-1].shape[:2], 128)
+                terms[-1][:, :, start : start + 128] = blocks
+            else:
+                terms[-1][:, start : start + 128] = value
 
     @pl.when(step >= steps)
     def _():
-        if near:
-            at_slot(per * step, {s: e for s, e in plan.items() if s % per == 0 and per * steps <= s < last})
         grad_x = sum_ref[...]
         for group in range(GROUPS):
+            if near:
+                here = {s - per * steps: e for s, e in plan.items() if per * steps <= s < last}
+                at_slot(GROUPS * (step - steps) + group, {s: e for s, e in here.items() if s % GROUPS == group})
+                grad_x = grad_x if group == 0 else gx_ref[...]
             grad_x = grad_x + dot_right(dqkv_ref[group, pl.ds(at, length), :], w_refs[group][...])
-        gx_ref[...] = grad_x
-        if near and per > 1:
-            at_slot(per * step, {s - 1: e for s, e in plan.items() if s % per and per * steps < s < last})
+            if near or group == GROUPS - 1:
+                gx_ref[...] = grad_x
 
     if near:
 
@@ -977,7 +977,7 @@
         tokens,
         late,
         whole(rest.shape),
-    ] + [whole(w.shape) for w in w_groups]
+    ] + [whole((width, width))] * GROUPS
     scratch = [
         pltpu.VMEM((width, count), BF16),
         pltpu.VMEM((GROUPS, count, width), BF16),
@@ -987,8 +987,8 @@
     out_shape = [shape((count, width), F32)]
     remotely = {}
     if near:
-        in_specs += [pl.BlockSpec(memory_space=pl.ANY)] * 3
-        made = [(16, width // 16, width)] * GROUPS + [(16, width // 16, 256)]
+        in_specs += [pl.BlockSpec(memory_space=pl.ANY)] * 2
+        made = [(16, width // 16, width)] * (GROUPS - 1) + [(16, width // 16, width + 256)]
         scratch += [pltpu.VMEM(m, BF16) for m in made]
         every_shape = [g.shape for g in given] + made
         out_shape += [shape((s[1] // 2, s[2]), F32) for s in every_shape]
@@ -996,7 +996,7 @@
             scratch += scatter_buffers(s[1], s[2], line_last)
         remotely = dict(collective_id=1, has_side_effects=True)
     else:
-        out_shape += [shape((width, width), BF16)] * GROUPS + [shape((width, 256), BF16)]
+        out_shape += [shape((width, width), BF16)] * (GROUPS - 1) + [shape((width, width + 256), BF16)]
     return pl.pallas_call(
         partial(backward_kernel, near),
         name="attention_backward",
@@ -1015,8 +1015,8 @@
     return jnp.concatenate(cut, 1)
 
 
-def finish_kernel(wd_ref, win_ref, wo_ref, *refs):
-    parts, small_ref, outs = refs[:GROUPS], refs[GROUPS], refs[GROUPS + 1 :]
+def finish_kernel(wd_ref, both_ref, *refs):
+    parts, outs = refs[:GROUPS], refs[GROUPS:]
     qkv_ref, o_wd, o_win, o_wo = outs[:4]
     width = parts[0].shape[1]
     part = width // GROUPS
@@ -1025,10 +1025,11 @@
             cols = slice(third * width + group * part, third * width + (group + 1) * part)
             qkv_ref[:, cols] = parts[group][:, third * part : (third + 1) * part]
     o_wd[...] = wd_ref[...]
-    o_win[...] = win_ref[...]
-    o_wo[...] = wo_ref[...]
+    o_win[...] = both_ref[:, : o_win.shape[1]]
+    o_wo[...] = both_ref[:, o_win.shape[1] :]
+    small_ref = parts[-1].at[:, pl.ds(width, 128)]
     mine = small_ref.shape[0]
-    square = jnp.concatenate([small_ref[:, :128], jnp.zeros((128 - mine, 128), F32)], 0)
+    square = jnp.concatenate([small_ref[...], jnp.zeros((128 - mine, 128), F32)], 0)
     vectors = jnp.transpose(square)
     for row in range(BIN):
         outs[4 + row][...] = vectors[row : row + 1, :mine]
@@ -1036,17 +1037,17 @@
 
 
 def finish(sums):
-    wd, win, wo, *rest = sums
-    mine, width = rest[0].shape
+    wd, both, *parts = sums
+    mine, width = parts[0].shape
     shape = jax.ShapeDtypeStruct
     vmem = pl.BlockSpec(memory_space=pltpu.VMEM)
     outs = pl.pallas_call(
         finish_kernel,
         name="finish",
-        in_specs=[vmem] * 7,
+        in_specs=[vmem] * (2 + GROUPS),
         out_specs=[vmem] * (5 + BIN),
         out_shape=[shape((mine, 3 * width), F32)]
-        + [shape(a.shape, F32) for a in (wd, win, wo)]
+        + [shape(wd.shape, F32), shape((mine, both.shape[1] - width), F32), shape((mine, width), F32)]
         + [shape((1, mine), F32)] * BIN
         + [shape((1, (VECTORS - BIN) * mine), F32)],
     )(*sums)
@@ -1065,30 +1066,33 @@
     rows = hidden_in.reshape(-1, width)
     if near:
         weights = [*vectors, w_qkv, w_out, w_in, w_down]
-        qkv, att, lse, vectors, bin_full, _, *full = attention_forward(True, rows, segment_ids, pad_mask, weights)
+        qkv, att, lse, vectors, bin_full, *full = attention_forward(True, rows, segment_ids, pad_mask, weights)
     else:
         packed = jnp.transpose(jnp.concatenate(vectors).reshape(VECTORS, mine))
         packed = jnp.pad(packed, ((0, 0), (0, 256 - VECTORS)))
         cut = w_qkv.reshape(mine, 3, GROUPS, part)
         groups = [cut[:, :, g].reshape(mine, width) for g in range(GROUPS)]
-        full = [lax.all_gather(w, AXES, axis=0, tiled=True) for w in (packed, *groups, w_out, w_in, w_down)]
+        full = [lax.all_gather(w, AXES, axis=0, tiled=True) for w in (packed, *groups, w_in, w_down, w_out)]
         qkv, att, lse, vectors, bin_full = attention_forward(False, rows, segment_ids, pad_mask, full[:4])
         full = full[1:]
-    *w_groups, wo_full, win_full, wd_full = full
-    hidden_out, grad_sum, datt, g_wo, g_win, g_wd, g_rest = middle(
+    *w_groups, win_full, wd_full = full[:5]
+    wo_full = win_full if near else full[5]
+    hidden_out, grad_sum, datt, g_both, g_wd, g_rest = middle(
         task_weight, rows, att, out_grad.reshape(-1, width), wo_full, win_full, wd_full, vectors, bin_full, mine
     )
-    given = [g.reshape(16, -1, g.shape[1]) for g in (g_wd, g_win, g_wo)] if near else []
+    given = [g.reshape(16, -1, g.shape[1]) for g in (g_wd, g_both)] if near else []
     grad_x, *terms = attention_backward(
         near, task_weight, rows, qkv, datt, lse, segment_ids, pad_mask, grad_sum, g_rest, w_groups, given
     )
     if near:
         s_qkv, (s_wd, s_win, s_wo), s_vec = finish(terms)
     else:
-        s_wd, s_win, s_wo, *parts, small = [
-            lax.psum_scatter(t, AXES, scatter_dimension=0, tiled=True).astype(F32) for t in (g_wd, g_win, g_wo, *terms)
+        s_wd, both, *parts = [
+            lax.psum_scatter(t, AXES, scatter_dimension=0, tiled=True).astype(F32) for t in (g_wd, g_both, *terms)
         ]
+        s_win, s_wo = both[:, :-width], both[:, -width:]
         s_qkv = join_groups(parts, width)
+        small = parts[-1][:, width:]
         s_vec = [small[:, row] for row in range(BIN)] + [jnp.transpose(small[:, BIN:VECTORS]).reshape(-1)]
     return (
         hidden_out.reshape(hidden_in.shape),

time: 294 us -> 290 us (0.986)
  Pallas kernels: 286 us -> 282 us
    pallas_call x1, Pallas kernels: 102 us -> 98 us  [attention_backward(): pl.pallas_call(partial(backward_kernel, near), name='attention_backward',...]
where the time goes in v6:
time: 290 us
  Pallas kernels  282 us (97%)
  local copies, waits for them, and re-layouts  6.09 us (2%)
    pallas_call x1, Pallas kernels, attention_backward(): pl.pallas_call(partial(backward_kernel, near), name='attention_backward',...  98 us
    pallas_call x1, Pallas kernels, middle(): pl.pallas_call(partial(middle_kernel, mine), name='middle', grid=(count /...  94.4 us
    pallas_call x1, Pallas kernels, attention_forward(): pl.pallas_call(partial(forward_kernel, near, lax.axis_size(AXES)), name='...  87.9 us
    unnamed x1, local copies, waits for them, and re-layouts  6.09 us

profile of v6, /device:TPU:0, one launch (start us, length us, event | category | flops | bytes accessed | tf_op | source)
XLA Modules:
  0.0 289.8 jit_solution(2102627979509654303)
XLA Ops:
  1.3 87.9 %attention_forward.1 = (bf16[2048,2304]{1,0:T(8,128)(2,1)}, bf16[2048,768]{1,0:T(8,128)(2,1)}, f32[12,8,512]{2,1,0:T(8,128)}, f32[16,768]{1,0:T(8,128)}, f32[1,3...) custom-call(bf16[2048,768]{1,0:T(8,128)(2,1)} %bitcast.15, ...), custom_call_target="tpu_custom_call" | custom-call | tf_op jit(solution)/shard_map/attention_forward/pallas_call | solution.py:689
  89.2 94.4 %middle.1 = (bf16[2048,768]{1,0:T(8,128)(2,1)}, f32[2048,768]{1,0:T(8,128)}, bf16[2048,768]{1,0:T(8,128)(2,1)}, bf16[768,3840]{1,0:T(8,128)(2,1)}, bf16[3072,768]{1,0:T(8,128)(2,1)}, /*index=5*/f32[16,768]{1,0:T(8,128)}) custom-call(f32[1]{0:T(128)S(6)} %copy.34.scale_ref, bf16[2048,768]{1,0:T(8,128)(2,1)} %bitcast.16, ...), custom_call_target="tpu_custom_call" | custom-call | flops 65000001536 | bytes 60000000 | tf_op jit(solution)/shard_map/middle/pallas_call | solution.py:808
  183.6 98.0 %attention_backward.1 = (f32[2048,768]{1,0:T(8,128)}, f32[96,768]{1,0:T(8,128)}, f32[24,3840]{1,0:T(8,128)}, f32[24,768]{1,0:T(8,128)}, f32[24,768]{1,0:T(8,128)}, /*index=5*/f32[24,1024]{1,0:T(8,128)}) custom-call(f32[1]{0:T(128)S(6)} %copy.34.scale_ref, bf16[2048,768]{1,0:T(8,128)(2,1)} %bitcast.17, bf16[2048,2304]{1,0:T(8,128)(2,1)} %get-tuple-element.56.qkv_ref, ...), custom_call_target="tpu_custom_call" | custom-call | tf_op jit(solution)/shard_map/attention_backward/pallas_call | solution.py:1000
  281.5 2.2 finish.1
  283.8 6.1 %copy.35 = f32[4,512,768]{2,1,0:T(8,128)} copy(f32[4,512,768]{2,1,0:T(8,128)} %bitcast.18) | data formatting | bytes 12582912

commit v7 on v6

--- a/solution.py
+++ b/solution.py
@@ -18,23 +18,23 @@
 VECTORS = 12
 
 GATHER_TABLE = [
-    (0, 0, 0), (0, 0, 1), (0, 1, 0), (0, 1, 1), (0, 0, 2), (0, 0, 3), (0, 0, 4), (0, 0, 5), (0, 2, 0), (0, 3, 0),
-    (0, 1, 2), (0, 1, 3), (0, 1, 4), (0, 1, 5), (0, 0, 6), (0, 0, 7), (0, 0, 8), (0, 0, 9), (0, 2, 1), (0, 3, 1),
-    (0, 0, 10), (0, 0, 11), (0, 0, 12), (0, 1, 6), (0, 4, 0), (0, 1, 7), (0, 1, 8), (0, 1, 9), (0, 1, 10), (0, 1, 11),
-    (0, 1, 12), (0, 0, 13), (0, 0, 14), (0, 0, 15), (0, 0, 16), (0, 4, 1), (0, 2, 2), (0, 2, 3), (0, 2, 4), (0, 2, 5),
-    (0, 0, 19), (0, 3, 2), (0, 3, 3), (0, 3, 4), (0, 3, 5), (0, 0, 17), (0, 0, 18), (0, 0, 20), (0, 0, 21),
-    (0, 0, 22), (0, 1, 13), (0, 1, 14), (0, 1, 15), (0, 1, 16), (0, 1, 17), (0, 1, 18), (0, 1, 19), (0, 1, 20),
-    (0, 0, 23), (0, 0, 24), (0, 0, 25), (0, 4, 2), (0, 4, 5), (0, 0, 26), (0, 1, 23), (0, 1, 24), (0, 2, 6),
-    (0, 2, 7), (0, 2, 8), (0, 2, 9), (0, 2, 10), (0, 2, 11), (0, 2, 12), (0, 4, 3), (0, 4, 4), (0, 3, 6), (0, 3, 7),
-    (0, 3, 8), (0, 3, 10), (0, 0, 27), (0, 1, 25), (0, 1, 26), (0, 0, 28), (0, 0, 29), (0, 4, 7), (0, 4, 8),
-    (1, 1, 21), (1, 1, 22), (1, 1, 27), (1, 1, 28), (1, 2, 15), (1, 2, 16), (1, 2, 19), (1, 2, 20), (1, 3, 9),
-    (1, 3, 11), (1, 3, 14), (2, 1, 29), (2, 2, 13), (2, 2, 14), (2, 2, 17), (2, 2, 18), (2, 4, 6), (2, 4, 11),
-    (2, 4, 12), (3, 2, 26), (3, 4, 9), (3, 4, 10), (3, 3, 12), (3, 3, 13), (4, 2, 23), (4, 2, 24), (4, 2, 25),
-    (4, 4, 15), (4, 4, 16), (4, 3, 15), (4, 3, 16), (4, 3, 17), (4, 3, 18), (5, 4, 13), (5, 4, 19), (5, 4, 20),
-    (5, 3, 21), (6, 2, 21), (6, 2, 22), (6, 2, 27), (6, 2, 28), (6, 4, 14), (6, 4, 23), (6, 4, 24), (6, 3, 19),
-    (6, 3, 20), (6, 3, 22), (6, 3, 23), (6, 3, 24), (7, 2, 29), (7, 4, 17), (7, 4, 18), (7, 4, 21), (7, 4, 22),
-    (7, 4, 25), (7, 4, 26), (8, 4, 27), (8, 4, 28), (8, 3, 25), (8, 3, 26), (8, 3, 27), (8, 3, 28), (9, 4, 29),
-    (9, 3, 29),
+    (0, 0, 0), (0, 1, 0), (0, 2, 0), (0, 0, 1), (0, 1, 1), (0, 2, 1), (0, 0, 2), (0, 0, 3), (0, 0, 4), (0, 0, 5),
+    (0, 1, 2), (0, 1, 3), (0, 1, 4), (0, 1, 5), (0, 2, 2), (0, 2, 3), (0, 2, 4), (0, 2, 5), (0, 0, 6), (0, 0, 7),
+    (0, 0, 8), (0, 0, 9), (0, 0, 10), (0, 0, 11), (0, 0, 12), (0, 1, 6), (0, 1, 9), (0, 1, 7), (0, 1, 8), (0, 1, 10),
+    (0, 1, 11), (0, 1, 12), (0, 2, 6), (0, 2, 7), (0, 2, 8), (0, 2, 9), (0, 2, 10), (0, 4, 0), (0, 0, 13), (0, 0, 14),
+    (0, 2, 11), (0, 2, 12), (0, 0, 15), (0, 0, 16), (0, 0, 17), (0, 0, 18), (0, 1, 13), (0, 1, 14), (0, 4, 1),
+    (0, 0, 19), (0, 0, 20), (0, 1, 15), (0, 1, 16), (0, 1, 17), (0, 1, 18), (0, 2, 13), (0, 2, 14), (0, 3, 0),
+    (0, 0, 21), (0, 0, 22), (0, 1, 19), (0, 1, 20), (0, 2, 17), (0, 2, 18), (0, 2, 15), (0, 2, 16), (0, 0, 23),
+    (0, 2, 19), (0, 2, 20), (0, 3, 1), (0, 0, 24), (0, 0, 25), (0, 4, 2), (0, 4, 5), (0, 0, 26), (0, 0, 27),
+    (0, 1, 21), (0, 1, 22), (0, 1, 23), (0, 1, 24), (0, 1, 25), (0, 1, 26), (0, 2, 21), (0, 2, 22), (0, 2, 26),
+    (0, 4, 3), (0, 4, 4), (0, 0, 28), (0, 2, 23), (0, 2, 24), (0, 2, 25), (0, 3, 2), (0, 3, 3), (0, 3, 4), (0, 3, 5),
+    (0, 0, 29), (1, 1, 27), (1, 1, 28), (1, 4, 6), (1, 4, 7), (1, 4, 8), (2, 1, 29), (2, 2, 27), (2, 2, 28),
+    (2, 4, 9), (2, 4, 10), (2, 4, 11), (2, 4, 12), (3, 2, 29), (3, 3, 6), (3, 3, 7), (3, 3, 8), (3, 3, 10),
+    (4, 4, 15), (4, 4, 16), (4, 3, 9), (4, 3, 11), (4, 3, 14), (5, 4, 13), (5, 4, 14), (5, 4, 19), (5, 4, 20),
+    (6, 4, 17), (6, 4, 18), (6, 3, 12), (6, 3, 13), (7, 4, 23), (7, 4, 24), (7, 4, 25), (7, 4, 26), (7, 3, 15),
+    (7, 3, 16), (7, 3, 17), (7, 3, 18), (7, 3, 21), (8, 4, 21), (8, 4, 22), (8, 3, 19), (8, 3, 20), (8, 3, 22),
+    (8, 3, 23), (8, 3, 24), (9, 4, 27), (9, 4, 28), (9, 3, 25), (9, 3, 26), (10, 4, 29), (10, 3, 27), (10, 3, 28),
+    (11, 3, 29),
 ]
 SCATTER_TABLE = [
     (0, 1, 0), (1, 1, 1), (1, 0, 0), (2, 1, 2), (2, 1, 3), (2, 1, 4), (3, 1, 5), (3, 1, 6), (3, 1, 7), (3, 1, 8),

time: 290 us -> 285 us (0.983)
  Pallas kernels: 282 us -> 277 us
    pallas_call x1, Pallas kernels: 87.9 us -> 81.5 us  [attention_forward(): pl.pallas_call(partial(forward_kernel, near, lax.axis_size(AXES)), name='...]
where the time goes in v7:
time: 285 us; the launch traced here: 284 us
  Pallas kernels  277 us (97%)
  local copies, waits for them, and re-layouts  6.09 us (2%)
    pallas_call x1, Pallas kernels, attention_backward(): pl.pallas_call(partial(backward_kernel, near), name='attention_backward',...  99 us
    pallas_call x1, Pallas kernels, middle(): pl.pallas_call(partial(middle_kernel, mine), name='middle', grid=(count /...  94.4 us
    pallas_call x1, Pallas kernels, attention_forward(): pl.pallas_call(partial(forward_kernel, near, lax.axis_size(AXES)), name='...  81.5 us
    unnamed x1, local copies, waits for them, and re-layouts  6.09 us

profile of v7, /device:TPU:0, one launch (start us, length us, event | category | flops | bytes accessed | tf_op | source)
XLA Modules:
  0.0 284.5 jit_solution(9796790518451069353)
XLA Ops:
  1.3 81.5 %attention_forward.1 = (bf16[2048,2304]{1,0:T(8,128)(2,1)}, bf16[2048,768]{1,0:T(8,128)(2,1)}, f32[12,8,512]{2,1,0:T(8,128)}, f32[16,768]{1,0:T(8,128)}, f32[1,3...) custom-call(bf16[2048,768]{1,0:T(8,128)(2,1)} %bitcast.15, ...), custom_call_target="tpu_custom_call" | custom-call | tf_op jit(solution)/shard_map/attention_forward/pallas_call | solution.py:689
  82.8 94.4 %middle.1 = (bf16[2048,768]{1,0:T(8,128)(2,1)}, f32[2048,768]{1,0:T(8,128)}, bf16[2048,768]{1,0:T(8,128)(2,1)}, bf16[768,3840]{1,0:T(8,128)(2,1)}, bf16[3072,768]{1,0:T(8,128)(2,1)}, /*index=5*/f32[16,768]{1,0:T(8,128)}) custom-call(f32[1]{0:T(128)S(6)} %copy.34.scale_ref, bf16[2048,768]{1,0:T(8,128)(2,1)} %bitcast.16, ...), custom_call_target="tpu_custom_call" | custom-call | flops 65000001536 | bytes 60000000 | tf_op jit(solution)/shard_map/middle/pallas_call | solution.py:808
  177.1 99.0 %attention_backward.1 = (f32[2048,768]{1,0:T(8,128)}, f32[96,768]{1,0:T(8,128)}, f32[24,3840]{1,0:T(8,128)}, f32[24,768]{1,0:T(8,128)}, f32[24,768]{1,0:T(8,128)}, /*index=5*/f32[24,1024]{1,0:T(8,128)}) custom-call(f32[1]{0:T(128)S(6)} %copy.34.scale_ref, bf16[2048,768]{1,0:T(8,128)(2,1)} %bitcast.17, bf16[2048,2304]{1,0:T(8,128)(2,1)} %get-tuple-element.56.qkv_ref, ...), custom_call_target="tpu_custom_call" | custom-call | tf_op jit(solution)/shard_map/attention_backward/pallas_call | solution.py:1000
  276.2 2.2 finish.1
  278.4 6.1 %copy.35 = f32[4,512,768]{2,1,0:T(8,128)} copy(f32[4,512,768]{2,1,0:T(8,128)} %bitcast.18) | data formatting | bytes 12582912
